TPU v7x, 256 devices: a whole 4x4x8 slice. The times are simulated.
256 devices in a mesh: row: 16 (over z_lo, x, core), col: 16 (over y, z_hi).
Axes of the slice: x: 4, y: 4, z: 8 (z_hi: 4, z_lo: 2; z = z_hi * 2 + z_lo), core: 2. Of those that a mesh axis runs over, the one named last changes fastest.
Arguments:
- left_factor: bfloat16 [128, 32, 2048], P('col', None, 'row'), may hold values from -6 to 6
- right_factor: bfloat16 [128, 32, 2048], P('row', None, 'col'), may hold values from -6 to 6
- pair_grad: bfloat16 [2048, 128, 2048], P('row', None, 'col'), may hold values from -6 to 6
- projection: bfloat16 [1024, 128], replicated, may hold values from -0.1875 to 0.1875
Outputs:
- left_grad: float32 [128, 32, 2048], P('col', None, 'row')
- right_grad: float32 [128, 32, 2048], P('row', None, 'col')
All inputs are finite; a program needn't handle non-finite values.
Results may differ from a plain program's by a relative error of at most 0.0029.
Values may be sent and summed in bfloat16 or wider, within the bound.
No kernel may reach another device: no remote copies, remote signals or barrier semaphores. Data moves between devices by JAX's collectives and lax.ppermute only.
A program may use at most 256 MiB of HBM per device.

v0:
```python
import jax
import jax.numpy as jnp
from jax import lax
from jax.sharding import Mesh
from jax.sharding import PartitionSpec as P

COL = ("col_0", "col_1")


def scatter_axes(shard, axes, dim):
    if not axes:
        return shard
    nearer = lax.psum_scatter(shard, axes[0], scatter_dimension=dim, tiled=True)
    return scatter_axes(nearer, axes[1:], dim)


def split_up(shard, dim, length):
    lengths = shard.shape
    blocks = shard.reshape(*lengths[:dim], length, lengths[dim] // length, *lengths[dim + 1 :])
    return jnp.moveaxis(blocks, dim, 0)


def sent_and_summed(shard, axis, dim):
    length = lax.axis_size(axis)
    blocks = lax.all_to_all(split_up(shard, dim, length), axis, 0, 0, tiled=True)
    return jnp.sum(blocks, axis=0)


def on_device(left_factor, right_factor, pair_grad, projection):
    tile_rows, pair_width, tile_cols = pair_grad.shape
    channels = left_factor.shape[1]
    left_whole = lax.all_gather(left_factor, COL, axis=0, tiled=True)
    right_whole = lax.all_gather(right_factor, "row", axis=0, tiled=True)
    sequences = left_whole.shape[0]
    inverse = 1.0 / sequences
    right_flat = right_whole.reshape(sequences, channels * tile_cols)
    group_rows = tile_rows // 4
    widened = jnp.broadcast_to(projection, (group_rows,) + projection.shape)
    left_pieces = []
    right_terms = []
    for number in range(4):
        lower = number * group_rows
        grad_slab = pair_grad[lower : lower + group_rows]
        expanded = lax.dot_general(
            widened, grad_slab, (((2,), (1,)), ((0,), (0,))), preferred_element_type=jnp.float32
        )
        expanded = expanded.astype(jnp.bfloat16).reshape(group_rows, channels, channels * tile_cols)
        left_raw = lax.dot_general(
            right_flat, expanded, (((1,), (2,)), ((), ())), preferred_element_type=jnp.float32
        )
        left_part = jnp.transpose(left_raw, (0, 2, 1)) * inverse
        left_slab = jnp.transpose(left_whole[:, :, lower : lower + group_rows], (0, 2, 1))
        left_slab = left_slab.reshape(sequences, group_rows * channels)
        right_part = jnp.dot(
            left_slab,
            expanded.reshape(group_rows * channels, channels * tile_cols),
            preferred_element_type=jnp.float32,
        )
        right_part = right_part.reshape(sequences, channels, tile_cols) * inverse
        left_pieces.append(left_part)
        right_terms.append(right_part)
    joined = jnp.concatenate(left_pieces, axis=2)
    left_grad = scatter_axes(joined, COL, 0)
    summed = right_terms[0] + right_terms[1] + right_terms[2] + right_terms[3]
    right_grad = sent_and_summed(summed, "row", 0)
    return (left_grad, right_grad)


def solution(mesh):
    torus = Mesh(mesh.devices.reshape(mesh.shape["row"], 4, 4), ("row", "col_0", "col_1"))
    return jax.shard_map(
        on_device,
        mesh=torus,
        in_specs=(P(COL, None, "row"), P("row", None, COL), P("row", None, COL), P()),
        out_specs=(P(COL, None, "row"), P("row", None, COL)),
        check_vma=False,
    )
```

profile of v0, /device:TPU:24, one launch (start us, length us, event | category | flops | bytes accessed | tf_op | source)
XLA Modules:
  0.0 253.8 jit_solution(16307443281897249371)
XLA Ops:
  8.7 5.7 %convolution_convert_fusion = bf16[32,1024,128]{2,1,0:T(8,128)(2,1)} fusion(bf16[1024,128]{1,0:T(8,128)(2,1)S(1)} %copy-done, bf16[128,128,128]{2,1,0:T(8,128)(2,1)} %param.6), kind=kOutput, calls=%fused_computation | convolution fusion | flops 1077936128 | bytes 9699328 | tf_op jit(solution)/shard_map/dot_general | solution.py:44
  14.4 13.4 %reshape_reshape.15 = bf16[1024,4096]{1,0:T(8,128)(2,1)} reshape(bf16[32,1024,128]{2,1,0:T(8,128)(2,1)} %convolution_convert_fusion) | data formatting | bytes 16777216 | tf_op jit(solution)/shard_map/reshape;reshape | solution.py:56
  27.8 13.3 %reshape.49 = bf16[32,32,4096]{2,1,0:T(8,128)(2,1)} reshape(bf16[32,1024,128]{2,1,0:T(8,128)(2,1)} %convolution_convert_fusion) | data formatting | bytes 16777216 | tf_op jit(solution)/shard_map/reshape | solution.py:47
  41.1 5.7 %convolution_convert_fusion.1 = bf16[32,1024,128]{2,1,0:T(8,128)(2,1)} fusion(bf16[1024,128]{1,0:T(8,128)(2,1)S(1)} %copy-done, bf16[128,128,128]{2,1,0:T(8,128)(2,1)} %param.6), kind=kOutput, calls=%fused_computation.1 | convolution fusion | flops 1077936128 | bytes 9699328 | tf_op jit(solution)/shard_map/dot_general | solution.py:44
  46.8 13.3 %reshape_reshape.14 = bf16[1024,4096]{1,0:T(8,128)(2,1)} reshape(bf16[32,1024,128]{2,1,0:T(8,128)(2,1)} %convolution_convert_fusion.1) | data formatting | bytes 16777216 | tf_op jit(solution)/shard_map/reshape;reshape | solution.py:56
  60.1 13.3 %reshape.48 = bf16[32,32,4096]{2,1,0:T(8,128)(2,1)} reshape(bf16[32,1024,128]{2,1,0:T(8,128)(2,1)} %convolution_convert_fusion.1) | data formatting | bytes 16777216 | tf_op jit(solution)/shard_map/reshape | solution.py:47
  73.5 5.7 %convolution_convert_fusion.2 = bf16[32,1024,128]{2,1,0:T(8,128)(2,1)} fusion(bf16[1024,128]{1,0:T(8,128)(2,1)S(1)} %copy-done, bf16[128,128,128]{2,1,0:T(8,128)(2,1)} %param.6), kind=kOutput, calls=%fused_computation.2 | convolution fusion | flops 1077936128 | bytes 9699328 | tf_op jit(solution)/shard_map/dot_general | solution.py:44
  79.1 13.4 %reshape_reshape.13 = bf16[1024,4096]{1,0:T(8,128)(2,1)} reshape(bf16[32,1024,128]{2,1,0:T(8,128)(2,1)} %convolution_convert_fusion.2) | data formatting | bytes 16777216 | tf_op jit(solution)/shard_map/reshape;reshape | solution.py:56
  92.5 13.4 %reshape.47 = bf16[32,32,4096]{2,1,0:T(8,128)(2,1)} reshape(bf16[32,1024,128]{2,1,0:T(8,128)(2,1)} %convolution_convert_fusion.2) | data formatting | bytes 16777216 | tf_op jit(solution)/shard_map/reshape | solution.py:47
  105.9 5.7 %convolution_convert_fusion.3 = bf16[32,1024,128]{2,1,0:T(8,128)(2,1)} fusion(bf16[1024,128]{1,0:T(8,128)(2,1)S(1)} %copy-done, bf16[128,128,128]{2,1,0:T(8,128)(2,1)} %param.6), kind=kOutput, calls=%fused_computation.3 | convolution fusion | flops 1077936128 | bytes 9699328 | tf_op jit(solution)/shard_map/dot_general | solution.py:44
  111.6 13.3 %reshape_reshape.12 = bf16[1024,4096]{1,0:T(8,128)(2,1)} reshape(bf16[32,1024,128]{2,1,0:T(8,128)(2,1)} %convolution_convert_fusion.3) | data formatting | bytes 16777216 | tf_op jit(solution)/shard_map/reshape;reshape | solution.py:56
  124.9 13.3 %reshape.45 = bf16[32,32,4096]{2,1,0:T(8,128)(2,1)} reshape(bf16[32,1024,128]{2,1,0:T(8,128)(2,1)} %convolution_convert_fusion.3) | data formatting | bytes 16777216 | tf_op jit(solution)/shard_map/reshape | solution.py:47
  138.2 4.4 %fusion.14 = (bf16[128,32,32]{2,1,0:T(8,128)(2,1)S(1)}, bf16[128,32,32]{2,1,0:T(8,128)(2,1)}, bf16[128,32,32]{2,1,0:T(8,128)(2,1)S(1)}, bf16[128,32,32]{2,1,0:T(8,128)(2,1)S(1)}) fusion(bf16[128,32,128]{2,1,0:T(8,128)(2,1)} %all-gather.5.cloned.1.call-done), kind=kLoop, calls=%fused_computation.27 | loop fusion | bytes 2097152 | tf_op jit(solution)/shard_map/slice | solution.py:52
  147.7 5.7 %fusion.6 = f32[128,32,32]{0,1,2:T(8,128)S(1)} fusion(bf16[32,32,4096]{2,1,0:T(8,128)(2,1)} %reshape.49, bf16[128,4096,1]{1,0,2:T(8,128)(2,1)S(1)} %reshape.54), kind=kOutput, calls=%fused_computation.16 | convolution fusion | flops 1073872896 | bytes 9961472 | tf_op jit(solution)/shard_map/dot_general | solution.py:48
  153.4 5.9 %fusion.7 = f32[128,32,32]{0,1,2:T(8,128)S(1)} fusion(bf16[32,32,4096]{2,1,0:T(8,128)(2,1)} %reshape.48, bf16[128,4096,1]{1,0,2:T(8,128)(2,1)S(1)} %reshape.54), kind=kOutput, calls=%fused_computation.18 | convolution fusion | flops 1073872896 | bytes 9961472 | tf_op jit(solution)/shard_map/dot_general | solution.py:48
  159.3 5.9 %fusion.8 = f32[128,32,32]{0,1,2:T(8,128)S(1)} fusion(bf16[32,32,4096]{2,1,0:T(8,128)(2,1)} %reshape.47, bf16[128,4096,1]{1,0,2:T(8,128)(2,1)S(1)} %reshape.54), kind=kOutput, calls=%fused_computation.20 | convolution fusion | flops 1073872896 | bytes 9961472 | tf_op jit(solution)/shard_map/dot_general | solution.py:48
  170.1 5.8 %fusion.15 = f32[4096,128]{1,0:T(8,128)S(1)} fusion(bf16[1024,4096]{1,0:T(8,128)(2,1)} %reshape_reshape.12, bf16[128,1024]{0,1:T(8,128)(2,1)} %bitcast.49), kind=kOutput, calls=%fused_computation.28 | convolution fusion | flops 1073741824 | bytes 10747904 | tf_op jit(solution)/shard_map/dot_general | solution.py:54
  175.9 5.8 %convolution_add_fusion.2 = f32[4096,128]{1,0:T(8,128)S(1)} fusion(f32[4096,128]{1,0:T(8,128)S(1)} %fusion.15, bf16[1024,4096]{1,0:T(8,128)(2,1)} %reshape_reshape.13, bf16[128,1024]{0,1:T(8,128)(2,1)S(1)} %bitcast.46), kind=kOutput, calls=%fused_computation.8 | convolution fusion | flops 1074266112 | bytes 12845056 | tf_op jit(solution)/shard_map/dot_general | solution.py:54
  181.7 2.6 %copy.18 = bf16[128,32,32]{0,1,2:T(8,128)(2,1)S(1)} copy(bf16[128,32,32]{2,1,0:T(8,128)(2,1)} %get-tuple-element.7) | data formatting | bytes 524288
  186.4 5.9 %convolution_add_fusion.1 = f32[4096,128]{1,0:T(8,128)S(1)} fusion(f32[4096,128]{1,0:T(8,128)S(1)} %convolution_add_fusion.2, bf16[1024,4096]{1,0:T(8,128)(2,1)} %reshape_reshape.14, bf16[128,1024]{0,1:T(8,128)(2,1)S(1)} %bitcast.47), kind=kOutput, calls=%fused_computation.7 | convolution fusion | flops 1074266112 | bytes 12845056 | tf_op jit(solution)/shard_map/dot_general | solution.py:54
  192.3 6.0 %fusion.1 = f32[128,4096]{0,1:T(8,128)S(1)} fusion(f32[4096,128]{1,0:T(8,128)S(1)} %convolution_add_fusion.1, bf16[1024,4096]{1,0:T(8,128)(2,1)} %reshape_reshape.15, bf16[128,1024]{0,1:T(8,128)(2,1)S(1)} %bitcast.48), kind=kOutput, calls=%fused_computation.6 | convolution fusion | flops 1074790400 | bytes 12845056 | tf_op jit(solution)/shard_map/dot_general | solution.py:54
  200.1 3.3 %copy.22 = f32[16,8,32,128]{3,2,1,0:T(8,128)} copy(f32[16,8,32,128]{3,1,2,0:T(8,128)} %bitcast.45) | data formatting | bytes 4194304
  203.4 5.8 %all-to-all-start = ((f32[16,8,32,128]{3,2,1,0:T(8,128)}), f32[16,8,32,128]{3,2,1,0:T(8,128)S(1)}, u32[]{:S(2)}, u32[]{:S(2)}) async-start(f32[16,8,32,128]{3,2,1,0:T(8,128)} %copy.22), calls=%async_computation.2 | async-start | bytes 4194304 | tf_op jit(solution)/shard_map/all_to_all | solution.py:25
  209.8 36.6 %all-to-all-done = f32[16,8,32,128]{3,2,1,0:T(8,128)S(1)} async-done(((f32[16,8,32,128]{3,2,1,0:T(8,128)}), f32[16,8,32,128]{3,2,1,0:T(8,128)S(1)}, u32[]{:S(2)}, u32[]{:S(2)}) %all-to-all-start) | async-done | bytes 2097184 | tf_op jit(solution)/shard_map/all_to_all | solution.py:25
  (32 shorter events, 16.6 us)
Async XLA Ops:
  7.2 1.6 copy-start
  7.2 131.0 %all-gather.5.cloned.1.call-start = ((), (), s32[]{:S(2)}) async-start(), calls=%async_computation.6 | async-start | bytes 1114112 | tf_op jit(solution)/shard_map/all_gather | solution.py:32
  7.9 138.1 %all-gather.3.cloned.1.call-start = ((), (), s32[]{:S(2)}) async-start(), calls=%async_computation.3 | async-start | bytes 1114112 | tf_op jit(solution)/shard_map/all_gather | solution.py:33
  8.7 200.6 %reduce-scatter.3.cloned.1.call-start = ((), (), s32[]{:S(2)}) async-start(), calls=%async_computation.4 | async-start | bytes 2621440 | tf_op jit(solution)/shard_map/reduce_scatter | solution.py:13
  153.4 11.8 %slice-start = ((s8[8388608]{0:T(1024)(128)(4,1)}), s8[4194304]{0:T(1024)(128)(4,1)S(1)}, s32[]{:S(2)}) async-start(s8[8388608]{0:T(1024)(128)(4,1)} %bitcast.43), calls=%async_computation.7 | async-start | bytes 8388608
  159.3 5.9 %slice-start.1 = ((s8[8388608]{0:T(1024)(128)(4,1)}), s8[4194304]{0:T(1024)(128)(4,1)S(1)}, s32[]{:S(2)}) async-start(s8[8388608]{0:T(1024)(128)(4,1)} %bitcast.43), calls=%async_computation.8 | async-start | bytes 8388608
  186.4 5.9 %copy-start.2 = (bf16[128,32,32]{0,1,2:T(8,128)(2,1)S(1)}, bf16[128,32,32]{0,1,2:T(8,128)(2,1)}, u32[]{:S(2)}) copy-start(bf16[128,32,32]{0,1,2:T(8,128)(2,1)} %copy.19) | copy-start | bytes 786436
  192.3 55.0 %copy-start.1 = (bf16[1024,128]{1,0:T(8,128)(2,1)S(1)}, bf16[1024,128]{1,0:T(8,128)(2,1)}, u32[]{:S(2)}) copy-start(bf16[1024,128]{1,0:T(8,128)(2,1)} %param.7) | copy-start | bytes 786436
  203.4 43.0 %all-to-all-start = ((f32[16,8,32,128]{3,2,1,0:T(8,128)}), f32[16,8,32,128]{3,2,1,0:T(8,128)S(1)}, u32[]{:S(2)}, u32[]{:S(2)}) async-start(f32[16,8,32,128]{3,2,1,0:T(8,128)} %copy.22), calls=%async_computation.2 | async-start | bytes 4194304 | tf_op jit(solution)/shard_map/all_to_all | solution.py:25
  209.2 38.0 %reduce-scatter.5.cloned.1.call-start = ((), (), s32[]{:S(2)}) async-start(), calls=%async_computation.5 | async-start | bytes 655360 | tf_op jit(solution)/shard_map/reduce_scatter | solution.py:13
Sparse Core Ops, SparseCore 0:
  10.4 54.6 all-gather.4
  67.0 33.8 all-gather.2
  170.2 32.9 reduce-scatter.2
  213.0 33.0 reduce-scatter.4
where the time goes:
time: 257 us; the launch traced here: 254 us
  local copies, waits for them, and re-layouts  128 us (50%)
  matrix products  66.1 us (26%)
  waiting for transfers between devices  38.5 us (15%)
  between operations  13.9 us (5%)
  starting transfers between devices  5.95 us (2%)
    another operation x4, local copies, waits for them, and re-layouts, on_device(): expanded.reshape(group_rows * channels, channels * tile_cols)  53.4 us
    reshape x4, local copies, waits for them, and re-layouts, on_device(): expanded.astype(jnp.bfloat16)  53.3 us
    all_to_all x1, waiting for transfers between devices, sent_and_summed(): lax.all_to_all(split_up(shard, dim, length), axis, 0, 0, tiled=True)  36.6 us
    dot_general x4, matrix products, on_device(): jnp.dot(left_slab, expanded.reshape(group_rows * channels, channels * til...  23.5 us
    dot_general x4, matrix products, on_device(): lax.dot_general(widened, grad_slab, (((2,), (1,)), ((0,), (0,))), preferr...  22.7 us
    dot_general x4, matrix products, on_device(): lax.dot_general(right_flat, expanded, (((1,), (2,)), ((), ())), preferred...  19.8 us
    unnamed x15, local copies, waits for them, and re-layouts  11.2 us
    all_to_all x1, starting transfers between devices, sent_and_summed(): lax.all_to_all(split_up(shard, dim, length), axis, 0, 0, tiled=True)  5.8 us
  transfers between devices with their start and end apart: 5, of which 1 were waited for; matrix products, arithmetic and copies ran while one was open for 67% of the time, Pallas kernels for 0%

commit v1 on v0

v1 whole, which is shorter than its diff:
```python
import jax
import jax.numpy as jnp
from jax import lax
from jax.experimental import pallas as pl
from jax.experimental.pallas import tpu as pltpu
from jax.sharding import Mesh
from jax.sharding import PartitionSpec as P

ROW = ("z_lo", "x", "core")
COL = ("y", "z_hi")
VMEM = 48 << 20


def expand(pair_grad, weights, channels, group):
    rows, width, cols = pair_grad.shape
    wide = weights.shape[0]
    entries = wide // channels
    step = 8

    def body(weight_ref, grad_ref, out_ref):
        for i in range(0, group, 2):
            pair = jnp.concatenate([grad_ref[i], grad_ref[i + 1]], axis=1)
            for first in range(0, entries, step):
                piece = weight_ref[first * channels : (first + step) * channels, :]
                value = jnp.dot(piece, pair, preferred_element_type=jnp.float32).astype(jnp.bfloat16)
                for k in range(step):
                    for half in range(2):
                        top = (i + half) * channels
                        side = (first + k) * cols
                        out_ref[top : top + channels, side : side + cols] = value[
                            k * channels : (k + 1) * channels, half * cols : (half + 1) * cols
                        ]

    return pl.pallas_call(
        body,
        grid=(rows // group,),
        in_specs=[
            pl.BlockSpec((wide, width), lambda i: (0, 0)),
            pl.BlockSpec((group, width, cols), lambda i: (i, 0, 0)),
        ],
        out_specs=pl.BlockSpec((group * channels, entries * cols), lambda i: (i, 0)),
        out_shape=jax.ShapeDtypeStruct((rows * channels, entries * cols), jnp.bfloat16),
        compiler_params=pltpu.CompilerParams(vmem_limit_bytes=VMEM),
        name="expand",
    )(weights, pair_grad)


def left_partial(right_flat, expanded, inverse, block):
    sequences, depth = right_flat.shape
    total = expanded.shape[0]

    def body(right_ref, expanded_ref, out_ref):
        value = lax.dot_general(
            right_ref[...], expanded_ref[...], (((1,), (1,)), ((), ())), preferred_element_type=jnp.float32
        )
        out_ref[...] = (value * inverse).astype(jnp.bfloat16)

    return pl.pallas_call(
        body,
        grid=(total // block,),
        in_specs=[
            pl.BlockSpec((sequences, depth), lambda i: (0, 0)),
            pl.BlockSpec((block, depth), lambda i: (i, 0)),
        ],
        out_specs=pl.BlockSpec((sequences, block), lambda i: (0, i)),
        out_shape=jax.ShapeDtypeStruct((sequences, total), jnp.bfloat16),
        compiler_params=pltpu.CompilerParams(vmem_limit_bytes=VMEM),
        name="left_partial",
    )(right_flat, expanded)


def right_partial(left_flat, expanded, inverse, block):
    sequences, depth = left_flat.shape
    total = expanded.shape[1]

    def body(left_ref, expanded_ref, out_ref):
        value = jnp.dot(left_ref[...], expanded_ref[...], preferred_element_type=jnp.float32)
        out_ref[...] = (value * inverse).astype(jnp.bfloat16)

    return pl.pallas_call(
        body,
        grid=(total // block,),
        in_specs=[
            pl.BlockSpec((sequences, depth), lambda i: (0, 0)),
            pl.BlockSpec((depth, block), lambda i: (0, i)),
        ],
        out_specs=pl.BlockSpec((sequences, block), lambda i: (0, i)),
        out_shape=jax.ShapeDtypeStruct((sequences, total), jnp.bfloat16),
        compiler_params=pltpu.CompilerParams(vmem_limit_bytes=VMEM),
        name="right_partial",
    )(left_flat, expanded)


def gathered(shard, axes):
    count = lax.axis_size(axes)
    copies = jnp.broadcast_to(shard[None], (count,) + shard.shape)
    blocks = lax.all_to_all(copies, axes, 0, 0, tiled=True)
    return blocks.reshape((count * shard.shape[0],) + shard.shape[1:])


def sent_and_summed(partial, axes):
    count = lax.axis_size(axes)
    blocks = partial.reshape((count, partial.shape[0] // count) + partial.shape[1:])
    blocks = lax.all_to_all(blocks, axes, 0, 0, tiled=True)
    return jnp.sum(blocks.astype(jnp.float32), axis=0)


def on_device(left_factor, right_factor, pair_grad, projection):
    shared, channels, rows = left_factor.shape
    held, entries, cols = right_factor.shape
    left_flat = jnp.transpose(left_factor, (0, 2, 1)).reshape(shared, rows * channels)
    right_flat = right_factor.reshape(held, entries * cols)
    right_whole = gathered(right_flat, ROW)
    left_whole = gathered(left_flat, COL)
    inverse = 1.0 / left_whole.shape[0]
    weights = jnp.swapaxes(projection.reshape(channels, entries, -1), 0, 1).reshape(projection.shape)
    expanded = expand(pair_grad, weights, channels, 16)
    left_sum = left_partial(right_whole, expanded, inverse, 512)
    left_grad = sent_and_summed(left_sum, COL)
    right_sum = right_partial(left_whole, expanded, inverse, 1024)
    right_grad = sent_and_summed(right_sum, ROW)
    left_grad = jnp.swapaxes(left_grad.reshape(shared, rows, channels), 1, 2)
    return (left_grad, right_grad.reshape(held, entries, cols))


def solution(mesh):
    names = ("z_lo", "x", "core", "y", "z_hi")
    torus = Mesh(mesh.devices.reshape(2, 4, 2, 4, 4), names)
    return jax.shard_map(
        on_device,
        mesh=torus,
        in_specs=(P(COL, None, ROW), P(ROW, None, COL), P(ROW, None, COL), P()),
        out_specs=(P(COL, None, ROW), P(ROW, None, COL)),
        check_vma=False,
    )
```

time: 257 us -> 132 us (0.51)
  the two profiles are of different devices: /device:TPU:24 before, /device:TPU:1 now
where the time goes in v1:
time: 132 us; the launch traced here: 131 us
  Pallas kernels  45.1 us (34%)
  waiting for transfers between devices  43.1 us (33%)
  starting transfers between devices  33.6 us (25%)
  local copies, waits for them, and re-layouts  8.37 us (6%)
    all_to_all x2, waiting for transfers between devices, sent_and_summed(): blocks = lax.all_to_all(blocks, axes, 0, 0, tiled=True)  28.6 us
    pallas_call x1, Pallas kernels, left_partial(): pl.pallas_call(body, grid=(total // block,), in_specs=[pl.BlockSpec((sequ...  17.7 us
    all_to_all x2, starting transfers between devices, gathered(): blocks = lax.all_to_all(copies, axes, 0, 0, tiled=True)  17.2 us
    all_to_all x2, starting transfers between devices, sent_and_summed(): blocks = lax.all_to_all(blocks, axes, 0, 0, tiled=True)  16.4 us
    all_to_all x2, waiting for transfers between devices, gathered(): blocks = lax.all_to_all(copies, axes, 0, 0, tiled=True)  14.5 us
    pallas_call x1, Pallas kernels, expand(): pl.pallas_call(body, grid=(rows // group,), in_specs=[pl.BlockSpec((wide,...  14.4 us
    pallas_call x1, Pallas kernels, right_partial(): pl.pallas_call(body, grid=(total // block,), in_specs=[pl.BlockSpec((sequ...  13 us
    unnamed x7, local copies, waits for them, and re-layouts  4.61 us
  transfers between devices with their start and end apart: 4, of which 3 were waited for; matrix products, arithmetic and copies ran while one was open for 2% of the time, Pallas kernels for 34%

profile of v1, /device:TPU:1, one launch (start us, length us, event | category | flops | bytes accessed | tf_op | source)
XLA Modules:
  0.0 131.2 jit_solution(16003718946935315570)
XLA Ops:
  0.6 0.9 copy.15
  1.6 1.1 broadcast_in_dim.15
  2.6 7.2 %all-to-all-start = ((bf16[16,8,4096]{2,1,0:T(8,128)(2,1)}), bf16[16,8,4096]{2,1,0:T(8,128)(2,1)S(1)}, u32[]{:S(2)}, u32[]{:S(2)}) async-start(bf16[16,8,4096]{2,1,0:T(8,128)(2,1)} %broadcast_in_dim.15), calls=%async_computation | async-start | bytes 2097152 | tf_op jit(solution)/shard_map/all_to_all | solution.py:97
  9.8 1.0 copy.8
  10.8 0.3 broadcast_in_dim.16
  11.1 14.5 %all-to-all-done = bf16[16,8,4096]{2,1,0:T(8,128)(2,1)S(1)} async-done(((bf16[16,8,4096]{2,1,0:T(8,128)(2,1)}), bf16[16,8,4096]{2,1,0:T(8,128)(2,1)S(1)}, u32[]{:S(2)}, u32[]{:S(2)}) %all-to-all-start) | async-done | bytes 1048608 | tf_op jit(solution)/shard_map/all_to_all | solution.py:97
  25.6 1.1 broadcast_in_dim.17
  26.7 10.0 %all-to-all-start.2 = ((bf16[16,8,4096]{2,1,0:T(8,128)(2,1)}), bf16[16,8,4096]{2,1,0:T(8,128)(2,1)S(1)}, u32[]{:S(2)}, u32[]{:S(2)}) async-start(bf16[16,8,4096]{2,1,0:T(8,128)(2,1)} %broadcast_in_dim.17), calls=%async_computation.2 | async-start | bytes 2097152 | tf_op jit(solution)/shard_map/all_to_all | solution.py:97
  36.8 0.1 copy.7
  36.9 0.0 copy-start
  36.9 2.2 %copy-done = bf16[128,128,128]{2,1,0:T(8,128)(2,1)S(1)} copy-done((bf16[128,128,128]{2,1,0:T(8,128)(2,1)S(1)}, bf16[128,128,128]{2,1,0:T(8,128)(2,1)}, u32[]{:S(2)}) %copy-start) | copy-done | bytes 4194328
  39.1 14.4 %expand.1.expanded_ref = bf16[4096,4096]{1,0:T(8,128)(2,1)} custom-call(bf16[1024,128]{1,0:T(8,128)(2,1)S(1)} %bitcast.20, bf16[128,128,128]{2,1,0:T(8,128)(2,1)S(1)} %copy-done), custom_call_target="tpu_custom_call" | custom-call | tf_op jit(solution)/shard_map/expand/pallas_call | solution.py:34
  53.5 17.7 %left_partial.1 = bf16[128,4096]{1,0:T(8,128)(2,1)} custom-call(bf16[128,4096]{1,0:T(8,128)(2,1)S(1)} %bitcast.18, bf16[4096,4096]{1,0:T(8,128)(2,1)} %expand.1.expanded_ref), custom_call_target="tpu_custom_call" | custom-call | tf_op jit(solution)/shard_map/left_partial/pallas_call | solution.py:58
  71.2 0.0 all-to-all-done.2
  71.2 9.1 %all-to-all-start.1 = ((bf16[16,8,4096]{2,1,0:T(8,128)(2,1)}), bf16[16,8,4096]{2,1,0:T(8,128)(2,1)S(1)}, u32[]{:S(2)}, u32[]{:S(2)}) async-start(bf16[16,8,4096]{2,1,0:T(8,128)(2,1)} %bitcast.4), calls=%async_computation.1 | async-start | bytes 2097152 | tf_op jit(solution)/shard_map/all_to_all | solution.py:104
  80.2 13.0 %right_partial.1 = bf16[128,4096]{1,0:T(8,128)(2,1)} custom-call(bf16[128,4096]{1,0:T(8,128)(2,1)S(1)} %bitcast.19, bf16[4096,4096]{1,0:T(8,128)(2,1)} %expand.1.expanded_ref), custom_call_target="tpu_custom_call" | custom-call | tf_op jit(solution)/shard_map/right_partial/pallas_call | solution.py:80
  93.3 13.8 %all-to-all-done.1 = bf16[16,8,4096]{2,1,0:T(8,128)(2,1)S(1)} async-done(((bf16[16,8,4096]{2,1,0:T(8,128)(2,1)}), bf16[16,8,4096]{2,1,0:T(8,128)(2,1)S(1)}, u32[]{:S(2)}, u32[]{:S(2)}) %all-to-all-start.1) | async-done | bytes 1048608 | tf_op jit(solution)/shard_map/all_to_all | solution.py:104
  107.1 7.4 %all-to-all-start.3 = ((bf16[16,8,4096]{2,1,0:T(8,128)(2,1)}), bf16[16,8,4096]{2,1,0:T(8,128)(2,1)S(1)}, u32[]{:S(2)}, u32[]{:S(2)}) async-start(bf16[16,8,4096]{2,1,0:T(8,128)(2,1)} %bitcast.8), calls=%async_computation.3 | async-start | bytes 2097152 | tf_op jit(solution)/shard_map/all_to_all | solution.py:104
  114.4 0.1 convert_reduce_fusion.1
  114.6 0.2 reshape.34
  114.7 0.8 copy.9
  115.6 14.8 %all-to-all-done.3 = bf16[16,8,4096]{2,1,0:T(8,128)(2,1)S(1)} async-done(((bf16[16,8,4096]{2,1,0:T(8,128)(2,1)}), bf16[16,8,4096]{2,1,0:T(8,128)(2,1)S(1)}, u32[]{:S(2)}, u32[]{:S(2)}) %all-to-all-start.3) | async-done | bytes 1048608 | tf_op jit(solution)/shard_map/all_to_all | solution.py:104
  130.3 0.1 convert_reduce_fusion
  130.5 0.7 copy.14
  (2 shorter events, 0.0 us)
Async XLA Ops:
  0.6 36.1 %copy-start.1 = (bf16[1024,128]{1,0:T(8,128)(2,1)S(1)}, bf16[1024,128]{1,0:T(8,128)(2,1)}, u32[]{:S(2)}) copy-start(bf16[1024,128]{1,0:T(8,128)(2,1)} %param.7) | copy-start | bytes 786436
  2.6 23.0 %all-to-all-start = ((bf16[16,8,4096]{2,1,0:T(8,128)(2,1)}), bf16[16,8,4096]{2,1,0:T(8,128)(2,1)S(1)}, u32[]{:S(2)}, u32[]{:S(2)}) async-start(bf16[16,8,4096]{2,1,0:T(8,128)(2,1)} %broadcast_in_dim.15), calls=%async_computation | async-start | bytes 2097152 | tf_op jit(solution)/shard_map/all_to_all | solution.py:97
  26.7 44.4 %all-to-all-start.2 = ((bf16[16,8,4096]{2,1,0:T(8,128)(2,1)}), bf16[16,8,4096]{2,1,0:T(8,128)(2,1)S(1)}, u32[]{:S(2)}, u32[]{:S(2)}) async-start(bf16[16,8,4096]{2,1,0:T(8,128)(2,1)} %broadcast_in_dim.17), calls=%async_computation.2 | async-start | bytes 2097152 | tf_op jit(solution)/shard_map/all_to_all | solution.py:97
  36.9 2.2 %copy-start = (bf16[128,128,128]{2,1,0:T(8,128)(2,1)S(1)}, bf16[128,128,128]{2,1,0:T(8,128)(2,1)}, u32[]{:S(2)}) copy-start(bf16[128,128,128]{2,1,0:T(8,128)(2,1)} %grad_ref.1) | copy-start | bytes 12582916
  71.2 35.9 %all-to-all-start.1 = ((bf16[16,8,4096]{2,1,0:T(8,128)(2,1)}), bf16[16,8,4096]{2,1,0:T(8,128)(2,1)S(1)}, u32[]{:S(2)}, u32[]{:S(2)}) async-start(bf16[16,8,4096]{2,1,0:T(8,128)(2,1)} %bitcast.4), calls=%async_computation.1 | async-start | bytes 2097152 | tf_op jit(solution)/shard_map/all_to_all | solution.py:104
  107.1 23.3 %all-to-all-start.3 = ((bf16[16,8,4096]{2,1,0:T(8,128)(2,1)}), bf16[16,8,4096]{2,1,0:T(8,128)(2,1)S(1)}, u32[]{:S(2)}, u32[]{:S(2)}) async-start(bf16[16,8,4096]{2,1,0:T(8,128)(2,1)} %bitcast.8), calls=%async_computation.3 | async-start | bytes 2097152 | tf_op jit(solution)/shard_map/all_to_all | solution.py:104

commit v2 on v1

v2 whole, which is shorter than its diff:
```python
import jax
import jax.numpy as jnp
from jax import lax
from jax.experimental import pallas as pl
from jax.experimental.pallas import tpu as pltpu
from jax.sharding import Mesh
from jax.sharding import PartitionSpec as P

ROW = ("z_lo", "x", "core")
COL = ("y", "z_hi")
VMEM = 12 << 20
PIECES = 4
WHOLE = pl.BlockSpec(memory_space=pltpu.VMEM)
TABLE = pl.BlockSpec(memory_space=pltpu.SMEM)


def params():
    return pltpu.CompilerParams(vmem_limit_bytes=VMEM)


def expand(pair_grad, weights, channels, number):
    rows, width, cols = pair_grad.shape
    wide = weights.shape[0]
    entries = wide // channels
    held = rows // PIECES
    step = 8

    def body(weight_ref, grad_ref, out_ref):
        def two(t, carry):
            i = number * held + t * 2
            pair = jnp.concatenate([grad_ref[i], grad_ref[i + 1]], axis=1)
            base = pl.multiple_of(t * (2 * channels), 2 * channels)
            for first in range(0, entries, step):
                piece = weight_ref[first * channels : (first + step) * channels, :]
                value = jnp.dot(piece, pair, preferred_element_type=jnp.float32).astype(jnp.bfloat16)
                for k in range(step):
                    block = value[k * channels : (k + 1) * channels]
                    stacked = jnp.concatenate([block[:, :cols], block[:, cols:]], axis=0)
                    side = (first + k) * cols
                    out_ref[pl.ds(base, 2 * channels), side : side + cols] = stacked
            return carry

        lax.fori_loop(0, held // 2, two, 0, unroll=2)

    return pl.pallas_call(
        body,
        in_specs=[WHOLE, WHOLE],
        out_specs=WHOLE,
        out_shape=pltpu.VMEM((held * channels, entries * cols), jnp.bfloat16),
        compiler_params=params(),
        cost_estimate=pl.CostEstimate(flops=4 * held * wide * width * cols, transcendentals=0, bytes_accessed=1 << 20),
        name="expand",
    )(weights, pair_grad)


def place(scratch, table_ref, sources, size):
    at = 0
    for source in sources:
        for top in range(0, source.shape[0], size):
            scratch[table_ref[at]] = source[top : top + size, :]
            at += 1


def left_partial(table, sources, expanded, size, inverse):
    count = table.shape[0]
    sequences = count * size
    depth = expanded[0].shape[1]
    total = sum(e.shape[0] for e in expanded)
    part = sequences // 4
    block = 512

    def body(table_ref, *refs):
        source_refs = refs[: len(sources)]
        expanded_refs = refs[len(sources) : len(sources) + len(expanded)]
        own_ref, *other_refs = refs[len(sources) + len(expanded) : -2]
        placed, turned = refs[-2:]
        place(placed, table_ref, source_refs, size)
        turned[...] = placed[...].reshape(sequences, depth).T
        at = 0
        for expanded_ref in expanded_refs:
            for top in range(0, expanded_ref.shape[0], block):
                value = jnp.dot(
                    expanded_ref[top : top + block, :], turned[...], preferred_element_type=jnp.float32
                )
                value = value.T * inverse
                own_ref[:, at : at + block] = value[:part]
                for k, other_ref in enumerate(other_refs):
                    lower = (k + 1) * part
                    other_ref[:, at : at + block] = value[lower : lower + part].astype(jnp.bfloat16)
                at += block

    other = jax.ShapeDtypeStruct((part, total), jnp.bfloat16)
    return pl.pallas_call(
        body,
        in_specs=[TABLE] + [WHOLE] * (len(sources) + len(expanded)),
        out_specs=[WHOLE] * 4,
        out_shape=[jax.ShapeDtypeStruct((part, total), jnp.float32), other, other, other],
        scratch_shapes=[pltpu.VMEM((count, size, depth), jnp.bfloat16), pltpu.VMEM((depth, sequences), jnp.bfloat16)],
        compiler_params=params(),
        cost_estimate=pl.CostEstimate(flops=4 * sequences * depth * total, transcendentals=0, bytes_accessed=1 << 20),
        name="left_partial",
    )(table, *sources, *expanded)


def right_partial(table, sources, expanded, size, inverse):
    count = table.shape[0]
    sequences = count * size
    depth = sum(e.shape[0] for e in expanded)
    total = expanded[0].shape[1]
    part = sequences // 2
    block = 512

    def body(table_ref, *refs):
        source_refs = refs[: len(sources)]
        expanded_refs = refs[len(sources) : len(sources) + len(expanded)]
        own_ref, other_ref, blocked, placed = refs[len(sources) + len(expanded) :]
        place(blocked, table_ref, source_refs, size)
        placed[...] = blocked[...].reshape(sequences, depth)
        for side in range(0, total, block):
            value = 0.0
            at = 0
            for expanded_ref in expanded_refs:
                high = expanded_ref.shape[0]
                value = value + jnp.dot(
                    placed[:, at : at + high],
                    expanded_ref[:, side : side + block],
                    preferred_element_type=jnp.float32,
                )
                at += high
            value = value * inverse
            own_ref[:, side : side + block] = value[:part]
            other_ref[:, side : side + block] = value[part:]

    half = jax.ShapeDtypeStruct((part, total), jnp.float32)
    return pl.pallas_call(
        body,
        in_specs=[TABLE] + [WHOLE] * (len(sources) + len(expanded)),
        out_specs=[WHOLE] * 2,
        out_shape=[half, half],
        scratch_shapes=[pltpu.VMEM((count, size, depth), jnp.bfloat16), pltpu.VMEM((sequences, depth), jnp.bfloat16)],
        compiler_params=params(),
        cost_estimate=pl.CostEstimate(flops=2 * sequences * depth * total, transcendentals=0, bytes_accessed=1 << 20),
        name="right_partial",
    )(table, *sources, *expanded)


def moved(value, axis, distance):
    size = lax.axis_size(axis)
    return lax.ppermute(value, axis, [(k, (k + distance) % size) for k in range(size)])


def swapped(value, axis, bit):
    return lax.ppermute(value, axis, [(k, k ^ bit) for k in range(lax.axis_size(axis))])


def orders(blocks):
    z_lo, x, core, y, z_hi = (lax.axis_index(name) for name in ROW + COL)
    at = lax.iota(jnp.int32, blocks)
    block = (z_lo ^ (at // 4 % 2)) * 8 + (x - at) % 4 * 2 + (core ^ (at // 8))
    left_table = (block // 4 - y) % 4 * 4 + (block - z_hi) % 4
    block = (y - at // 4) % 4 * 4 + (z_hi ^ (at % 4))
    right_table = (block - core) % 2 * 8 + (block // 8 - z_lo) % 2 * 4 + (block // 2 - x) % 4
    return left_table, right_table


def on_device(left_factor, right_factor, pair_grad, projection):
    shared, channels, rows = left_factor.shape
    held, entries, cols = right_factor.shape
    left_flat = jnp.transpose(left_factor, (0, 2, 1)).reshape(shared, rows * channels)
    right_flat = right_factor.reshape(held, entries * cols)
    weights = jnp.swapaxes(projection.reshape(channels, entries, -1), 0, 1).reshape(projection.shape)

    blocks = 4 * 4
    inverse = 1.0 / (blocks * shared)
    left_table, right_table = orders(blocks)
    left_table, right_table, pair_grad = lax.optimization_barrier((left_table, right_table, pair_grad))

    along_x = jnp.concatenate([right_flat] + [moved(right_flat, "x", d) for d in (1, 2, 3)], axis=0)
    near_left = jnp.concatenate([left_flat, swapped(left_flat, "z_hi", 1)], axis=0)
    near_left = jnp.concatenate([near_left, swapped(near_left, "z_hi", 2)], axis=0)
    along_z = jnp.concatenate([along_x, swapped(along_x, "z_lo", 1)], axis=0)
    along_core = swapped(along_z, "core", 1)

    expanded = [expand(pair_grad, weights, channels, number) for number in range(PIECES)]
    own, *others = left_partial(left_table, [along_z, along_core], expanded, held, inverse)

    far_left = [near_left] + [moved(near_left, "y", d) for d in (1, 2, 3)]
    right_table, others = lax.optimization_barrier((right_table, others))
    right_own, right_other = right_partial(right_table, far_left, expanded, shared, inverse)

    left_sum = own
    for d, other in enumerate(others):
        left_sum = left_sum + moved(other, "y", d + 1).astype(jnp.float32)
    left_grad = left_sum[:shared]
    for d in (1, 2, 3):
        piece = left_sum[d * shared : (d + 1) * shared].astype(jnp.bfloat16)
        left_grad = left_grad + moved(piece, "z_hi", d).astype(jnp.float32)
    left_grad = jnp.swapaxes(left_grad.reshape(shared, rows, channels), 1, 2)

    right_sum = right_own + swapped(right_other, "core", 1)
    middle = 4 * held
    right_sum = right_sum[:middle] + swapped(right_sum[middle:].astype(jnp.bfloat16), "z_lo", 1).astype(jnp.float32)
    right_grad = right_sum[:held]
    for d in (1, 2, 3):
        piece = right_sum[d * held : (d + 1) * held].astype(jnp.bfloat16)
        right_grad = right_grad + moved(piece, "x", d).astype(jnp.float32)
    return (left_grad, right_grad.reshape(held, entries, cols))


def solution(mesh):
    names = ("z_lo", "x", "core", "y", "z_hi")
    torus = Mesh(mesh.devices.reshape(2, 4, 2, 4, 4), names)
    return jax.shard_map(
        on_device,
        mesh=torus,
        in_specs=(P(COL, None, ROW), P(ROW, None, COL), P(ROW, None, COL), P()),
        out_specs=(P(COL, None, ROW), P(ROW, None, COL)),
        check_vma=False,
    )
```

time: 132 us -> 93.9 us (0.71)
  the two profiles are of different devices: /device:TPU:1 before, /device:TPU:24 now
where the time goes in v2:
time: 93.9 us; the launch traced here: 93.6 us
  starting transfers between devices  33.7 us (36%)
  Pallas kernels  28.8 us (31%)
  waiting for transfers between devices  21.6 us (23%)
  local copies, waits for them, and re-layouts  8.06 us (9%)
    ppermute x15, starting transfers between devices, moved(): lax.ppermute(value, axis, [(k, (k + distance) % size) for k in range(size)])  23.5 us
    ppermute x6, waiting for transfers between devices, swapped(): lax.ppermute(value, axis, [(k, k ^ bit) for k in range(lax.axis_size(axis...  15.7 us
    pallas_call x4, Pallas kernels, expand(): pl.pallas_call(body, in_specs=[WHOLE, WHOLE], out_specs=WHOLE, out_shape=...  14 us
    ppermute x6, starting transfers between devices, swapped(): lax.ppermute(value, axis, [(k, k ^ bit) for k in range(lax.axis_size(axis...  10.2 us
    pallas_call x1, Pallas kernels, left_partial(): pl.pallas_call(body, in_specs=[TABLE] + [WHOLE] * (len(sources) + len(exp...  9.65 us
    ppermute x15, waiting for transfers between devices, moved(): lax.ppermute(value, axis, [(k, (k + distance) % size) for k in range(size)])  5.94 us
    unnamed x11, local copies, waits for them, and re-layouts  5.47 us
    pallas_call x1, Pallas kernels, right_partial(): pl.pallas_call(body, in_specs=[TABLE] + [WHOLE] * (len(sources) + len(exp...  5.2 us
  transfers between devices with their start and end apart: 21, of which 8 were waited for; matrix products, arithmetic and copies ran while one was open for 5% of the time, Pallas kernels for 31%

profile of v2, /device:TPU:24, one launch (start us, length us, event | category | flops | bytes accessed | tf_op | source)
XLA Modules:
  0.0 93.6 jit_solution(4046441275605342338)
XLA Ops:
  1.5 1.6 %collective-permute-start = (bf16[8,4096]{1,0:T(8,128)(2,1)S(1)}, bf16[8,4096]{1,0:T(8,128)(2,1)S(1)}, u32[]{:S(2)}, u32[]{:S(2)}) collective-permute-start(bf16[8,4096]{1,0:T(8,128)(2,1)S(1)} %bitcast.22), channel_id=1, source_target_pairs={{0,32},{32,64},{64,96},{96,0},{1,33},{33,65},{65,97},{97,1},{2,34}... | collective-permute-start | bytes 196616 | tf_op jit(solution)/shard_map/ppermute | solution.py:149
  3.1 2.7 %collective-permute-start.1 = (bf16[8,4096]{1,0:T(8,128)(2,1)S(1)}, bf16[8,4096]{1,0:T(8,128)(2,1)S(1)}, u32[]{:S(2)}, u32[]{:S(2)}) collective-permute-start(bf16[8,4096]{1,0:T(8,128)(2,1)S(1)} %bitcast.23), channel_id=1, source_target_pairs={{0,64},{32,96},{64,0},{96,32},{1,65},{33,97},{65,1},{97,33},{2,66}... | collective-permute-start | bytes 196616 | tf_op jit(solution)/shard_map/ppermute | solution.py:149
  5.8 1.4 %collective-permute-start.2 = (bf16[8,4096]{1,0:T(8,128)(2,1)S(1)}, bf16[8,4096]{1,0:T(8,128)(2,1)S(1)}, u32[]{:S(2)}, u32[]{:S(2)}) collective-permute-start(bf16[8,4096]{1,0:T(8,128)(2,1)S(1)} %bitcast.24), channel_id=1, source_target_pairs={{0,96},{32,0},{64,32},{96,64},{1,97},{33,1},{65,33},{97,65},{2,98}... | collective-permute-start | bytes 196616 | tf_op jit(solution)/shard_map/ppermute | solution.py:149
  8.5 3.4 %collective-permute-start.11 = (bf16[8,4096]{1,0:T(8,128)(2,1)S(1)}, bf16[8,4096]{1,0:T(8,128)(2,1)S(1)}, u32[]{:S(2)}, u32[]{:S(2)}) collective-permute-start(bf16[8,4096]{1,0:T(8,128)(2,1)S(1)} %reshape.26), channel_id=1, source_target_pairs={{0,1},{1,0},{2,3},{3,2},{4,5},{5,4},{6,7},{7,6},{8,9},{9,8},{10,11... | collective-permute-start | bytes 196616 | tf_op jit(solution)/shard_map/ppermute | solution.py:153
  13.9 2.2 %copy-done = bf16[128,128,128]{2,1,0:T(8,128)(2,1)S(1)} copy-done((bf16[128,128,128]{2,1,0:T(8,128)(2,1)S(1)}, bf16[128,128,128]{2,1,0:T(8,128)(2,1)}, u32[]{:S(2)}) %copy-start) | copy-done | bytes 4194328
  16.0 3.5 %expand.4.refs_2_.refs_4_ = bf16[1024,4096]{1,0:T(8,128)(2,1)S(1)} custom-call(bf16[1024,128]{1,0:T(8,128)(2,1)S(1)} %bitcast.14, bf16[128,128,128]{2,1,0:T(8,128)(2,1)S(1)} %copy-done), custom_call_target="tpu_custom_call" | custom-call | flops 2147483648 | bytes 1048576 | tf_op jit(solution)/shard_map/expand/pallas_call | solution.py:45
  19.6 3.5 %expand.5.refs_3_.refs_5_ = bf16[1024,4096]{1,0:T(8,128)(2,1)S(1)} custom-call(bf16[1024,128]{1,0:T(8,128)(2,1)S(1)} %bitcast.15, bf16[128,128,128]{2,1,0:T(8,128)(2,1)S(1)} %copy-done), custom_call_target="tpu_custom_call" | custom-call | flops 2147483648 | bytes 1048576 | tf_op jit(solution)/shard_map/expand/pallas_call | solution.py:45
  23.1 3.5 %expand.6.refs_4_.refs_6_ = bf16[1024,4096]{1,0:T(8,128)(2,1)S(1)} custom-call(bf16[1024,128]{1,0:T(8,128)(2,1)S(1)} %bitcast.16, bf16[128,128,128]{2,1,0:T(8,128)(2,1)S(1)} %copy-done), custom_call_target="tpu_custom_call" | custom-call | flops 2147483648 | bytes 1048576 | tf_op jit(solution)/shard_map/expand/pallas_call | solution.py:45
  26.6 3.5 %expand.7.refs_5_.refs_7_ = bf16[1024,4096]{1,0:T(8,128)(2,1)S(1)} custom-call(bf16[1024,128]{1,0:T(8,128)(2,1)S(1)} %bitcast.17, bf16[128,128,128]{2,1,0:T(8,128)(2,1)S(1)} %copy-done), custom_call_target="tpu_custom_call" | custom-call | flops 2147483648 | bytes 1048576 | tf_op jit(solution)/shard_map/expand/pallas_call | solution.py:45
  30.1 2.0 %collective-permute-start.3 = (bf16[32,4096]{1,0:T(8,128)(2,1)S(1)}, bf16[32,4096]{1,0:T(8,128)(2,1)S(1)}, u32[]{:S(2)}, u32[]{:S(2)}) collective-permute-start(bf16[32,4096]{1,0:T(8,128)(2,1)S(1)} %pad_maximum_fusion), channel_id=1, source_target_pairs={{0,128},{128,0},{1,129},{129,1},{2,130},{130,2},{3,131},{131,3},{4... | collective-permute-start | bytes 786440 | tf_op jit(solution)/shard_map/ppermute | solution.py:153
  32.2 4.6 %collective-permute-start.12 = (bf16[16,4096]{1,0:T(8,128)(2,1)S(1)}, bf16[16,4096]{1,0:T(8,128)(2,1)S(1)}, u32[]{:S(2)}, u32[]{:S(2)}) collective-permute-start(bf16[16,4096]{1,0:T(8,128)(2,1)S(1)} %pad_maximum_fusion.1), channel_id=1, source_target_pairs={{0,2},{1,3},{2,0},{3,1},{4,6},{5,7},{6,4},{7,5},{8,10},{9,11},{10,... | collective-permute-start | bytes 393224 | tf_op jit(solution)/shard_map/ppermute | solution.py:153
  36.8 2.5 %collective-permute-done.3 = bf16[32,4096]{1,0:T(8,128)(2,1)S(1)} collective-permute-done((bf16[32,4096]{1,0:T(8,128)(2,1)S(1)}, bf16[32,4096]{1,0:T(8,128)(2,1)S(1)}, u32[]{:S(2)}, u32[]{:S(2)}) %collective-permute-start.3) | collective-permute-done | bytes 262176 | tf_op jit(solution)/shard_map/ppermute | solution.py:153
  39.4 7.8 %collective-permute-done.12 = bf16[16,4096]{1,0:T(8,128)(2,1)S(1)} collective-permute-done((bf16[16,4096]{1,0:T(8,128)(2,1)S(1)}, bf16[16,4096]{1,0:T(8,128)(2,1)S(1)}, u32[]{:S(2)}, u32[]{:S(2)}) %collective-permute-start.12) | collective-permute-done | bytes 131104 | tf_op jit(solution)/shard_map/ppermute | solution.py:153
  47.5 2.6 %collective-permute-start.14 = (bf16[32,4096]{1,0:T(8,128)(2,1)S(1)}, bf16[32,4096]{1,0:T(8,128)(2,1)S(1)}, u32[]{:S(2)}, u32[]{:S(2)}) collective-permute-start(bf16[32,4096]{1,0:T(8,128)(2,1)S(1)} %constant_dynamic-update-slice_fusion.5.refs_0_), channel_id=1, source_target_pairs={{0,8},{4,12},{8,0},{12,4},{1,9},{5,13},{9,1},{13,5},{2,10},{6,14},... | collective-permute-start | bytes 786440 | tf_op jit(solution)/shard_map/ppermute | solution.py:149
  50.1 9.7 %left_partial.1 = (f32[32,4096]{1,0:T(8,128)S(1)}, bf16[32,4096]{1,0:T(8,128)(2,1)S(1)}, bf16[32,4096]{1,0:T(8,128)(2,1)S(1)}, bf16[32,4096]{1,0:T(8,128)(2,1)S(1)}) custom-call(s32[16]{0:T(128)S(1)} %get-tuple-element.15.table_ref, bf16[64,4096]{1,0:T(8,128)(2,1)S(1)} %constant_dynamic-update-slice_fusion.refs_0_, ...), custom_call_target="tpu_custom_call" | custom-call | flops 8589934592 | bytes 1048576 | tf_op jit(solution)/shard_map/left_partial/pallas_call | solution.py:93
  60.7 3.8 %collective-permute-start.6 = (bf16[32,4096]{1,0:T(8,128)(2,1)S(1)}, bf16[32,4096]{1,0:T(8,128)(2,1)S(1)}, u32[]{:S(2)}, u32[]{:S(2)}) collective-permute-start(bf16[32,4096]{1,0:T(8,128)(2,1)S(1)} %get-tuple-element.23), channel_id=1, source_target_pairs={{0,8},{4,12},{8,0},{12,4},{1,9},{5,13},{9,1},{13,5},{2,10},{6,14},... | collective-permute-start | bytes 786440 | tf_op jit(solution)/shard_map/ppermute | solution.py:149
  64.5 1.3 %collective-permute-start.5 = (bf16[32,4096]{1,0:T(8,128)(2,1)S(1)}, bf16[32,4096]{1,0:T(8,128)(2,1)S(1)}, u32[]{:S(2)}, u32[]{:S(2)}) collective-permute-start(bf16[32,4096]{1,0:T(8,128)(2,1)S(1)} %get-tuple-element.22), channel_id=1, source_target_pairs={{0,4},{4,8},{8,12},{12,0},{1,5},{5,9},{9,13},{13,1},{2,6},{6,10},{... | collective-permute-start | bytes 786440 | tf_op jit(solution)/shard_map/ppermute | solution.py:149
  65.8 5.2 %right_partial.1 = (f32[64,4096]{1,0:T(8,128)S(1)}, f32[64,4096]{1,0:T(8,128)S(1)}) custom-call(s32[16]{0:T(128)S(1)} %get-tuple-element.25.table_ref, bf16[32,4096]{1,0:T(8,128)(2,1)S(1)} %constant_dynamic-update-slice_fusion.5.refs_0_, bf16[32,4096]{1,0:T(8,128)(2,1)S(1)} %collective-permute-done.13.refs_1_, ...), custom_call_target="tpu_custom_call" | custom-call | flops 4294967296 | bytes 1048576 | tf_op jit(solution)/shard_map/right_partial/pallas_call | solution.py:135
  71.1 1.5 %collective-permute-done.6 = bf16[32,4096]{1,0:T(8,128)(2,1)S(1)} collective-permute-done((bf16[32,4096]{1,0:T(8,128)(2,1)S(1)}, bf16[32,4096]{1,0:T(8,128)(2,1)S(1)}, u32[]{:S(2)}, u32[]{:S(2)}) %collective-permute-start.6) | collective-permute-done | bytes 262176 | tf_op jit(solution)/shard_map/ppermute | solution.py:149
  74.7 5.5 %collective-permute-start.9 = (bf16[8,4096]{1,0:T(8,128)(2,1)S(1)}, bf16[8,4096]{1,0:T(8,128)(2,1)S(1)}, u32[]{:S(2)}, u32[]{:S(2)}) collective-permute-start(bf16[8,4096]{1,0:T(8,128)(2,1)S(1)} %get-tuple-element.41), channel_id=1, source_target_pairs={{0,2},{1,3},{2,0},{3,1},{4,6},{5,7},{6,4},{7,5},{8,10},{9,11},{10,... | collective-permute-start | bytes 196616 | tf_op jit(solution)/shard_map/ppermute | solution.py:149
  80.1 4.4 %collective-permute-done.17 = bf16[32,4096]{1,0:T(8,128)(2,1)S(1)} collective-permute-done((bf16[32,4096]{1,0:T(8,128)(2,1)S(1)}, bf16[32,4096]{1,0:T(8,128)(2,1)S(1)}, u32[]{:S(2)}, u32[]{:S(2)}) %collective-permute-start.17) | collective-permute-done | bytes 262176 | tf_op jit(solution)/shard_map/ppermute | solution.py:153
  85.0 2.4 %collective-permute-start.19 = (bf16[8,4096]{1,0:T(8,128)(2,1)S(1)}, bf16[8,4096]{1,0:T(8,128)(2,1)S(1)}, u32[]{:S(2)}, u32[]{:S(2)}) collective-permute-start(bf16[8,4096]{1,0:T(8,128)(2,1)S(1)} %get-tuple-element.38), channel_id=1, source_target_pairs={{0,64},{32,96},{64,0},{96,32},{1,65},{33,97},{65,1},{97,33},{2,66}... | collective-permute-start | bytes 196616 | tf_op jit(solution)/shard_map/ppermute | solution.py:149
  89.0 1.8 %collective-permute-done.19 = bf16[8,4096]{1,0:T(8,128)(2,1)S(1)} collective-permute-done((bf16[8,4096]{1,0:T(8,128)(2,1)S(1)}, bf16[8,4096]{1,0:T(8,128)(2,1)S(1)}, u32[]{:S(2)}, u32[]{:S(2)}) %collective-permute-start.19) | collective-permute-done | bytes 65568 | tf_op jit(solution)/shard_map/ppermute | solution.py:149
  90.8 2.0 %collective-permute-done.18 = bf16[8,4096]{1,0:T(8,128)(2,1)S(1)} collective-permute-done((bf16[8,4096]{1,0:T(8,128)(2,1)S(1)}, bf16[8,4096]{1,0:T(8,128)(2,1)S(1)}, u32[]{:S(2)}, u32[]{:S(2)}) %collective-permute-start.18) | collective-permute-done | bytes 65568 | tf_op jit(solution)/shard_map/ppermute | solution.py:149
  (52 shorter events, 10.4 us)
Async XLA Ops:
  1.5 28.6 %collective-permute-start = (bf16[8,4096]{1,0:T(8,128)(2,1)S(1)}, bf16[8,4096]{1,0:T(8,128)(2,1)S(1)}, u32[]{:S(2)}, u32[]{:S(2)}) collective-permute-start(bf16[8,4096]{1,0:T(8,128)(2,1)S(1)} %bitcast.22), channel_id=1, source_target_pairs={{0,32},{32,64},{64,96},{96,0},{1,33},{33,65},{65,97},{97,1},{2,34}... | collective-permute-start | bytes 196616 | tf_op jit(solution)/shard_map/ppermute | solution.py:149
  3.1 27.0 %collective-permute-start.1 = (bf16[8,4096]{1,0:T(8,128)(2,1)S(1)}, bf16[8,4096]{1,0:T(8,128)(2,1)S(1)}, u32[]{:S(2)}, u32[]{:S(2)}) collective-permute-start(bf16[8,4096]{1,0:T(8,128)(2,1)S(1)} %bitcast.23), channel_id=1, source_target_pairs={{0,64},{32,96},{64,0},{96,32},{1,65},{33,97},{65,1},{97,33},{2,66}... | collective-permute-start | bytes 196616 | tf_op jit(solution)/shard_map/ppermute | solution.py:149
  5.8 24.3 %collective-permute-start.2 = (bf16[8,4096]{1,0:T(8,128)(2,1)S(1)}, bf16[8,4096]{1,0:T(8,128)(2,1)S(1)}, u32[]{:S(2)}, u32[]{:S(2)}) collective-permute-start(bf16[8,4096]{1,0:T(8,128)(2,1)S(1)} %bitcast.24), channel_id=1, source_target_pairs={{0,96},{32,0},{64,32},{96,64},{1,97},{33,1},{65,33},{97,65},{2,98}... | collective-permute-start | bytes 196616 | tf_op jit(solution)/shard_map/ppermute | solution.py:149
  8.5 23.6 %collective-permute-start.11 = (bf16[8,4096]{1,0:T(8,128)(2,1)S(1)}, bf16[8,4096]{1,0:T(8,128)(2,1)S(1)}, u32[]{:S(2)}, u32[]{:S(2)}) collective-permute-start(bf16[8,4096]{1,0:T(8,128)(2,1)S(1)} %reshape.26), channel_id=1, source_target_pairs={{0,1},{1,0},{2,3},{3,2},{4,5},{5,4},{6,7},{7,6},{8,9},{9,8},{10,11... | collective-permute-start | bytes 196616 | tf_op jit(solution)/shard_map/ppermute | solution.py:153
  13.9 2.2 %copy-start = (bf16[128,128,128]{2,1,0:T(8,128)(2,1)S(1)}, bf16[128,128,128]{2,1,0:T(8,128)(2,1)}, u32[]{:S(2)}) copy-start(bf16[128,128,128]{2,1,0:T(8,128)(2,1)} %grad_ref.3) | copy-start | bytes 12582916
  30.1 9.1 %collective-permute-start.3 = (bf16[32,4096]{1,0:T(8,128)(2,1)S(1)}, bf16[32,4096]{1,0:T(8,128)(2,1)S(1)}, u32[]{:S(2)}, u32[]{:S(2)}) collective-permute-start(bf16[32,4096]{1,0:T(8,128)(2,1)S(1)} %pad_maximum_fusion), channel_id=1, source_target_pairs={{0,128},{128,0},{1,129},{129,1},{2,130},{130,2},{3,131},{131,3},{4... | collective-permute-start | bytes 786440 | tf_op jit(solution)/shard_map/ppermute | solution.py:153
  32.2 15.0 %collective-permute-start.12 = (bf16[16,4096]{1,0:T(8,128)(2,1)S(1)}, bf16[16,4096]{1,0:T(8,128)(2,1)S(1)}, u32[]{:S(2)}, u32[]{:S(2)}) collective-permute-start(bf16[16,4096]{1,0:T(8,128)(2,1)S(1)} %pad_maximum_fusion.1), channel_id=1, source_target_pairs={{0,2},{1,3},{2,0},{3,1},{4,6},{5,7},{6,4},{7,5},{8,10},{9,11},{10,... | collective-permute-start | bytes 393224 | tf_op jit(solution)/shard_map/ppermute | solution.py:153
  39.3 10.8 %collective-permute-start.4 = (bf16[64,4096]{1,0:T(8,128)(2,1)S(1)}, bf16[64,4096]{1,0:T(8,128)(2,1)S(1)}, u32[]{:S(2)}, u32[]{:S(2)}) collective-permute-start(bf16[64,4096]{1,0:T(8,128)(2,1)S(1)} %constant_dynamic-update-slice_fusion.refs_0_), channel_id=1, source_target_pairs={{0,16},{16,0},{1,17},{17,1},{2,18},{18,2},{3,19},{19,3},{4,20},{20... | collective-permute-start | bytes 1572872 | tf_op jit(solution)/shard_map/ppermute | solution.py:153
  47.2 17.3 %collective-permute-start.13 = (bf16[32,4096]{1,0:T(8,128)(2,1)S(1)}, bf16[32,4096]{1,0:T(8,128)(2,1)S(1)}, u32[]{:S(2)}, u32[]{:S(2)}) collective-permute-start(bf16[32,4096]{1,0:T(8,128)(2,1)S(1)} %constant_dynamic-update-slice_fusion.5.refs_0_), channel_id=1, source_target_pairs={{0,4},{4,8},{8,12},{12,0},{1,5},{5,9},{9,13},{13,1},{2,6},{6,10},{... | collective-permute-start | bytes 786440 | tf_op jit(solution)/shard_map/ppermute | solution.py:149
  47.5 18.3 %collective-permute-start.14 = (bf16[32,4096]{1,0:T(8,128)(2,1)S(1)}, bf16[32,4096]{1,0:T(8,128)(2,1)S(1)}, u32[]{:S(2)}, u32[]{:S(2)}) collective-permute-start(bf16[32,4096]{1,0:T(8,128)(2,1)S(1)} %constant_dynamic-update-slice_fusion.5.refs_0_), channel_id=1, source_target_pairs={{0,8},{4,12},{8,0},{12,4},{1,9},{5,13},{9,1},{13,5},{2,10},{6,14},... | collective-permute-start | bytes 786440 | tf_op jit(solution)/shard_map/ppermute | solution.py:149
  50.1 15.7 %collective-permute-start.15 = (bf16[32,4096]{1,0:T(8,128)(2,1)S(1)}, bf16[32,4096]{1,0:T(8,128)(2,1)S(1)}, u32[]{:S(2)}, u32[]{:S(2)}) collective-permute-start(bf16[32,4096]{1,0:T(8,128)(2,1)S(1)} %constant_dynamic-update-slice_fusion.5.refs_0_), channel_id=1, source_target_pairs={{0,12},{4,0},{8,4},{12,8},{1,13},{5,1},{9,5},{13,9},{2,14},{6,2},{... | collective-permute-start | bytes 786440 | tf_op jit(solution)/shard_map/ppermute | solution.py:149
  59.7 11.4 %collective-permute-start.7 = (bf16[32,4096]{1,0:T(8,128)(2,1)S(1)}, bf16[32,4096]{1,0:T(8,128)(2,1)S(1)}, u32[]{:S(2)}, u32[]{:S(2)}) collective-permute-start(bf16[32,4096]{1,0:T(8,128)(2,1)S(1)} %get-tuple-element.24), channel_id=1, source_target_pairs={{0,12},{4,0},{8,4},{12,8},{1,13},{5,1},{9,5},{13,9},{2,14},{6,2},{... | collective-permute-start | bytes 786440 | tf_op jit(solution)/shard_map/ppermute | solution.py:149
  60.7 11.9 %collective-permute-start.6 = (bf16[32,4096]{1,0:T(8,128)(2,1)S(1)}, bf16[32,4096]{1,0:T(8,128)(2,1)S(1)}, u32[]{:S(2)}, u32[]{:S(2)}) collective-permute-start(bf16[32,4096]{1,0:T(8,128)(2,1)S(1)} %get-tuple-element.23), channel_id=1, source_target_pairs={{0,8},{4,12},{8,0},{12,4},{1,9},{5,13},{9,1},{13,5},{2,10},{6,14},... | collective-permute-start | bytes 786440 | tf_op jit(solution)/shard_map/ppermute | solution.py:149
  64.5 8.1 %collective-permute-start.5 = (bf16[32,4096]{1,0:T(8,128)(2,1)S(1)}, bf16[32,4096]{1,0:T(8,128)(2,1)S(1)}, u32[]{:S(2)}, u32[]{:S(2)}) collective-permute-start(bf16[32,4096]{1,0:T(8,128)(2,1)S(1)} %get-tuple-element.22), channel_id=1, source_target_pairs={{0,4},{4,8},{8,12},{12,0},{1,5},{5,9},{9,13},{13,1},{2,6},{6,10},{... | collective-permute-start | bytes 786440 | tf_op jit(solution)/shard_map/ppermute | solution.py:149
  71.0 2.7 %collective-permute-start.16 = (f32[64,4096]{1,0:T(8,128)S(1)}, f32[64,4096]{1,0:T(8,128)S(1)}, u32[]{:S(2)}, u32[]{:S(2)}) collective-permute-start(f32[64,4096]{1,0:T(8,128)S(1)} %get-tuple-element.27), channel_id=1, source_target_pairs={{0,16},{16,0},{1,17},{17,1},{2,18},{18,2},{3,19},{19,3},{4,20},{20... | collective-permute-start | bytes 3145736 | tf_op jit(solution)/shard_map/ppermute | solution.py:153
  73.9 10.6 %collective-permute-start.17 = (bf16[32,4096]{1,0:T(8,128)(2,1)S(1)}, bf16[32,4096]{1,0:T(8,128)(2,1)S(1)}, u32[]{:S(2)}, u32[]{:S(2)}) collective-permute-start(bf16[32,4096]{1,0:T(8,128)(2,1)S(1)} %slice.71), channel_id=1, source_target_pairs={{0,128},{128,0},{1,129},{129,1},{2,130},{130,2},{3,131},{131,3},{4... | collective-permute-start | bytes 786440 | tf_op jit(solution)/shard_map/ppermute | solution.py:153
  74.1 13.3 %collective-permute-start.10 = (bf16[8,4096]{1,0:T(8,128)(2,1)S(1)}, bf16[8,4096]{1,0:T(8,128)(2,1)S(1)}, u32[]{:S(2)}, u32[]{:S(2)}) collective-permute-start(bf16[8,4096]{1,0:T(8,128)(2,1)S(1)} %get-tuple-element.40), channel_id=1, source_target_pairs={{0,3},{1,0},{2,1},{3,2},{4,7},{5,4},{6,5},{7,6},{8,11},{9,8},{10,9... | collective-permute-start | bytes 196616 | tf_op jit(solution)/shard_map/ppermute | solution.py:149
  74.7 12.7 %collective-permute-start.9 = (bf16[8,4096]{1,0:T(8,128)(2,1)S(1)}, bf16[8,4096]{1,0:T(8,128)(2,1)S(1)}, u32[]{:S(2)}, u32[]{:S(2)}) collective-permute-start(bf16[8,4096]{1,0:T(8,128)(2,1)S(1)} %get-tuple-element.41), channel_id=1, source_target_pairs={{0,2},{1,3},{2,0},{3,1},{4,6},{5,7},{6,4},{7,5},{8,10},{9,11},{10,... | collective-permute-start | bytes 196616 | tf_op jit(solution)/shard_map/ppermute | solution.py:149
  80.1 7.3 %collective-permute-start.8 = (bf16[8,4096]{1,0:T(8,128)(2,1)S(1)}, bf16[8,4096]{1,0:T(8,128)(2,1)S(1)}, u32[]{:S(2)}, u32[]{:S(2)}) collective-permute-start(bf16[8,4096]{1,0:T(8,128)(2,1)S(1)} %get-tuple-element.39), channel_id=1, source_target_pairs={{0,1},{1,2},{2,3},{3,0},{4,5},{5,6},{6,7},{7,4},{8,9},{9,10},{10,1... | collective-permute-start | bytes 196616 | tf_op jit(solution)/shard_map/ppermute | solution.py:149
  84.7 4.3 %collective-permute-start.20 = (bf16[8,4096]{1,0:T(8,128)(2,1)S(1)}, bf16[8,4096]{1,0:T(8,128)(2,1)S(1)}, u32[]{:S(2)}, u32[]{:S(2)}) collective-permute-start(bf16[8,4096]{1,0:T(8,128)(2,1)S(1)} %get-tuple-element.37), channel_id=1, source_target_pairs={{0,96},{32,0},{64,32},{96,64},{1,97},{33,1},{65,33},{97,65},{2,98}... | collective-permute-start | bytes 196616 | tf_op jit(solution)/shard_map/ppermute | solution.py:149
  85.0 5.8 %collective-permute-start.19 = (bf16[8,4096]{1,0:T(8,128)(2,1)S(1)}, bf16[8,4096]{1,0:T(8,128)(2,1)S(1)}, u32[]{:S(2)}, u32[]{:S(2)}) collective-permute-start(bf16[8,4096]{1,0:T(8,128)(2,1)S(1)} %get-tuple-element.38), channel_id=1, source_target_pairs={{0,64},{32,96},{64,0},{96,32},{1,65},{33,97},{65,1},{97,33},{2,66}... | collective-permute-start | bytes 196616 | tf_op jit(solution)/shard_map/ppermute | solution.py:149
  87.4 5.5 %collective-permute-start.18 = (bf16[8,4096]{1,0:T(8,128)(2,1)S(1)}, bf16[8,4096]{1,0:T(8,128)(2,1)S(1)}, u32[]{:S(2)}, u32[]{:S(2)}) collective-permute-start(bf16[8,4096]{1,0:T(8,128)(2,1)S(1)} %get-tuple-element.36), channel_id=1, source_target_pairs={{0,32},{32,64},{64,96},{96,0},{1,33},{33,65},{65,97},{97,1},{2,34}... | collective-permute-start | bytes 196616 | tf_op jit(solution)/shard_map/ppermute | solution.py:149

commit v3 on v2

--- a/solution.py
+++ b/solution.py
@@ -18,39 +18,85 @@
     return pltpu.CompilerParams(vmem_limit_bytes=VMEM)
 
 
-def expand(pair_grad, weights, channels, number):
+def expand(pair_grad, weights, channels, number, after=()):
     rows, width, cols = pair_grad.shape
     wide = weights.shape[0]
     entries = wide // channels
     held = rows // PIECES
-    step = 8
-
-    def body(weight_ref, grad_ref, out_ref):
-        def two(t, carry):
+    step = 2
+    chunk = 8
+    first = number == 0
+
+    def body(weight_ref, grad_ref, *rest):
+        out_ref, token_ref, *rest = rest[len(after) :]
+        copies = []
+        if first:
+            source_ref = grad_ref
+            grad_ref, sems = rest
+            for k in range(rows // chunk):
+                part = pl.ds(k * chunk, chunk)
+                copies.append(pltpu.make_async_copy(source_ref.at[part], grad_ref.at[part], sems.at[k]))
+                copies[k].start()
+        for t in range(held // 2):
+            if first and t * 2 % chunk == 0:
+                copies[t * 2 // chunk].wait()
             i = number * held + t * 2
             pair = jnp.concatenate([grad_ref[i], grad_ref[i + 1]], axis=1)
-            base = pl.multiple_of(t * (2 * channels), 2 * channels)
-            for first in range(0, entries, step):
-                piece = weight_ref[first * channels : (first + step) * channels, :]
+            base = t * 2 * channels
+            for entry in range(0, entries, step):
+                piece = weight_ref[entry * channels : (entry + step) * channels, :]
                 value = jnp.dot(piece, pair, preferred_element_type=jnp.float32).astype(jnp.bfloat16)
                 for k in range(step):
                     block = value[k * channels : (k + 1) * channels]
                     stacked = jnp.concatenate([block[:, :cols], block[:, cols:]], axis=0)
-                    side = (first + k) * cols
-                    out_ref[pl.ds(base, 2 * channels), side : side + cols] = stacked
-            return carry
-
-        lax.fori_loop(0, held // 2, two, 0, unroll=2)
-
-    return pl.pallas_call(
-        body,
-        in_specs=[WHOLE, WHOLE],
-        out_specs=WHOLE,
-        out_shape=pltpu.VMEM((held * channels, entries * cols), jnp.bfloat16),
+                    side = (entry + k) * cols
+                    out_ref[base : base + 2 * channels, side : side + cols] = stacked
+        for copy in copies[held // chunk :]:
+            copy.wait()
+        token_ref[...] = out_ref[:16, :128]
+
+    moved_shape = pltpu.VMEM(pair_grad.shape, pair_grad.dtype)
+    return pl.pallas_call(
+        body,
+        in_specs=[WHOLE, pl.BlockSpec(memory_space=pltpu.HBM) if first else WHOLE] + [WHOLE] * len(after),
+        out_specs=[WHOLE] * (3 if first else 2),
+        out_shape=[
+            pltpu.VMEM((held * channels, entries * cols), jnp.bfloat16),
+            jax.ShapeDtypeStruct((16, 128), jnp.bfloat16),
+        ]
+        + ([moved_shape] if first else []),
+        scratch_shapes=[pltpu.SemaphoreType.DMA((rows // chunk,))] if first else [],
         compiler_params=params(),
         cost_estimate=pl.CostEstimate(flops=4 * held * wide * width * cols, transcendentals=0, bytes_accessed=1 << 20),
         name="expand",
-    )(weights, pair_grad)
+    )(weights, pair_grad, *after)
+
+
+def join(groups, after):
+    parts = [part for group in groups for part in group]
+
+    def body(*refs):
+        source_refs = refs[: len(parts)]
+        out_refs = refs[len(parts) + len(after) : -1]
+        at = 0
+        for group, out_ref in zip(groups, out_refs):
+            top = 0
+            for part in group:
+                out_ref[top : top + part.shape[0], :] = source_refs[at][...]
+                top += part.shape[0]
+                at += 1
+        refs[-1][...] = refs[len(parts)][...]
+
+    shapes = [(sum(part.shape[0] for part in group), group[0].shape[1]) for group in groups] + [after[0].shape]
+    return pl.pallas_call(
+        body,
+        in_specs=[WHOLE] * (len(parts) + len(after)),
+        out_specs=[WHOLE] * len(shapes),
+        out_shape=[jax.ShapeDtypeStruct(shape, jnp.bfloat16) for shape in shapes],
+        compiler_params=params(),
+        cost_estimate=pl.CostEstimate(flops=0, transcendentals=0, bytes_accessed=1 << 20),
+        name="join",
+    )(*parts, *after)
 
 
 def place(scratch, table_ref, sources, size):
@@ -72,7 +118,7 @@
     def body(table_ref, *refs):
         source_refs = refs[: len(sources)]
         expanded_refs = refs[len(sources) : len(sources) + len(expanded)]
-        own_ref, *other_refs = refs[len(sources) + len(expanded) : -2]
+        token_ref, own_ref, *other_refs = refs[len(sources) + len(expanded) : -2]
         placed, turned = refs[-2:]
         place(placed, table_ref, source_refs, size)
         turned[...] = placed[...].reshape(sequences, depth).T
@@ -88,13 +134,20 @@
                     lower = (k + 1) * part
                     other_ref[:, at : at + block] = value[lower : lower + part].astype(jnp.bfloat16)
                 at += block
+        token_ref[...] = other_refs[0][:16, :128]
 
     other = jax.ShapeDtypeStruct((part, total), jnp.bfloat16)
     return pl.pallas_call(
         body,
         in_specs=[TABLE] + [WHOLE] * (len(sources) + len(expanded)),
-        out_specs=[WHOLE] * 4,
-        out_shape=[jax.ShapeDtypeStruct((part, total), jnp.float32), other, other, other],
+        out_specs=[WHOLE] * 5,
+        out_shape=[
+            jax.ShapeDtypeStruct((16, 128), jnp.bfloat16),
+            jax.ShapeDtypeStruct((part, total), jnp.float32),
+            other,
+            other,
+            other,
+        ],
         scratch_shapes=[pltpu.VMEM((count, size, depth), jnp.bfloat16), pltpu.VMEM((depth, sequences), jnp.bfloat16)],
         compiler_params=params(),
         cost_estimate=pl.CostEstimate(flops=4 * sequences * depth * total, transcendentals=0, bytes_accessed=1 << 20),
@@ -102,7 +155,7 @@
     )(table, *sources, *expanded)
 
 
-def right_partial(table, sources, expanded, size, inverse):
+def right_partial(table, sources, expanded, size, inverse, after):
     count = table.shape[0]
     sequences = count * size
     depth = sum(e.shape[0] for e in expanded)
@@ -113,7 +166,7 @@
     def body(table_ref, *refs):
         source_refs = refs[: len(sources)]
         expanded_refs = refs[len(sources) : len(sources) + len(expanded)]
-        own_ref, other_ref, blocked, placed = refs[len(sources) + len(expanded) :]
+        own_ref, other_ref, blocked, placed = refs[len(sources) + len(expanded) + 1 :]
         place(blocked, table_ref, source_refs, size)
         placed[...] = blocked[...].reshape(sequences, depth)
         for side in range(0, total, block):
@@ -134,14 +187,14 @@
     half = jax.ShapeDtypeStruct((part, total), jnp.float32)
     return pl.pallas_call(
         body,
-        in_specs=[TABLE] + [WHOLE] * (len(sources) + len(expanded)),
+        in_specs=[TABLE] + [WHOLE] * (len(sources) + len(expanded) + 1),
         out_specs=[WHOLE] * 2,
         out_shape=[half, half],
         scratch_shapes=[pltpu.VMEM((count, size, depth), jnp.bfloat16), pltpu.VMEM((sequences, depth), jnp.bfloat16)],
         compiler_params=params(),
         cost_estimate=pl.CostEstimate(flops=2 * sequences * depth * total, transcendentals=0, bytes_accessed=1 << 20),
         name="right_partial",
-    )(table, *sources, *expanded)
+    )(table, *sources, *expanded, after)
 
 
 def moved(value, axis, distance):
@@ -156,10 +209,10 @@
 def orders(blocks):
     z_lo, x, core, y, z_hi = (lax.axis_index(name) for name in ROW + COL)
     at = lax.iota(jnp.int32, blocks)
-    block = (z_lo ^ (at // 4 % 2)) * 8 + (x - at) % 4 * 2 + (core ^ (at // 8))
+    block = (z_lo ^ (at % 2)) * 8 + (x - at // 2) % 4 * 2 + (core ^ (at // 8))
     left_table = (block // 4 - y) % 4 * 4 + (block - z_hi) % 4
     block = (y - at // 4) % 4 * 4 + (z_hi ^ (at % 4))
-    right_table = (block - core) % 2 * 8 + (block // 8 - z_lo) % 2 * 4 + (block // 2 - x) % 4
+    right_table = (block - core) % 2 * 8 + (block // 2 - x) % 4 * 2 + (block // 8 - z_lo) % 2
     return left_table, right_table
 
 
@@ -173,20 +226,25 @@
     blocks = 4 * 4
     inverse = 1.0 / (blocks * shared)
     left_table, right_table = orders(blocks)
-    left_table, right_table, pair_grad = lax.optimization_barrier((left_table, right_table, pair_grad))
-
-    along_x = jnp.concatenate([right_flat] + [moved(right_flat, "x", d) for d in (1, 2, 3)], axis=0)
-    near_left = jnp.concatenate([left_flat, swapped(left_flat, "z_hi", 1)], axis=0)
-    near_left = jnp.concatenate([near_left, swapped(near_left, "z_hi", 2)], axis=0)
-    along_z = jnp.concatenate([along_x, swapped(along_x, "z_lo", 1)], axis=0)
-    along_core = swapped(along_z, "core", 1)
-
-    expanded = [expand(pair_grad, weights, channels, number) for number in range(PIECES)]
-    own, *others = left_partial(left_table, [along_z, along_core], expanded, held, inverse)
-
-    far_left = [near_left] + [moved(near_left, "y", d) for d in (1, 2, 3)]
-    right_table, others = lax.optimization_barrier((right_table, others))
-    right_own, right_other = right_partial(right_table, far_left, expanded, shared, inverse)
+    left_table, right_table, weights = lax.optimization_barrier((left_table, right_table, weights))
+
+    from_z = swapped(right_flat, "z_lo", 1)
+    from_hi = swapped(left_flat, "z_hi", 1)
+    piece, token, pair_grad = expand(pair_grad, weights, channels, 0)
+    expanded = [piece]
+    near_right, near_left, token = join([[right_flat, from_z], [left_flat, from_hi]], [token])
+    from_x = [moved(near_right, "x", d) for d in (1, 2, 3)]
+    from_hi = swapped(near_left, "z_hi", 2)
+    for number in (1, 2):
+        piece, token = expand(pair_grad, weights, channels, number, [token])
+        expanded.append(piece)
+    along_x, along_z, token = join([[near_right, *from_x], [near_left, from_hi]], [token])
+    right_sources = [along_x, swapped(along_x, "core", 1)]
+    left_sources = [along_z] + [moved(along_z, "y", d) for d in (1, 2, 3)]
+    expanded.append(expand(pair_grad, weights, channels, 3, [token])[0])
+
+    token, own, *others = left_partial(left_table, right_sources, expanded, held, inverse)
+    right_own, right_other = right_partial(right_table, left_sources, expanded, shared, inverse, token)
 
     left_sum = own
     for d, other in enumerate(others):
@@ -198,12 +256,12 @@
     left_grad = jnp.swapaxes(left_grad.reshape(shared, rows, channels), 1, 2)
 
     right_sum = right_own + swapped(right_other, "core", 1)
-    middle = 4 * held
-    right_sum = right_sum[:middle] + swapped(right_sum[middle:].astype(jnp.bfloat16), "z_lo", 1).astype(jnp.float32)
-    right_grad = right_sum[:held]
+    part = 2 * held
+    right_near = right_sum[:part]
     for d in (1, 2, 3):
-        piece = right_sum[d * held : (d + 1) * held].astype(jnp.bfloat16)
-        right_grad = right_grad + moved(piece, "x", d).astype(jnp.float32)
+        piece = right_sum[d * part : (d + 1) * part].astype(jnp.bfloat16)
+        right_near = right_near + moved(piece, "x", d).astype(jnp.float32)
+    right_grad = right_near[:held] + swapped(right_near[held:].astype(jnp.bfloat16), "z_lo", 1).astype(jnp.float32)
     return (left_grad, right_grad.reshape(held, entries, cols))
 
 

time: 93.9 us -> 83 us (0.88)
  waiting for transfers between devices: 21.6 us -> 12.2 us
  Pallas kernels: 28.8 us -> 25.3 us
  starting transfers between devices: 33.7 us -> 36.9 us
    ppermute x6, waiting for transfers between devices: 15.7 us -> 2 us  [swapped(): lax.ppermute(value, axis, [(k, k ^ bit) for k in range(lax.axis_size(axis...]
    ppermute x15, waiting for transfers between devices: 5.94 us -> 10.2 us  [moved(): lax.ppermute(value, axis, [(k, (k + distance) % size) for k in range(size)])]
    pallas_call x4 -> x6, Pallas kernels: 14 us -> 10.4 us  [the longest x4 10.3 us: expand(): pl.pallas_call(body, in_specs=[WHOLE, pl.BlockSpec(memory_space=pltpu.HBM...]
    ppermute x6, starting transfers between devices: 10.2 us -> 12.2 us  [swapped(): lax.ppermute(value, axis, [(k, k ^ bit) for k in range(lax.axis_size(axis...]
    ppermute x15, starting transfers between devices: 23.5 us -> 24.7 us  [moved(): lax.ppermute(value, axis, [(k, (k + distance) % size) for k in range(size)])]
    unnamed x11 -> x5, local copies, waits for them, and re-layouts: 5.47 us -> 4.57 us
  transfers between devices with their start and end apart: 21 -> 21, of which waited for: 8 -> 6; matrix products, arithmetic and copies ran while one was open for 5% -> 4% of each run, Pallas kernels for 31% -> 31%
where the time goes in v3:
time: 83 us; the launch traced here: 82.8 us
  starting transfers between devices  36.9 us (44%)
  Pallas kernels  25.3 us (30%)
  waiting for transfers between devices  12.2 us (15%)
  local copies, waits for them, and re-layouts  7.13 us (9%)
    ppermute x15, starting transfers between devices, moved(): lax.ppermute(value, axis, [(k, (k + distance) % size) for k in range(size)])  24.7 us
    ppermute x6, starting transfers between devices, swapped(): lax.ppermute(value, axis, [(k, k ^ bit) for k in range(lax.axis_size(axis...  12.2 us
    pallas_call x4, Pallas kernels, expand(): pl.pallas_call(body, in_specs=[WHOLE, pl.BlockSpec(memory_space=pltpu.HBM...  10.3 us
    ppermute x15, waiting for transfers between devices, moved(): lax.ppermute(value, axis, [(k, (k + distance) % size) for k in range(size)])  10.2 us
    pallas_call x1, Pallas kernels, left_partial(): pl.pallas_call(body, in_specs=[TABLE] + [WHOLE] * (len(sources) + len(exp...  9.67 us
    pallas_call x1, Pallas kernels, right_partial(): pl.pallas_call(body, in_specs=[TABLE] + [WHOLE] * (len(sources) + len(exp...  5.3 us
    unnamed x5, local copies, waits for them, and re-layouts  4.57 us
    ppermute x6, waiting for transfers between devices, swapped(): lax.ppermute(value, axis, [(k, k ^ bit) for k in range(lax.axis_size(axis...  2 us
  transfers between devices with their start and end apart: 21, of which 6 were waited for; matrix products, arithmetic and copies ran while one was open for 4% of the time, Pallas kernels for 31%

profile of v3, /device:TPU:24, one launch (start us, length us, event | category | flops | bytes accessed | tf_op | source)
XLA Modules:
  0.0 82.8 jit_solution(16060154727862850577)
XLA Ops:
  1.9 3.4 %collective-permute-start.1 = (bf16[8,4096]{1,0:T(8,128)(2,1)S(1)}, bf16[8,4096]{1,0:T(8,128)(2,1)S(1)}, u32[]{:S(2)}, u32[]{:S(2)}) collective-permute-start(bf16[8,4096]{1,0:T(8,128)(2,1)S(1)} %reshape.25.refs_2_), channel_id=1, source_target_pairs={{0,1},{1,0},{2,3},{3,2},{4,5},{5,4},{6,7},{7,6},{8,9},{9,8},{10,11... | collective-permute-start | bytes 196616 | tf_op jit(solution)/shard_map/ppermute | solution.py:206
  6.2 2.0 %collective-permute-start = (bf16[8,4096]{1,0:T(8,128)(2,1)S(1)}, bf16[8,4096]{1,0:T(8,128)(2,1)S(1)}, u32[]{:S(2)}, u32[]{:S(2)}) collective-permute-start(bf16[8,4096]{1,0:T(8,128)(2,1)S(1)} %bitcast.16), channel_id=1, source_target_pairs={{0,128},{128,0},{1,129},{129,1},{2,130},{130,2},{3,131},{131,3},{4... | collective-permute-start | bytes 196616 | tf_op jit(solution)/shard_map/ppermute | solution.py:206
  9.3 2.2 %copy-done = bf16[128,128,128]{2,1,0:T(8,128)(2,1)S(1)} copy-done((bf16[128,128,128]{2,1,0:T(8,128)(2,1)S(1)}, bf16[128,128,128]{2,1,0:T(8,128)(2,1)}, u32[]{:S(2)}) %copy-start) | copy-done | bytes 4194328
  11.4 3.3 %expand.4 = (bf16[1024,4096]{1,0:T(8,128)(2,1)S(1)}, bf16[16,128]{1,0:T(8,128)(2,1)S(1)}, bf16[128,128,128]{2,1,0:T(8,128)(2,1)S(1)}) custom-call(bf16[1024,128]{1,0:T(8,128)(2,1)S(1)} %bitcast.12, bf16[128,128,128]{2,1,0:T(8,128)(2,1)S(1)} %copy-done), custom_call_target="tpu_custom_call" | custom-call | flops 2147483648 | bytes 1048576 | tf_op jit(solution)/shard_map/expand/pallas_call | solution.py:59
  14.8 1.6 %collective-permute-start.2 = (bf16[16,4096]{1,0:T(8,128)(2,1)S(1)}, bf16[16,4096]{1,0:T(8,128)(2,1)S(1)}, u32[]{:S(2)}, u32[]{:S(2)}) collective-permute-start(bf16[16,4096]{1,0:T(8,128)(2,1)S(1)} %get-tuple-element.29.refs_0_), channel_id=1, source_target_pairs={{0,32},{32,64},{64,96},{96,0},{1,33},{33,65},{65,97},{97,1},{2,34}... | collective-permute-start | bytes 393224 | tf_op jit(solution)/shard_map/ppermute | solution.py:202
  16.4 2.7 %collective-permute-start.3 = (bf16[16,4096]{1,0:T(8,128)(2,1)S(1)}, bf16[16,4096]{1,0:T(8,128)(2,1)S(1)}, u32[]{:S(2)}, u32[]{:S(2)}) collective-permute-start(bf16[16,4096]{1,0:T(8,128)(2,1)S(1)} %get-tuple-element.29.refs_0_), channel_id=1, source_target_pairs={{0,64},{32,96},{64,0},{96,32},{1,65},{33,97},{65,1},{97,33},{2,66}... | collective-permute-start | bytes 393224 | tf_op jit(solution)/shard_map/ppermute | solution.py:202
  19.1 1.4 %collective-permute-start.4 = (bf16[16,4096]{1,0:T(8,128)(2,1)S(1)}, bf16[16,4096]{1,0:T(8,128)(2,1)S(1)}, u32[]{:S(2)}, u32[]{:S(2)}) collective-permute-start(bf16[16,4096]{1,0:T(8,128)(2,1)S(1)} %get-tuple-element.29.refs_0_), channel_id=1, source_target_pairs={{0,96},{32,0},{64,32},{96,64},{1,97},{33,1},{65,33},{97,65},{2,98}... | collective-permute-start | bytes 393224 | tf_op jit(solution)/shard_map/ppermute | solution.py:202
  20.5 4.5 %collective-permute-start.5 = (bf16[16,4096]{1,0:T(8,128)(2,1)S(1)}, bf16[16,4096]{1,0:T(8,128)(2,1)S(1)}, u32[]{:S(2)}, u32[]{:S(2)}) collective-permute-start(bf16[16,4096]{1,0:T(8,128)(2,1)S(1)} %get-tuple-element.30.refs_4_), channel_id=1, source_target_pairs={{0,2},{1,3},{2,0},{3,1},{4,6},{5,7},{6,4},{7,5},{8,10},{9,11},{10,... | collective-permute-start | bytes 393224 | tf_op jit(solution)/shard_map/ppermute | solution.py:206
  25.0 2.3 %expand.5 = (bf16[1024,4096]{1,0:T(8,128)(2,1)S(1)}, bf16[16,128]{1,0:T(8,128)(2,1)S(1)}) custom-call(bf16[1024,128]{1,0:T(8,128)(2,1)S(1)} %bitcast.13, bf16[128,128,128]{2,1,0:T(8,128)(2,1)S(1)} %get-tuple-element.31.grad_ref, bf16[16,128]{1,0:T(8,128)(2,1)S(1)} %get-tuple-element.32.rest_0_), custom_call_target="tpu_custom_call" | custom-call | flops 2147483648 | bytes 1048576 | tf_op jit(solution)/shard_map/expand/pallas_call | solution.py:59
  27.3 2.3 %expand.6 = (bf16[1024,4096]{1,0:T(8,128)(2,1)S(1)}, bf16[16,128]{1,0:T(8,128)(2,1)S(1)}) custom-call(bf16[1024,128]{1,0:T(8,128)(2,1)S(1)} %bitcast.14, bf16[128,128,128]{2,1,0:T(8,128)(2,1)S(1)} %get-tuple-element.31.grad_ref, bf16[16,128]{1,0:T(8,128)(2,1)S(1)} %get-tuple-element.33.rest_0_), custom_call_target="tpu_custom_call" | custom-call | flops 2147483648 | bytes 1048576 | tf_op jit(solution)/shard_map/expand/pallas_call | solution.py:59
  31.1 2.6 %collective-permute-start.14 = (bf16[32,4096]{1,0:T(8,128)(2,1)S(1)}, bf16[32,4096]{1,0:T(8,128)(2,1)S(1)}, u32[]{:S(2)}, u32[]{:S(2)}) collective-permute-start(bf16[32,4096]{1,0:T(8,128)(2,1)S(1)} %get-tuple-element.46.refs_0_), channel_id=1, source_target_pairs={{0,8},{4,12},{8,0},{12,4},{1,9},{5,13},{9,1},{13,5},{2,10},{6,14},... | collective-permute-start | bytes 786440 | tf_op jit(solution)/shard_map/ppermute | solution.py:202
  33.7 2.3 %expand.7 = (bf16[1024,4096]{1,0:T(8,128)(2,1)S(1)}, bf16[16,128]{1,0:T(8,128)(2,1)}) custom-call(bf16[1024,128]{1,0:T(8,128)(2,1)S(1)} %bitcast.15, bf16[128,128,128]{2,1,0:T(8,128)(2,1)S(1)} %get-tuple-element.31.grad_ref, bf16[16,128]{1,0:T(8,128)(2,1)S(1)} %get-tuple-element.39.rest_0_), custom_call_target="tpu_custom_call" | custom-call | flops 2147483648 | bytes 1048576 | tf_op jit(solution)/shard_map/expand/pallas_call | solution.py:59
  36.0 9.7 %left_partial.1 = (bf16[16,128]{1,0:T(8,128)(2,1)S(1)}, f32[32,4096]{1,0:T(8,128)S(1)}, bf16[32,4096]{1,0:T(8,128)(2,1)S(1)}, bf16[32,4096]{1,0:T(8,128)(2,1)S(1)}, bf16[32,4096]{1,0:T(8,128)(2,1)S(1)}) custom-call(s32[16]{0:T(128)S(1)} %get-tuple-element.26.table_ref, bf16[64,4096]{1,0:T(8,128)(2,1)S(1)} %get-tuple-element.35.refs_0_, ...), custom_call_target="tpu_custom_call" | custom-call | flops 8589934592 | bytes 1048576 | tf_op jit(solution)/shard_map/left_partial/pallas_call | solution.py:140
  45.7 3.3 %collective-permute-start.7 = (bf16[32,4096]{1,0:T(8,128)(2,1)S(1)}, bf16[32,4096]{1,0:T(8,128)(2,1)S(1)}, u32[]{:S(2)}, u32[]{:S(2)}) collective-permute-start(bf16[32,4096]{1,0:T(8,128)(2,1)S(1)} %get-tuple-element.42), channel_id=1, source_target_pairs={{0,4},{4,8},{8,12},{12,0},{1,5},{5,9},{9,13},{13,1},{2,6},{6,10},{... | collective-permute-start | bytes 786440 | tf_op jit(solution)/shard_map/ppermute | solution.py:202
  49.2 1.3 %collective-permute-start.9 = (bf16[32,4096]{1,0:T(8,128)(2,1)S(1)}, bf16[32,4096]{1,0:T(8,128)(2,1)S(1)}, u32[]{:S(2)}, u32[]{:S(2)}) collective-permute-start(bf16[32,4096]{1,0:T(8,128)(2,1)S(1)} %get-tuple-element.44), channel_id=1, source_target_pairs={{0,12},{4,0},{8,4},{12,8},{1,13},{5,1},{9,5},{13,9},{2,14},{6,2},{... | collective-permute-start | bytes 786440 | tf_op jit(solution)/shard_map/ppermute | solution.py:202
  50.6 5.3 %right_partial.1 = (f32[64,4096]{1,0:T(8,128)S(1)}, f32[64,4096]{1,0:T(8,128)S(1)}) custom-call(s32[16]{0:T(128)S(1)} %get-tuple-element.45.table_ref, bf16[32,4096]{1,0:T(8,128)(2,1)S(1)} %get-tuple-element.46.refs_0_, bf16[32,4096]{1,0:T(8,128)(2,1)S(1)} %collective-permute-done.13.refs_1_, bf16[32,4096]{1,0:T(8,128)(2,1)S(1)} %collective-permute-done.14.refs_2_, ...), custom_call_target="tpu_custom_call" | custom-call | flops 4294967296 | bytes 1048576 | tf_op jit(solution)/shard_map/right_partial/pallas_call | solution.py:188
  56.0 4.0 %collective-permute-done.7 = bf16[32,4096]{1,0:T(8,128)(2,1)S(1)} collective-permute-done((bf16[32,4096]{1,0:T(8,128)(2,1)S(1)}, bf16[32,4096]{1,0:T(8,128)(2,1)S(1)}, u32[]{:S(2)}, u32[]{:S(2)}) %collective-permute-start.7) | collective-permute-done | bytes 262176 | tf_op jit(solution)/shard_map/ppermute | solution.py:202
  60.0 3.6 %collective-permute-done.9 = bf16[32,4096]{1,0:T(8,128)(2,1)S(1)} collective-permute-done((bf16[32,4096]{1,0:T(8,128)(2,1)S(1)}, bf16[32,4096]{1,0:T(8,128)(2,1)S(1)}, u32[]{:S(2)}, u32[]{:S(2)}) %collective-permute-start.9) | collective-permute-done | bytes 262176 | tf_op jit(solution)/shard_map/ppermute | solution.py:202
  65.5 1.9 %collective-permute-start.19 = (bf16[16,4096]{1,0:T(8,128)(2,1)S(1)}, bf16[16,4096]{1,0:T(8,128)(2,1)S(1)}, u32[]{:S(2)}, u32[]{:S(2)}) collective-permute-start(bf16[16,4096]{1,0:T(8,128)(2,1)S(1)} %get-tuple-element.59), channel_id=1, source_target_pairs={{0,96},{32,0},{64,32},{96,64},{1,97},{33,1},{65,33},{97,65},{2,98}... | collective-permute-start | bytes 393224 | tf_op jit(solution)/shard_map/ppermute | solution.py:202
  68.2 4.4 %collective-permute-start.11 = (bf16[8,4096]{1,0:T(8,128)(2,1)S(1)}, bf16[8,4096]{1,0:T(8,128)(2,1)S(1)}, u32[]{:S(2)}, u32[]{:S(2)}) collective-permute-start(bf16[8,4096]{1,0:T(8,128)(2,1)S(1)} %get-tuple-element.63), channel_id=1, source_target_pairs={{0,2},{1,3},{2,0},{3,1},{4,6},{5,7},{6,4},{7,5},{8,10},{9,11},{10,... | collective-permute-start | bytes 196616 | tf_op jit(solution)/shard_map/ppermute | solution.py:202
  73.4 2.7 %collective-permute-start.12 = (bf16[8,4096]{1,0:T(8,128)(2,1)S(1)}, bf16[8,4096]{1,0:T(8,128)(2,1)S(1)}, u32[]{:S(2)}, u32[]{:S(2)}) collective-permute-start(bf16[8,4096]{1,0:T(8,128)(2,1)S(1)} %get-tuple-element.62), channel_id=1, source_target_pairs={{0,3},{1,0},{2,1},{3,2},{4,7},{5,4},{6,5},{7,6},{8,11},{9,8},{10,9... | collective-permute-start | bytes 196616 | tf_op jit(solution)/shard_map/ppermute | solution.py:202
  76.1 2.2 %collective-permute-start.20 = (bf16[8,4096]{1,0:T(8,128)(2,1)S(1)}, bf16[8,4096]{1,0:T(8,128)(2,1)S(1)}, u32[]{:S(2)}, u32[]{:S(2)}) collective-permute-start(bf16[8,4096]{1,0:T(8,128)(2,1)S(1)} %slice.71), channel_id=1, source_target_pairs={{0,128},{128,0},{1,129},{129,1},{2,130},{130,2},{3,131},{131,3},{4... | collective-permute-start | bytes 196616 | tf_op jit(solution)/shard_map/ppermute | solution.py:206
  78.3 1.7 %collective-permute-done.12 = bf16[8,4096]{1,0:T(8,128)(2,1)S(1)} collective-permute-done((bf16[8,4096]{1,0:T(8,128)(2,1)S(1)}, bf16[8,4096]{1,0:T(8,128)(2,1)S(1)}, u32[]{:S(2)}, u32[]{:S(2)}) %collective-permute-start.12) | collective-permute-done | bytes 65568 | tf_op jit(solution)/shard_map/ppermute | solution.py:202
  81.0 1.1 %collective-permute-done.20 = bf16[8,4096]{1,0:T(8,128)(2,1)S(1)} collective-permute-done((bf16[8,4096]{1,0:T(8,128)(2,1)S(1)}, bf16[8,4096]{1,0:T(8,128)(2,1)S(1)}, u32[]{:S(2)}, u32[]{:S(2)}) %collective-permute-start.20) | collective-permute-done | bytes 65568 | tf_op jit(solution)/shard_map/ppermute | solution.py:206
  (44 shorter events, 10.2 us)
Async XLA Ops:
  1.9 12.8 %collective-permute-start.1 = (bf16[8,4096]{1,0:T(8,128)(2,1)S(1)}, bf16[8,4096]{1,0:T(8,128)(2,1)S(1)}, u32[]{:S(2)}, u32[]{:S(2)}) collective-permute-start(bf16[8,4096]{1,0:T(8,128)(2,1)S(1)} %reshape.25.refs_2_), channel_id=1, source_target_pairs={{0,1},{1,0},{2,3},{3,2},{4,5},{5,4},{6,7},{7,6},{8,9},{9,8},{10,11... | collective-permute-start | bytes 196616 | tf_op jit(solution)/shard_map/ppermute | solution.py:206
  6.2 8.6 %collective-permute-start = (bf16[8,4096]{1,0:T(8,128)(2,1)S(1)}, bf16[8,4096]{1,0:T(8,128)(2,1)S(1)}, u32[]{:S(2)}, u32[]{:S(2)}) collective-permute-start(bf16[8,4096]{1,0:T(8,128)(2,1)S(1)} %bitcast.16), channel_id=1, source_target_pairs={{0,128},{128,0},{1,129},{129,1},{2,130},{130,2},{3,131},{131,3},{4... | collective-permute-start | bytes 196616 | tf_op jit(solution)/shard_map/ppermute | solution.py:206
  9.3 2.2 %copy-start = (bf16[128,128,128]{2,1,0:T(8,128)(2,1)S(1)}, bf16[128,128,128]{2,1,0:T(8,128)(2,1)}, u32[]{:S(2)}) copy-start(bf16[128,128,128]{2,1,0:T(8,128)(2,1)} %grad_ref.1) | copy-start | bytes 12582916
  14.8 14.9 %collective-permute-start.2 = (bf16[16,4096]{1,0:T(8,128)(2,1)S(1)}, bf16[16,4096]{1,0:T(8,128)(2,1)S(1)}, u32[]{:S(2)}, u32[]{:S(2)}) collective-permute-start(bf16[16,4096]{1,0:T(8,128)(2,1)S(1)} %get-tuple-element.29.refs_0_), channel_id=1, source_target_pairs={{0,32},{32,64},{64,96},{96,0},{1,33},{33,65},{65,97},{97,1},{2,34}... | collective-permute-start | bytes 393224 | tf_op jit(solution)/shard_map/ppermute | solution.py:202
  16.4 13.3 %collective-permute-start.3 = (bf16[16,4096]{1,0:T(8,128)(2,1)S(1)}, bf16[16,4096]{1,0:T(8,128)(2,1)S(1)}, u32[]{:S(2)}, u32[]{:S(2)}) collective-permute-start(bf16[16,4096]{1,0:T(8,128)(2,1)S(1)} %get-tuple-element.29.refs_0_), channel_id=1, source_target_pairs={{0,64},{32,96},{64,0},{96,32},{1,65},{33,97},{65,1},{97,33},{2,66}... | collective-permute-start | bytes 393224 | tf_op jit(solution)/shard_map/ppermute | solution.py:202
  19.1 10.6 %collective-permute-start.4 = (bf16[16,4096]{1,0:T(8,128)(2,1)S(1)}, bf16[16,4096]{1,0:T(8,128)(2,1)S(1)}, u32[]{:S(2)}, u32[]{:S(2)}) collective-permute-start(bf16[16,4096]{1,0:T(8,128)(2,1)S(1)} %get-tuple-element.29.refs_0_), channel_id=1, source_target_pairs={{0,96},{32,0},{64,32},{96,64},{1,97},{33,1},{65,33},{97,65},{2,98}... | collective-permute-start | bytes 393224 | tf_op jit(solution)/shard_map/ppermute | solution.py:202
  20.5 10.1 %collective-permute-start.5 = (bf16[16,4096]{1,0:T(8,128)(2,1)S(1)}, bf16[16,4096]{1,0:T(8,128)(2,1)S(1)}, u32[]{:S(2)}, u32[]{:S(2)}) collective-permute-start(bf16[16,4096]{1,0:T(8,128)(2,1)S(1)} %get-tuple-element.30.refs_4_), channel_id=1, source_target_pairs={{0,2},{1,3},{2,0},{3,1},{4,6},{5,7},{6,4},{7,5},{8,10},{9,11},{10,... | collective-permute-start | bytes 393224 | tf_op jit(solution)/shard_map/ppermute | solution.py:206
  30.7 5.3 %collective-permute-start.6 = (bf16[64,4096]{1,0:T(8,128)(2,1)S(1)}, bf16[64,4096]{1,0:T(8,128)(2,1)S(1)}, u32[]{:S(2)}, u32[]{:S(2)}) collective-permute-start(bf16[64,4096]{1,0:T(8,128)(2,1)S(1)} %get-tuple-element.35.refs_0_), channel_id=1, source_target_pairs={{0,16},{16,0},{1,17},{17,1},{2,18},{18,2},{3,19},{19,3},{4,20},{20... | collective-permute-start | bytes 1572872 | tf_op jit(solution)/shard_map/ppermute | solution.py:206
  30.8 18.5 %collective-permute-start.13 = (bf16[32,4096]{1,0:T(8,128)(2,1)S(1)}, bf16[32,4096]{1,0:T(8,128)(2,1)S(1)}, u32[]{:S(2)}, u32[]{:S(2)}) collective-permute-start(bf16[32,4096]{1,0:T(8,128)(2,1)S(1)} %get-tuple-element.46.refs_0_), channel_id=1, source_target_pairs={{0,4},{4,8},{8,12},{12,0},{1,5},{5,9},{9,13},{13,1},{2,6},{6,10},{... | collective-permute-start | bytes 786440 | tf_op jit(solution)/shard_map/ppermute | solution.py:202
  31.1 19.5 %collective-permute-start.14 = (bf16[32,4096]{1,0:T(8,128)(2,1)S(1)}, bf16[32,4096]{1,0:T(8,128)(2,1)S(1)}, u32[]{:S(2)}, u32[]{:S(2)}) collective-permute-start(bf16[32,4096]{1,0:T(8,128)(2,1)S(1)} %get-tuple-element.46.refs_0_), channel_id=1, source_target_pairs={{0,8},{4,12},{8,0},{12,4},{1,9},{5,13},{9,1},{13,5},{2,10},{6,14},... | collective-permute-start | bytes 786440 | tf_op jit(solution)/shard_map/ppermute | solution.py:202
  33.7 16.9 %collective-permute-start.15 = (bf16[32,4096]{1,0:T(8,128)(2,1)S(1)}, bf16[32,4096]{1,0:T(8,128)(2,1)S(1)}, u32[]{:S(2)}, u32[]{:S(2)}) collective-permute-start(bf16[32,4096]{1,0:T(8,128)(2,1)S(1)} %get-tuple-element.46.refs_0_), channel_id=1, source_target_pairs={{0,12},{4,0},{8,4},{12,8},{1,13},{5,1},{9,5},{13,9},{2,14},{6,2},{... | collective-permute-start | bytes 786440 | tf_op jit(solution)/shard_map/ppermute | solution.py:202
  45.7 14.3 %collective-permute-start.7 = (bf16[32,4096]{1,0:T(8,128)(2,1)S(1)}, bf16[32,4096]{1,0:T(8,128)(2,1)S(1)}, u32[]{:S(2)}, u32[]{:S(2)}) collective-permute-start(bf16[32,4096]{1,0:T(8,128)(2,1)S(1)} %get-tuple-element.42), channel_id=1, source_target_pairs={{0,4},{4,8},{8,12},{12,0},{1,5},{5,9},{9,13},{13,1},{2,6},{6,10},{... | collective-permute-start | bytes 786440 | tf_op jit(solution)/shard_map/ppermute | solution.py:202
  49.0 10.9 %collective-permute-start.8 = (bf16[32,4096]{1,0:T(8,128)(2,1)S(1)}, bf16[32,4096]{1,0:T(8,128)(2,1)S(1)}, u32[]{:S(2)}, u32[]{:S(2)}) collective-permute-start(bf16[32,4096]{1,0:T(8,128)(2,1)S(1)} %get-tuple-element.43), channel_id=1, source_target_pairs={{0,8},{4,12},{8,0},{12,4},{1,9},{5,13},{9,1},{13,5},{2,10},{6,14},... | collective-permute-start | bytes 786440 | tf_op jit(solution)/shard_map/ppermute | solution.py:202
  49.2 14.4 %collective-permute-start.9 = (bf16[32,4096]{1,0:T(8,128)(2,1)S(1)}, bf16[32,4096]{1,0:T(8,128)(2,1)S(1)}, u32[]{:S(2)}, u32[]{:S(2)}) collective-permute-start(bf16[32,4096]{1,0:T(8,128)(2,1)S(1)} %get-tuple-element.44), channel_id=1, source_target_pairs={{0,12},{4,0},{8,4},{12,8},{1,13},{5,1},{9,5},{13,9},{2,14},{6,2},{... | collective-permute-start | bytes 786440 | tf_op jit(solution)/shard_map/ppermute | solution.py:202
  55.9 7.9 %collective-permute-start.16 = (f32[64,4096]{1,0:T(8,128)S(1)}, f32[64,4096]{1,0:T(8,128)S(1)}, u32[]{:S(2)}, u32[]{:S(2)}) collective-permute-start(f32[64,4096]{1,0:T(8,128)S(1)} %get-tuple-element.49), channel_id=1, source_target_pairs={{0,16},{16,0},{1,17},{17,1},{2,18},{18,2},{3,19},{19,3},{4,20},{20... | collective-permute-start | bytes 3145736 | tf_op jit(solution)/shard_map/ppermute | solution.py:206
  64.0 9.4 %collective-permute-start.17 = (bf16[16,4096]{1,0:T(8,128)(2,1)S(1)}, bf16[16,4096]{1,0:T(8,128)(2,1)S(1)}, u32[]{:S(2)}, u32[]{:S(2)}) collective-permute-start(bf16[16,4096]{1,0:T(8,128)(2,1)S(1)} %get-tuple-element.58), channel_id=1, source_target_pairs={{0,32},{32,64},{64,96},{96,0},{1,33},{33,65},{65,97},{97,1},{2,34}... | collective-permute-start | bytes 393224 | tf_op jit(solution)/shard_map/ppermute | solution.py:202
  64.6 11.5 %collective-permute-start.18 = (bf16[16,4096]{1,0:T(8,128)(2,1)S(1)}, bf16[16,4096]{1,0:T(8,128)(2,1)S(1)}, u32[]{:S(2)}, u32[]{:S(2)}) collective-permute-start(bf16[16,4096]{1,0:T(8,128)(2,1)S(1)} %get-tuple-element.60), channel_id=1, source_target_pairs={{0,64},{32,96},{64,0},{96,32},{1,65},{33,97},{65,1},{97,33},{2,66}... | collective-permute-start | bytes 393224 | tf_op jit(solution)/shard_map/ppermute | solution.py:202
  65.5 10.6 %collective-permute-start.19 = (bf16[16,4096]{1,0:T(8,128)(2,1)S(1)}, bf16[16,4096]{1,0:T(8,128)(2,1)S(1)}, u32[]{:S(2)}, u32[]{:S(2)}) collective-permute-start(bf16[16,4096]{1,0:T(8,128)(2,1)S(1)} %get-tuple-element.59), channel_id=1, source_target_pairs={{0,96},{32,0},{64,32},{96,64},{1,97},{33,1},{65,33},{97,65},{2,98}... | collective-permute-start | bytes 393224 | tf_op jit(solution)/shard_map/ppermute | solution.py:202
  67.4 10.9 %collective-permute-start.10 = (bf16[8,4096]{1,0:T(8,128)(2,1)S(1)}, bf16[8,4096]{1,0:T(8,128)(2,1)S(1)}, u32[]{:S(2)}, u32[]{:S(2)}) collective-permute-start(bf16[8,4096]{1,0:T(8,128)(2,1)S(1)} %get-tuple-element.61), channel_id=1, source_target_pairs={{0,1},{1,2},{2,3},{3,0},{4,5},{5,6},{6,7},{7,4},{8,9},{9,10},{10,1... | collective-permute-start | bytes 196616 | tf_op jit(solution)/shard_map/ppermute | solution.py:202
  68.2 10.2 %collective-permute-start.11 = (bf16[8,4096]{1,0:T(8,128)(2,1)S(1)}, bf16[8,4096]{1,0:T(8,128)(2,1)S(1)}, u32[]{:S(2)}, u32[]{:S(2)}) collective-permute-start(bf16[8,4096]{1,0:T(8,128)(2,1)S(1)} %get-tuple-element.63), channel_id=1, source_target_pairs={{0,2},{1,3},{2,0},{3,1},{4,6},{5,7},{6,4},{7,5},{8,10},{9,11},{10,... | collective-permute-start | bytes 196616 | tf_op jit(solution)/shard_map/ppermute | solution.py:202
  73.4 6.6 %collective-permute-start.12 = (bf16[8,4096]{1,0:T(8,128)(2,1)S(1)}, bf16[8,4096]{1,0:T(8,128)(2,1)S(1)}, u32[]{:S(2)}, u32[]{:S(2)}) collective-permute-start(bf16[8,4096]{1,0:T(8,128)(2,1)S(1)} %get-tuple-element.62), channel_id=1, source_target_pairs={{0,3},{1,0},{2,1},{3,2},{4,7},{5,4},{6,5},{7,6},{8,11},{9,8},{10,9... | collective-permute-start | bytes 196616 | tf_op jit(solution)/shard_map/ppermute | solution.py:202
  76.1 6.0 %collective-permute-start.20 = (bf16[8,4096]{1,0:T(8,128)(2,1)S(1)}, bf16[8,4096]{1,0:T(8,128)(2,1)S(1)}, u32[]{:S(2)}, u32[]{:S(2)}) collective-permute-start(bf16[8,4096]{1,0:T(8,128)(2,1)S(1)} %slice.71), channel_id=1, source_target_pairs={{0,128},{128,0},{1,129},{129,1},{2,130},{130,2},{3,131},{131,3},{4... | collective-permute-start | bytes 196616 | tf_op jit(solution)/shard_map/ppermute | solution.py:206

commit v4 on v3

--- a/solution.py
+++ b/solution.py
@@ -197,6 +197,33 @@
     )(table, *sources, *expanded, after)
 
 
+def split_sum(own, others, part, after=()):
+    rows, width = own.shape
+    count = rows // part
+
+    def body(*refs):
+        given = refs[: 1 + len(others)]
+        token_ref, near_ref, *piece_refs = refs[1 + len(others) + len(after) :]
+        total = given[0][...]
+        for ref in given[1:]:
+            total = total + ref[...].astype(jnp.float32)
+        near_ref[...] = total[:part]
+        for k, piece_ref in enumerate(piece_refs):
+            piece_ref[...] = total[(k + 1) * part : (k + 2) * part].astype(jnp.bfloat16)
+        token_ref[...] = total[:8, :128]
+
+    return pl.pallas_call(
+        body,
+        in_specs=[WHOLE] * (1 + len(others) + len(after)),
+        out_specs=[WHOLE] * (1 + count),
+        out_shape=[jax.ShapeDtypeStruct((8, 128), jnp.float32), jax.ShapeDtypeStruct((part, width), jnp.float32)]
+        + [jax.ShapeDtypeStruct((part, width), jnp.bfloat16)] * (count - 1),
+        compiler_params=params(),
+        cost_estimate=pl.CostEstimate(flops=0, transcendentals=0, bytes_accessed=1 << 20),
+        name="split_sum",
+    )(own, *others, *after)
+
+
 def moved(value, axis, distance):
     size = lax.axis_size(axis)
     return lax.ppermute(value, axis, [(k, (k + distance) % size) for k in range(size)])
@@ -230,6 +257,7 @@
 
     from_z = swapped(right_flat, "z_lo", 1)
     from_hi = swapped(left_flat, "z_hi", 1)
+    pair_grad = pltpu.with_memory_space_constraint(pair_grad, pltpu.HBM)
     piece, token, pair_grad = expand(pair_grad, weights, channels, 0)
     expanded = [piece]
     near_right, near_left, token = join([[right_flat, from_z], [left_flat, from_hi]], [token])
@@ -246,21 +274,16 @@
     token, own, *others = left_partial(left_table, right_sources, expanded, held, inverse)
     right_own, right_other = right_partial(right_table, left_sources, expanded, shared, inverse, token)
 
-    left_sum = own
-    for d, other in enumerate(others):
-        left_sum = left_sum + moved(other, "y", d + 1).astype(jnp.float32)
-    left_grad = left_sum[:shared]
-    for d in (1, 2, 3):
-        piece = left_sum[d * shared : (d + 1) * shared].astype(jnp.bfloat16)
-        left_grad = left_grad + moved(piece, "z_hi", d).astype(jnp.float32)
+    left_terms = [moved(other, "y", d + 1) for d, other in enumerate(others)]
+    token, right_near, *pieces = split_sum(right_own, [swapped(right_other, "core", 1)], 2 * held)
+    right_terms = [moved(piece, "x", d + 1) for d, piece in enumerate(pieces)]
+    token, left_grad, *pieces = split_sum(own, left_terms, shared, [token])
+    for d, piece in enumerate(pieces):
+        left_grad = left_grad + moved(piece, "z_hi", d + 1).astype(jnp.float32)
     left_grad = jnp.swapaxes(left_grad.reshape(shared, rows, channels), 1, 2)
 
-    right_sum = right_own + swapped(right_other, "core", 1)
-    part = 2 * held
-    right_near = right_sum[:part]
-    for d in (1, 2, 3):
-        piece = right_sum[d * part : (d + 1) * part].astype(jnp.bfloat16)
-        right_near = right_near + moved(piece, "x", d).astype(jnp.float32)
+    for term in right_terms:
+        right_near = right_near + term.astype(jnp.float32)
     right_grad = right_near[:held] + swapped(right_near[held:].astype(jnp.bfloat16), "z_lo", 1).astype(jnp.float32)
     return (left_grad, right_grad.reshape(held, entries, cols))
 

time: 83 us -> 84.7 us (1.020)
  waiting for transfers between devices: 12.2 us -> 17.5 us
  starting transfers between devices: 36.9 us -> 34.1 us
  local copies, waits for them, and re-layouts: 7.13 us -> 4.9 us
  Pallas kernels: 25.3 us -> 27.1 us
    ppermute x15, waiting for transfers between devices: 10.2 us -> 16.1 us  [moved(): lax.ppermute(value, axis, [(k, (k + distance) % size) for k in range(size)])]
    unnamed x5 -> x3, local copies, waits for them, and re-layouts: 4.57 us -> 2.38 us
    ppermute x15, starting transfers between devices: 24.7 us -> 22.7 us  [moved(): lax.ppermute(value, axis, [(k, (k + distance) % size) for k in range(size)])]
  transfers between devices with their start and end apart: 21 -> 21, of which waited for: 6 -> 6; matrix products, arithmetic and copies ran while one was open for 4% -> 4% of each run, Pallas kernels for 31% -> 25%
where the time goes in v4:
time: 84.7 us; the launch traced here: 84.5 us
  starting transfers between devices  34.1 us (40%)
  Pallas kernels  27.1 us (32%)
  waiting for transfers between devices  17.5 us (21%)
  local copies, waits for them, and re-layouts  4.9 us (6%)
    ppermute x15, starting transfers between devices, moved(): lax.ppermute(value, axis, [(k, (k + distance) % size) for k in range(size)])  22.7 us
    ppermute x15, waiting for transfers between devices, moved(): lax.ppermute(value, axis, [(k, (k + distance) % size) for k in range(size)])  16.1 us
    ppermute x6, starting transfers between devices, swapped(): lax.ppermute(value, axis, [(k, k ^ bit) for k in range(lax.axis_size(axis...  11.5 us
    pallas_call x4, Pallas kernels, expand(): pl.pallas_call(body, in_specs=[WHOLE, pl.BlockSpec(memory_space=pltpu.HBM...  11 us
    pallas_call x1, Pallas kernels, left_partial(): pl.pallas_call(body, in_specs=[TABLE] + [WHOLE] * (len(sources) + len(exp...  9.67 us
    pallas_call x1, Pallas kernels, right_partial(): pl.pallas_call(body, in_specs=[TABLE] + [WHOLE] * (len(sources) + len(exp...  5.53 us
    unnamed x3, local copies, waits for them, and re-layouts  2.38 us
  transfers between devices with their start and end apart: 21, of which 6 were waited for; matrix products, arithmetic and copies ran while one was open for 4% of the time, Pallas kernels for 25%

profile of v4, /device:TPU:24, one launch (start us, length us, event | category | flops | bytes accessed | tf_op | source)
XLA Modules:
  0.0 84.5 jit_solution(9708391607879024164)
XLA Ops:
  0.6 1.0 %copy.11 = bf16[8,128,32]{2,1,0:T(8,128)(2,1)S(1)} copy(bf16[8,128,32]{1,2,0:T(8,128)(2,1)} %bitcast.20) | data formatting | bytes 131072 | tf_op jit(solution)/shard_map/transpose | solution.py:249
  1.9 3.4 %collective-permute-start.1 = (bf16[8,4096]{1,0:T(8,128)(2,1)S(1)}, bf16[8,4096]{1,0:T(8,128)(2,1)S(1)}, u32[]{:S(2)}, u32[]{:S(2)}) collective-permute-start(bf16[8,4096]{1,0:T(8,128)(2,1)S(1)} %reshape.25.refs_2_), channel_id=1, source_target_pairs={{0,1},{1,0},{2,3},{3,2},{4,5},{5,4},{6,7},{7,6},{8,9},{9,8},{10,11... | collective-permute-start | bytes 196616 | tf_op jit(solution)/shard_map/ppermute | solution.py:233
  6.2 2.0 %collective-permute-start = (bf16[8,4096]{1,0:T(8,128)(2,1)S(1)}, bf16[8,4096]{1,0:T(8,128)(2,1)S(1)}, u32[]{:S(2)}, u32[]{:S(2)}) collective-permute-start(bf16[8,4096]{1,0:T(8,128)(2,1)S(1)} %bitcast.16), channel_id=1, source_target_pairs={{0,128},{128,0},{1,129},{129,1},{2,130},{130,2},{3,131},{131,3},{4... | collective-permute-start | bytes 196616 | tf_op jit(solution)/shard_map/ppermute | solution.py:233
  8.2 1.1 %copy.10 = bf16[32,32,128]{2,0,1:T(8,128)(2,1)S(1)} copy(bf16[32,32,128]{2,1,0:T(8,128)(2,1)} %bitcast.19) | data formatting | bytes 524288 | tf_op jit(solution)/shard_map/reshape | solution.py:251
  9.3 3.9 %expand.4 = (bf16[1024,4096]{1,0:T(8,128)(2,1)S(1)}, bf16[16,128]{1,0:T(8,128)(2,1)S(1)}, bf16[128,128,128]{2,1,0:T(8,128)(2,1)S(1)}) custom-call(bf16[1024,128]{1,0:T(8,128)(2,1)S(1)} %bitcast.12, bf16[128,128,128]{2,1,0:T(8,128)(2,1)} %grad_ref.1), custom_call_target="tpu_custom_call" | custom-call | flops 2147483648 | bytes 1048576 | tf_op jit(solution)/shard_map/expand/pallas_call | solution.py:59
  13.3 1.6 %collective-permute-start.2 = (bf16[16,4096]{1,0:T(8,128)(2,1)S(1)}, bf16[16,4096]{1,0:T(8,128)(2,1)S(1)}, u32[]{:S(2)}, u32[]{:S(2)}) collective-permute-start(bf16[16,4096]{1,0:T(8,128)(2,1)S(1)} %get-tuple-element.38.refs_0_), channel_id=1, source_target_pairs={{0,32},{32,64},{64,96},{96,0},{1,33},{33,65},{65,97},{97,1},{2,34}... | collective-permute-start | bytes 393224 | tf_op jit(solution)/shard_map/ppermute | solution.py:229
  14.8 2.7 %collective-permute-start.3 = (bf16[16,4096]{1,0:T(8,128)(2,1)S(1)}, bf16[16,4096]{1,0:T(8,128)(2,1)S(1)}, u32[]{:S(2)}, u32[]{:S(2)}) collective-permute-start(bf16[16,4096]{1,0:T(8,128)(2,1)S(1)} %get-tuple-element.38.refs_0_), channel_id=1, source_target_pairs={{0,64},{32,96},{64,0},{96,32},{1,65},{33,97},{65,1},{97,33},{2,66}... | collective-permute-start | bytes 393224 | tf_op jit(solution)/shard_map/ppermute | solution.py:229
  17.5 1.4 %collective-permute-start.4 = (bf16[16,4096]{1,0:T(8,128)(2,1)S(1)}, bf16[16,4096]{1,0:T(8,128)(2,1)S(1)}, u32[]{:S(2)}, u32[]{:S(2)}) collective-permute-start(bf16[16,4096]{1,0:T(8,128)(2,1)S(1)} %get-tuple-element.38.refs_0_), channel_id=1, source_target_pairs={{0,96},{32,0},{64,32},{96,64},{1,97},{33,1},{65,33},{97,65},{2,98}... | collective-permute-start | bytes 393224 | tf_op jit(solution)/shard_map/ppermute | solution.py:229
  19.0 4.5 %collective-permute-start.5 = (bf16[16,4096]{1,0:T(8,128)(2,1)S(1)}, bf16[16,4096]{1,0:T(8,128)(2,1)S(1)}, u32[]{:S(2)}, u32[]{:S(2)}) collective-permute-start(bf16[16,4096]{1,0:T(8,128)(2,1)S(1)} %get-tuple-element.39.refs_4_), channel_id=1, source_target_pairs={{0,2},{1,3},{2,0},{3,1},{4,6},{5,7},{6,4},{7,5},{8,10},{9,11},{10,... | collective-permute-start | bytes 393224 | tf_op jit(solution)/shard_map/ppermute | solution.py:233
  23.5 2.3 %expand.5 = (bf16[1024,4096]{1,0:T(8,128)(2,1)S(1)}, bf16[16,128]{1,0:T(8,128)(2,1)S(1)}) custom-call(bf16[1024,128]{1,0:T(8,128)(2,1)S(1)} %bitcast.13, bf16[128,128,128]{2,1,0:T(8,128)(2,1)S(1)} %get-tuple-element.40.grad_ref, bf16[16,128]{1,0:T(8,128)(2,1)S(1)} %get-tuple-element.41.rest_0_), custom_call_target="tpu_custom_call" | custom-call | flops 2147483648 | bytes 1048576 | tf_op jit(solution)/shard_map/expand/pallas_call | solution.py:59
  25.8 2.3 %expand.6 = (bf16[1024,4096]{1,0:T(8,128)(2,1)S(1)}, bf16[16,128]{1,0:T(8,128)(2,1)S(1)}) custom-call(bf16[1024,128]{1,0:T(8,128)(2,1)S(1)} %bitcast.14, bf16[128,128,128]{2,1,0:T(8,128)(2,1)S(1)} %get-tuple-element.40.grad_ref, bf16[16,128]{1,0:T(8,128)(2,1)S(1)} %get-tuple-element.42.rest_0_), custom_call_target="tpu_custom_call" | custom-call | flops 2147483648 | bytes 1048576 | tf_op jit(solution)/shard_map/expand/pallas_call | solution.py:59
  28.2 0.9 %collective-permute-done.5.refs_5_ = bf16[16,4096]{1,0:T(8,128)(2,1)S(1)} collective-permute-done((bf16[16,4096]{1,0:T(8,128)(2,1)S(1)}, bf16[16,4096]{1,0:T(8,128)(2,1)S(1)}, u32[]{:S(2)}, u32[]{:S(2)}) %collective-permute-start.5) | collective-permute-done | bytes 131104 | tf_op jit(solution)/shard_map/ppermute | solution.py:233
  29.7 2.6 %collective-permute-start.11 = (bf16[32,4096]{1,0:T(8,128)(2,1)S(1)}, bf16[32,4096]{1,0:T(8,128)(2,1)S(1)}, u32[]{:S(2)}, u32[]{:S(2)}) collective-permute-start(bf16[32,4096]{1,0:T(8,128)(2,1)S(1)} %get-tuple-element.55.refs_0_), channel_id=1, source_target_pairs={{0,8},{4,12},{8,0},{12,4},{1,9},{5,13},{9,1},{13,5},{2,10},{6,14},... | collective-permute-start | bytes 786440 | tf_op jit(solution)/shard_map/ppermute | solution.py:229
  32.3 2.3 %expand.7 = (bf16[1024,4096]{1,0:T(8,128)(2,1)S(1)}, bf16[16,128]{1,0:T(8,128)(2,1)}) custom-call(bf16[1024,128]{1,0:T(8,128)(2,1)S(1)} %bitcast.15, bf16[128,128,128]{2,1,0:T(8,128)(2,1)S(1)} %get-tuple-element.40.grad_ref, bf16[16,128]{1,0:T(8,128)(2,1)S(1)} %get-tuple-element.48.rest_0_), custom_call_target="tpu_custom_call" | custom-call | flops 2147483648 | bytes 1048576 | tf_op jit(solution)/shard_map/expand/pallas_call | solution.py:59
  34.7 9.7 %left_partial.1 = (bf16[16,128]{1,0:T(8,128)(2,1)S(1)}, f32[32,4096]{1,0:T(8,128)S(1)}, bf16[32,4096]{1,0:T(8,128)(2,1)S(1)}, bf16[32,4096]{1,0:T(8,128)(2,1)S(1)}, bf16[32,4096]{1,0:T(8,128)(2,1)S(1)}) custom-call(s32[16]{0:T(128)S(1)} %get-tuple-element.35.table_ref, bf16[64,4096]{1,0:T(8,128)(2,1)S(1)} %get-tuple-element.44.refs_0_, ...), custom_call_target="tpu_custom_call" | custom-call | flops 8589934592 | bytes 1048576 | tf_op jit(solution)/shard_map/left_partial/pallas_call | solution.py:140
  45.3 5.5 %right_partial.1 = (f32[64,4096]{1,0:T(8,128)S(1)}, f32[64,4096]{1,0:T(8,128)S(1)}) custom-call(s32[16]{0:T(128)S(1)} %get-tuple-element.54.table_ref, bf16[32,4096]{1,0:T(8,128)(2,1)S(1)} %get-tuple-element.55.refs_0_, bf16[32,4096]{1,0:T(8,128)(2,1)S(1)} %collective-permute-done.10.refs_1_, bf16[32,4096]{1,0:T(8,128)(2,1)S(1)} %collective-permute-done.11.refs_2_, ...), custom_call_target="tpu_custom_call" | custom-call | flops 4294967296 | bytes 1048576 | tf_op jit(solution)/shard_map/right_partial/pallas_call | solution.py:188
  50.9 2.4 %collective-permute-start.7 = (bf16[32,4096]{1,0:T(8,128)(2,1)S(1)}, bf16[32,4096]{1,0:T(8,128)(2,1)S(1)}, u32[]{:S(2)}, u32[]{:S(2)}) collective-permute-start(bf16[32,4096]{1,0:T(8,128)(2,1)S(1)} %get-tuple-element.51), channel_id=1, source_target_pairs={{0,4},{4,8},{8,12},{12,0},{1,5},{5,9},{9,13},{13,1},{2,6},{6,10},{... | collective-permute-start | bytes 786440 | tf_op jit(solution)/shard_map/ppermute | solution.py:229
  55.7 0.9 %collective-permute-start.18 = (bf16[16,4096]{1,0:T(8,128)(2,1)S(1)}, bf16[16,4096]{1,0:T(8,128)(2,1)S(1)}, u32[]{:S(2)}, u32[]{:S(2)}) collective-permute-start(bf16[16,4096]{1,0:T(8,128)(2,1)S(1)} %get-tuple-element.66), channel_id=1, source_target_pairs={{0,64},{32,96},{64,0},{96,32},{1,65},{33,97},{65,1},{97,33},{2,66}... | collective-permute-start | bytes 393224 | tf_op jit(solution)/shard_map/ppermute | solution.py:229
  56.6 8.6 %collective-permute-done.7.refs_1_ = bf16[32,4096]{1,0:T(8,128)(2,1)S(1)} collective-permute-done((bf16[32,4096]{1,0:T(8,128)(2,1)S(1)}, bf16[32,4096]{1,0:T(8,128)(2,1)S(1)}, u32[]{:S(2)}, u32[]{:S(2)}) %collective-permute-start.7) | collective-permute-done | bytes 262176 | tf_op jit(solution)/shard_map/ppermute | solution.py:229
  65.2 3.7 %collective-permute-done.9.refs_3_ = bf16[32,4096]{1,0:T(8,128)(2,1)S(1)} collective-permute-done((bf16[32,4096]{1,0:T(8,128)(2,1)S(1)}, bf16[32,4096]{1,0:T(8,128)(2,1)S(1)}, u32[]{:S(2)}, u32[]{:S(2)}) %collective-permute-start.9) | collective-permute-done | bytes 262176 | tf_op jit(solution)/shard_map/ppermute | solution.py:229
  70.1 4.4 %collective-permute-start.15 = (bf16[8,4096]{1,0:T(8,128)(2,1)S(1)}, bf16[8,4096]{1,0:T(8,128)(2,1)S(1)}, u32[]{:S(2)}, u32[]{:S(2)}) collective-permute-start(bf16[8,4096]{1,0:T(8,128)(2,1)S(1)} %get-tuple-element.62), channel_id=1, source_target_pairs={{0,2},{1,3},{2,0},{3,1},{4,6},{5,7},{6,4},{7,5},{8,10},{9,11},{10,... | collective-permute-start | bytes 196616 | tf_op jit(solution)/shard_map/ppermute | solution.py:229
  74.5 3.5 %collective-permute-start.16 = (bf16[8,4096]{1,0:T(8,128)(2,1)S(1)}, bf16[8,4096]{1,0:T(8,128)(2,1)S(1)}, u32[]{:S(2)}, u32[]{:S(2)}) collective-permute-start(bf16[8,4096]{1,0:T(8,128)(2,1)S(1)} %get-tuple-element.63), channel_id=1, source_target_pairs={{0,3},{1,0},{2,1},{3,2},{4,7},{5,4},{6,5},{7,6},{8,11},{9,8},{10,9... | collective-permute-start | bytes 196616 | tf_op jit(solution)/shard_map/ppermute | solution.py:229
  78.1 1.3 %collective-permute-start.20 = (bf16[8,4096]{1,0:T(8,128)(2,1)S(1)}, bf16[8,4096]{1,0:T(8,128)(2,1)S(1)}, u32[]{:S(2)}, u32[]{:S(2)}) collective-permute-start(bf16[8,4096]{1,0:T(8,128)(2,1)S(1)} %slice.15), channel_id=1, source_target_pairs={{0,128},{128,0},{1,129},{129,1},{2,130},{130,2},{3,131},{131,3},{4... | collective-permute-start | bytes 196616 | tf_op jit(solution)/shard_map/ppermute | solution.py:233
  79.4 3.0 %collective-permute-done.16 = bf16[8,4096]{1,0:T(8,128)(2,1)S(1)} collective-permute-done((bf16[8,4096]{1,0:T(8,128)(2,1)S(1)}, bf16[8,4096]{1,0:T(8,128)(2,1)S(1)}, u32[]{:S(2)}, u32[]{:S(2)}) %collective-permute-start.16) | collective-permute-done | bytes 65568 | tf_op jit(solution)/shard_map/ppermute | solution.py:229
  (40 shorter events, 8.7 us)
Async XLA Ops:
  1.9 11.3 %collective-permute-start.1 = (bf16[8,4096]{1,0:T(8,128)(2,1)S(1)}, bf16[8,4096]{1,0:T(8,128)(2,1)S(1)}, u32[]{:S(2)}, u32[]{:S(2)}) collective-permute-start(bf16[8,4096]{1,0:T(8,128)(2,1)S(1)} %reshape.25.refs_2_), channel_id=1, source_target_pairs={{0,1},{1,0},{2,3},{3,2},{4,5},{5,4},{6,7},{7,6},{8,9},{9,8},{10,11... | collective-permute-start | bytes 196616 | tf_op jit(solution)/shard_map/ppermute | solution.py:233
  6.2 7.1 %collective-permute-start = (bf16[8,4096]{1,0:T(8,128)(2,1)S(1)}, bf16[8,4096]{1,0:T(8,128)(2,1)S(1)}, u32[]{:S(2)}, u32[]{:S(2)}) collective-permute-start(bf16[8,4096]{1,0:T(8,128)(2,1)S(1)} %bitcast.16), channel_id=1, source_target_pairs={{0,128},{128,0},{1,129},{129,1},{2,130},{130,2},{3,131},{131,3},{4... | collective-permute-start | bytes 196616 | tf_op jit(solution)/shard_map/ppermute | solution.py:233
  13.3 14.9 %collective-permute-start.2 = (bf16[16,4096]{1,0:T(8,128)(2,1)S(1)}, bf16[16,4096]{1,0:T(8,128)(2,1)S(1)}, u32[]{:S(2)}, u32[]{:S(2)}) collective-permute-start(bf16[16,4096]{1,0:T(8,128)(2,1)S(1)} %get-tuple-element.38.refs_0_), channel_id=1, source_target_pairs={{0,32},{32,64},{64,96},{96,0},{1,33},{33,65},{65,97},{97,1},{2,34}... | collective-permute-start | bytes 393224 | tf_op jit(solution)/shard_map/ppermute | solution.py:229
  14.8 13.3 %collective-permute-start.3 = (bf16[16,4096]{1,0:T(8,128)(2,1)S(1)}, bf16[16,4096]{1,0:T(8,128)(2,1)S(1)}, u32[]{:S(2)}, u32[]{:S(2)}) collective-permute-start(bf16[16,4096]{1,0:T(8,128)(2,1)S(1)} %get-tuple-element.38.refs_0_), channel_id=1, source_target_pairs={{0,64},{32,96},{64,0},{96,32},{1,65},{33,97},{65,1},{97,33},{2,66}... | collective-permute-start | bytes 393224 | tf_op jit(solution)/shard_map/ppermute | solution.py:229
  17.5 10.6 %collective-permute-start.4 = (bf16[16,4096]{1,0:T(8,128)(2,1)S(1)}, bf16[16,4096]{1,0:T(8,128)(2,1)S(1)}, u32[]{:S(2)}, u32[]{:S(2)}) collective-permute-start(bf16[16,4096]{1,0:T(8,128)(2,1)S(1)} %get-tuple-element.38.refs_0_), channel_id=1, source_target_pairs={{0,96},{32,0},{64,32},{96,64},{1,97},{33,1},{65,33},{97,65},{2,98}... | collective-permute-start | bytes 393224 | tf_op jit(solution)/shard_map/ppermute | solution.py:229
  19.0 10.1 %collective-permute-start.5 = (bf16[16,4096]{1,0:T(8,128)(2,1)S(1)}, bf16[16,4096]{1,0:T(8,128)(2,1)S(1)}, u32[]{:S(2)}, u32[]{:S(2)}) collective-permute-start(bf16[16,4096]{1,0:T(8,128)(2,1)S(1)} %get-tuple-element.39.refs_4_), channel_id=1, source_target_pairs={{0,2},{1,3},{2,0},{3,1},{4,6},{5,7},{6,4},{7,5},{8,10},{9,11},{10,... | collective-permute-start | bytes 393224 | tf_op jit(solution)/shard_map/ppermute | solution.py:233
  29.2 5.5 %collective-permute-start.6 = (bf16[64,4096]{1,0:T(8,128)(2,1)S(1)}, bf16[64,4096]{1,0:T(8,128)(2,1)S(1)}, u32[]{:S(2)}, u32[]{:S(2)}) collective-permute-start(bf16[64,4096]{1,0:T(8,128)(2,1)S(1)} %get-tuple-element.44.refs_0_), channel_id=1, source_target_pairs={{0,16},{16,0},{1,17},{17,1},{2,18},{18,2},{3,19},{19,3},{4,20},{20... | collective-permute-start | bytes 1572872 | tf_op jit(solution)/shard_map/ppermute | solution.py:233
  29.4 14.9 %collective-permute-start.10 = (bf16[32,4096]{1,0:T(8,128)(2,1)S(1)}, bf16[32,4096]{1,0:T(8,128)(2,1)S(1)}, u32[]{:S(2)}, u32[]{:S(2)}) collective-permute-start(bf16[32,4096]{1,0:T(8,128)(2,1)S(1)} %get-tuple-element.55.refs_0_), channel_id=1, source_target_pairs={{0,4},{4,8},{8,12},{12,0},{1,5},{5,9},{9,13},{13,1},{2,6},{6,10},{... | collective-permute-start | bytes 786440 | tf_op jit(solution)/shard_map/ppermute | solution.py:229
  29.7 14.6 %collective-permute-start.11 = (bf16[32,4096]{1,0:T(8,128)(2,1)S(1)}, bf16[32,4096]{1,0:T(8,128)(2,1)S(1)}, u32[]{:S(2)}, u32[]{:S(2)}) collective-permute-start(bf16[32,4096]{1,0:T(8,128)(2,1)S(1)} %get-tuple-element.55.refs_0_), channel_id=1, source_target_pairs={{0,8},{4,12},{8,0},{12,4},{1,9},{5,13},{9,1},{13,5},{2,10},{6,14},... | collective-permute-start | bytes 786440 | tf_op jit(solution)/shard_map/ppermute | solution.py:229
  32.3 12.9 %collective-permute-start.12 = (bf16[32,4096]{1,0:T(8,128)(2,1)S(1)}, bf16[32,4096]{1,0:T(8,128)(2,1)S(1)}, u32[]{:S(2)}, u32[]{:S(2)}) collective-permute-start(bf16[32,4096]{1,0:T(8,128)(2,1)S(1)} %get-tuple-element.55.refs_0_), channel_id=1, source_target_pairs={{0,12},{4,0},{8,4},{12,8},{1,13},{5,1},{9,5},{13,9},{2,14},{6,2},{... | collective-permute-start | bytes 786440 | tf_op jit(solution)/shard_map/ppermute | solution.py:229
  50.8 4.1 %collective-permute-start.13 = (f32[64,4096]{1,0:T(8,128)S(1)}, f32[64,4096]{1,0:T(8,128)S(1)}, u32[]{:S(2)}, u32[]{:S(2)}) collective-permute-start(f32[64,4096]{1,0:T(8,128)S(1)} %get-tuple-element.58), channel_id=1, source_target_pairs={{0,16},{16,0},{1,17},{17,1},{2,18},{18,2},{3,19},{19,3},{4,20},{20... | collective-permute-start | bytes 3145736 | tf_op jit(solution)/shard_map/ppermute | solution.py:233
  50.9 14.2 %collective-permute-start.7 = (bf16[32,4096]{1,0:T(8,128)(2,1)S(1)}, bf16[32,4096]{1,0:T(8,128)(2,1)S(1)}, u32[]{:S(2)}, u32[]{:S(2)}) collective-permute-start(bf16[32,4096]{1,0:T(8,128)(2,1)S(1)} %get-tuple-element.51), channel_id=1, source_target_pairs={{0,4},{4,8},{8,12},{12,0},{1,5},{5,9},{9,13},{13,1},{2,6},{6,10},{... | collective-permute-start | bytes 786440 | tf_op jit(solution)/shard_map/ppermute | solution.py:229
  53.4 11.8 %collective-permute-start.8 = (bf16[32,4096]{1,0:T(8,128)(2,1)S(1)}, bf16[32,4096]{1,0:T(8,128)(2,1)S(1)}, u32[]{:S(2)}, u32[]{:S(2)}) collective-permute-start(bf16[32,4096]{1,0:T(8,128)(2,1)S(1)} %get-tuple-element.52), channel_id=1, source_target_pairs={{0,8},{4,12},{8,0},{12,4},{1,9},{5,13},{9,1},{13,5},{2,10},{6,14},... | collective-permute-start | bytes 786440 | tf_op jit(solution)/shard_map/ppermute | solution.py:229
  54.2 14.7 %collective-permute-start.9 = (bf16[32,4096]{1,0:T(8,128)(2,1)S(1)}, bf16[32,4096]{1,0:T(8,128)(2,1)S(1)}, u32[]{:S(2)}, u32[]{:S(2)}) collective-permute-start(bf16[32,4096]{1,0:T(8,128)(2,1)S(1)} %get-tuple-element.53), channel_id=1, source_target_pairs={{0,12},{4,0},{8,4},{12,8},{1,13},{5,1},{9,5},{13,9},{2,14},{6,2},{... | collective-permute-start | bytes 786440 | tf_op jit(solution)/shard_map/ppermute | solution.py:229
  55.1 19.5 %collective-permute-start.17 = (bf16[16,4096]{1,0:T(8,128)(2,1)S(1)}, bf16[16,4096]{1,0:T(8,128)(2,1)S(1)}, u32[]{:S(2)}, u32[]{:S(2)}) collective-permute-start(bf16[16,4096]{1,0:T(8,128)(2,1)S(1)} %get-tuple-element.65), channel_id=1, source_target_pairs={{0,32},{32,64},{64,96},{96,0},{1,33},{33,65},{65,97},{97,1},{2,34}... | collective-permute-start | bytes 393224 | tf_op jit(solution)/shard_map/ppermute | solution.py:229
  55.7 22.3 %collective-permute-start.18 = (bf16[16,4096]{1,0:T(8,128)(2,1)S(1)}, bf16[16,4096]{1,0:T(8,128)(2,1)S(1)}, u32[]{:S(2)}, u32[]{:S(2)}) collective-permute-start(bf16[16,4096]{1,0:T(8,128)(2,1)S(1)} %get-tuple-element.66), channel_id=1, source_target_pairs={{0,64},{32,96},{64,0},{96,32},{1,65},{33,97},{65,1},{97,33},{2,66}... | collective-permute-start | bytes 393224 | tf_op jit(solution)/shard_map/ppermute | solution.py:229
  65.2 12.9 %collective-permute-start.19 = (bf16[16,4096]{1,0:T(8,128)(2,1)S(1)}, bf16[16,4096]{1,0:T(8,128)(2,1)S(1)}, u32[]{:S(2)}, u32[]{:S(2)}) collective-permute-start(bf16[16,4096]{1,0:T(8,128)(2,1)S(1)} %get-tuple-element.67), channel_id=1, source_target_pairs={{0,96},{32,0},{64,32},{96,64},{1,97},{33,1},{65,33},{97,65},{2,98}... | collective-permute-start | bytes 393224 | tf_op jit(solution)/shard_map/ppermute | solution.py:229
  69.5 9.9 %collective-permute-start.14 = (bf16[8,4096]{1,0:T(8,128)(2,1)S(1)}, bf16[8,4096]{1,0:T(8,128)(2,1)S(1)}, u32[]{:S(2)}, u32[]{:S(2)}) collective-permute-start(bf16[8,4096]{1,0:T(8,128)(2,1)S(1)} %get-tuple-element.61), channel_id=1, source_target_pairs={{0,1},{1,2},{2,3},{3,0},{4,5},{5,6},{6,7},{7,4},{8,9},{9,10},{10,1... | collective-permute-start | bytes 196616 | tf_op jit(solution)/shard_map/ppermute | solution.py:229
  70.1 9.2 %collective-permute-start.15 = (bf16[8,4096]{1,0:T(8,128)(2,1)S(1)}, bf16[8,4096]{1,0:T(8,128)(2,1)S(1)}, u32[]{:S(2)}, u32[]{:S(2)}) collective-permute-start(bf16[8,4096]{1,0:T(8,128)(2,1)S(1)} %get-tuple-element.62), channel_id=1, source_target_pairs={{0,2},{1,3},{2,0},{3,1},{4,6},{5,7},{6,4},{7,5},{8,10},{9,11},{10,... | collective-permute-start | bytes 196616 | tf_op jit(solution)/shard_map/ppermute | solution.py:229
  74.5 7.8 %collective-permute-start.16 = (bf16[8,4096]{1,0:T(8,128)(2,1)S(1)}, bf16[8,4096]{1,0:T(8,128)(2,1)S(1)}, u32[]{:S(2)}, u32[]{:S(2)}) collective-permute-start(bf16[8,4096]{1,0:T(8,128)(2,1)S(1)} %get-tuple-element.63), channel_id=1, source_target_pairs={{0,3},{1,0},{2,1},{3,2},{4,7},{5,4},{6,5},{7,6},{8,11},{9,8},{10,9... | collective-permute-start | bytes 196616 | tf_op jit(solution)/shard_map/ppermute | solution.py:229
  78.1 5.7 %collective-permute-start.20 = (bf16[8,4096]{1,0:T(8,128)(2,1)S(1)}, bf16[8,4096]{1,0:T(8,128)(2,1)S(1)}, u32[]{:S(2)}, u32[]{:S(2)}) collective-permute-start(bf16[8,4096]{1,0:T(8,128)(2,1)S(1)} %slice.15), channel_id=1, source_target_pairs={{0,128},{128,0},{1,129},{129,1},{2,130},{130,2},{3,131},{131,3},{4... | collective-permute-start | bytes 196616 | tf_op jit(solution)/shard_map/ppermute | solution.py:233

commit v5 on v4

--- a/solution.py
+++ b/solution.py
@@ -10,6 +10,7 @@
 COL = ("y", "z_hi")
 VMEM = 12 << 20
 PIECES = 4
+PARTS = 1
 WHOLE = pl.BlockSpec(memory_space=pltpu.VMEM)
 TABLE = pl.BlockSpec(memory_space=pltpu.SMEM)
 
@@ -166,7 +167,7 @@
     def body(table_ref, *refs):
         source_refs = refs[: len(sources)]
         expanded_refs = refs[len(sources) : len(sources) + len(expanded)]
-        own_ref, other_ref, blocked, placed = refs[len(sources) + len(expanded) + 1 :]
+        own_ref, *other_refs, blocked, placed = refs[len(sources) + len(expanded) + 1 :]
         place(blocked, table_ref, source_refs, size)
         placed[...] = blocked[...].reshape(sequences, depth)
         for side in range(0, total, block):
@@ -182,14 +183,17 @@
                 at += high
             value = value * inverse
             own_ref[:, side : side + block] = value[:part]
-            other_ref[:, side : side + block] = value[part:]
+            for k, other_ref in enumerate(other_refs):
+                lower = part + k * (part // PARTS)
+                other_ref[:, side : side + block] = value[lower : lower + part // PARTS].astype(other_ref.dtype)
 
     half = jax.ShapeDtypeStruct((part, total), jnp.float32)
+    other = jax.ShapeDtypeStruct((part // PARTS, total), jnp.float32)
     return pl.pallas_call(
         body,
         in_specs=[TABLE] + [WHOLE] * (len(sources) + len(expanded) + 1),
-        out_specs=[WHOLE] * 2,
-        out_shape=[half, half],
+        out_specs=[WHOLE] * (1 + PARTS),
+        out_shape=[half] + [other] * PARTS,
         scratch_shapes=[pltpu.VMEM((count, size, depth), jnp.bfloat16), pltpu.VMEM((sequences, depth), jnp.bfloat16)],
         compiler_params=params(),
         cost_estimate=pl.CostEstimate(flops=2 * sequences * depth * total, transcendentals=0, bytes_accessed=1 << 20),
@@ -197,7 +201,29 @@
     )(table, *sources, *expanded, after)
 
 
-def split_sum(own, others, part, after=()):
+def column_sum(own, others, part, after):
+    width = own.shape[1]
+
+    def body(own_ref, *refs):
+        total = own_ref[...]
+        for ref in refs[: len(others)]:
+            total = total + ref[...].astype(jnp.float32)
+        for k, out_ref in enumerate(refs[len(others) + 1 :]):
+            out_ref[...] = total[k * part : (k + 1) * part].astype(out_ref.dtype)
+
+    return pl.pallas_call(
+        body,
+        in_specs=[WHOLE] * (2 + len(others)),
+        out_specs=[WHOLE] * 4,
+        out_shape=[jax.ShapeDtypeStruct((part, width), jnp.float32)] * 2
+        + [jax.ShapeDtypeStruct((part, width), jnp.bfloat16)] * 2,
+        compiler_params=params(),
+        cost_estimate=pl.CostEstimate(flops=0, transcendentals=0, bytes_accessed=0),
+        name="column_sum",
+    )(own, *others, after)
+
+
+def split_sum(own, others, part, after=(), stacked=False):
     rows, width = own.shape
     count = rows // part
 
@@ -205,8 +231,11 @@
         given = refs[: 1 + len(others)]
         token_ref, near_ref, *piece_refs = refs[1 + len(others) + len(after) :]
         total = given[0][...]
-        for ref in given[1:]:
-            total = total + ref[...].astype(jnp.float32)
+        terms = [ref[...].astype(jnp.float32) for ref in given[1:]]
+        if stacked:
+            terms = [jnp.concatenate(terms, axis=0)]
+        for term in terms:
+            total = total + term
         near_ref[...] = total[:part]
         for k, piece_ref in enumerate(piece_refs):
             piece_ref[...] = total[(k + 1) * part : (k + 2) * part].astype(jnp.bfloat16)
@@ -219,7 +248,7 @@
         out_shape=[jax.ShapeDtypeStruct((8, 128), jnp.float32), jax.ShapeDtypeStruct((part, width), jnp.float32)]
         + [jax.ShapeDtypeStruct((part, width), jnp.bfloat16)] * (count - 1),
         compiler_params=params(),
-        cost_estimate=pl.CostEstimate(flops=0, transcendentals=0, bytes_accessed=1 << 20),
+        cost_estimate=pl.CostEstimate(flops=0, transcendentals=0, bytes_accessed=0),
         name="split_sum",
     )(own, *others, *after)
 
@@ -272,14 +301,20 @@
     expanded.append(expand(pair_grad, weights, channels, 3, [token])[0])
 
     token, own, *others = left_partial(left_table, right_sources, expanded, held, inverse)
-    right_own, right_other = right_partial(right_table, left_sources, expanded, shared, inverse, token)
+    right_own, *right_others = right_partial(right_table, left_sources, expanded, shared, inverse, token)
 
     left_terms = [moved(other, "y", d + 1) for d, other in enumerate(others)]
-    token, right_near, *pieces = split_sum(right_own, [swapped(right_other, "core", 1)], 2 * held)
+    right_terms = [swapped(other, "core", 1) for other in right_others]
+    token, right_near, *pieces = split_sum(right_own, right_terms, 2 * held, stacked=True)
     right_terms = [moved(piece, "x", d + 1) for d, piece in enumerate(pieces)]
-    token, left_grad, *pieces = split_sum(own, left_terms, shared, [token])
-    for d, piece in enumerate(pieces):
-        left_grad = left_grad + moved(piece, "z_hi", d + 1).astype(jnp.float32)
+    left_sum = own
+    for term in left_terms:
+        left_sum = left_sum + term.astype(jnp.float32)
+    nearest, next_one, opposite, last = column_sum(left_sum, [], shared, token)
+    from_next = moved(last, "z_hi", -1)
+    passed = moved(opposite, "z_hi", 1)
+    passed = moved((next_one + passed.astype(jnp.float32)).astype(jnp.bfloat16), "z_hi", 1)
+    left_grad = nearest + from_next.astype(jnp.float32) + passed.astype(jnp.float32)
     left_grad = jnp.swapaxes(left_grad.reshape(shared, rows, channels), 1, 2)
 
     for term in right_terms:

time: 84.7 us -> 79.3 us (0.936)
  waiting for transfers between devices: 17.5 us -> 13.1 us
  starting transfers between devices: 34.1 us -> 33 us
  Pallas kernels: 27.1 us -> 26.1 us
    ppermute x15, waiting for transfers between devices: 16.1 us -> 12.2 us  [moved(): lax.ppermute(value, axis, [(k, (k + distance) % size) for k in range(size)])]
  transfers between devices with their start and end apart: 21 -> 21, of which waited for: 6 -> 6; matrix products, arithmetic and copies ran while one was open for 4% -> 4% of each run, Pallas kernels for 25% -> 33%
where the time goes in v5:
time: 79.3 us; the launch traced here: 78.3 us
  starting transfers between devices  33 us (42%)
  Pallas kernels  26.1 us (33%)
  waiting for transfers between devices  13.1 us (17%)
  local copies, waits for them, and re-layouts  4.9 us (6%)
  between operations  0.83 us (1%)
    ppermute x15, starting transfers between devices, moved(): lax.ppermute(value, axis, [(k, (k + distance) % size) for k in range(size)])  21.8 us
    ppermute x15, waiting for transfers between devices, moved(): lax.ppermute(value, axis, [(k, (k + distance) % size) for k in range(size)])  12.2 us
    ppermute x6, starting transfers between devices, swapped(): lax.ppermute(value, axis, [(k, k ^ bit) for k in range(lax.axis_size(axis...  11.2 us
    pallas_call x4, Pallas kernels, expand(): pl.pallas_call(body, in_specs=[WHOLE, pl.BlockSpec(memory_space=pltpu.HBM...  11 us
    pallas_call x1, Pallas kernels, left_partial(): pl.pallas_call(body, in_specs=[TABLE] + [WHOLE] * (len(sources) + len(exp...  9.67 us
    pallas_call x1, Pallas kernels, right_partial(): pl.pallas_call(body, in_specs=[TABLE] + [WHOLE] * (len(sources) + len(exp...  5.3 us
    unnamed x3, local copies, waits for them, and re-layouts  2.38 us
  transfers between devices with their start and end apart: 21, of which 6 were waited for; matrix products, arithmetic and copies ran while one was open for 4% of the time, Pallas kernels for 33%

profile of v5, /device:TPU:24, one launch (start us, length us, event | category | flops | bytes accessed | tf_op | source)
XLA Modules:
  0.0 78.3 jit_solution(13322642520896915766)
XLA Ops:
  0.6 1.0 %copy.11 = bf16[8,128,32]{2,1,0:T(8,128)(2,1)S(1)} copy(bf16[8,128,32]{1,2,0:T(8,128)(2,1)} %bitcast.20) | data formatting | bytes 131072 | tf_op jit(solution)/shard_map/transpose | solution.py:278
  1.9 3.4 %collective-permute-start.1 = (bf16[8,4096]{1,0:T(8,128)(2,1)S(1)}, bf16[8,4096]{1,0:T(8,128)(2,1)S(1)}, u32[]{:S(2)}, u32[]{:S(2)}) collective-permute-start(bf16[8,4096]{1,0:T(8,128)(2,1)S(1)} %reshape.25.refs_2_), channel_id=1, source_target_pairs={{0,1},{1,0},{2,3},{3,2},{4,5},{5,4},{6,7},{7,6},{8,9},{9,8},{10,11... | collective-permute-start | bytes 196616 | tf_op jit(solution)/shard_map/ppermute | solution.py:262
  6.2 2.0 %collective-permute-start = (bf16[8,4096]{1,0:T(8,128)(2,1)S(1)}, bf16[8,4096]{1,0:T(8,128)(2,1)S(1)}, u32[]{:S(2)}, u32[]{:S(2)}) collective-permute-start(bf16[8,4096]{1,0:T(8,128)(2,1)S(1)} %bitcast.16), channel_id=1, source_target_pairs={{0,128},{128,0},{1,129},{129,1},{2,130},{130,2},{3,131},{131,3},{4... | collective-permute-start | bytes 196616 | tf_op jit(solution)/shard_map/ppermute | solution.py:262
  8.2 1.1 %copy.10 = bf16[32,32,128]{2,0,1:T(8,128)(2,1)S(1)} copy(bf16[32,32,128]{2,1,0:T(8,128)(2,1)} %bitcast.19) | data formatting | bytes 524288 | tf_op jit(solution)/shard_map/reshape | solution.py:280
  9.3 3.9 %expand.4 = (bf16[1024,4096]{1,0:T(8,128)(2,1)S(1)}, bf16[16,128]{1,0:T(8,128)(2,1)S(1)}, bf16[128,128,128]{2,1,0:T(8,128)(2,1)S(1)}) custom-call(bf16[1024,128]{1,0:T(8,128)(2,1)S(1)} %bitcast.12, bf16[128,128,128]{2,1,0:T(8,128)(2,1)} %grad_ref.1), custom_call_target="tpu_custom_call" | custom-call | flops 2147483648 | bytes 1048576 | tf_op jit(solution)/shard_map/expand/pallas_call | solution.py:60
  13.3 1.6 %collective-permute-start.2 = (bf16[16,4096]{1,0:T(8,128)(2,1)S(1)}, bf16[16,4096]{1,0:T(8,128)(2,1)S(1)}, u32[]{:S(2)}, u32[]{:S(2)}) collective-permute-start(bf16[16,4096]{1,0:T(8,128)(2,1)S(1)} %get-tuple-element.38.refs_0_), channel_id=1, source_target_pairs={{0,32},{32,64},{64,96},{96,0},{1,33},{33,65},{65,97},{97,1},{2,34}... | collective-permute-start | bytes 393224 | tf_op jit(solution)/shard_map/ppermute | solution.py:258
  14.8 2.7 %collective-permute-start.3 = (bf16[16,4096]{1,0:T(8,128)(2,1)S(1)}, bf16[16,4096]{1,0:T(8,128)(2,1)S(1)}, u32[]{:S(2)}, u32[]{:S(2)}) collective-permute-start(bf16[16,4096]{1,0:T(8,128)(2,1)S(1)} %get-tuple-element.38.refs_0_), channel_id=1, source_target_pairs={{0,64},{32,96},{64,0},{96,32},{1,65},{33,97},{65,1},{97,33},{2,66}... | collective-permute-start | bytes 393224 | tf_op jit(solution)/shard_map/ppermute | solution.py:258
  17.5 1.4 %collective-permute-start.4 = (bf16[16,4096]{1,0:T(8,128)(2,1)S(1)}, bf16[16,4096]{1,0:T(8,128)(2,1)S(1)}, u32[]{:S(2)}, u32[]{:S(2)}) collective-permute-start(bf16[16,4096]{1,0:T(8,128)(2,1)S(1)} %get-tuple-element.38.refs_0_), channel_id=1, source_target_pairs={{0,96},{32,0},{64,32},{96,64},{1,97},{33,1},{65,33},{97,65},{2,98}... | collective-permute-start | bytes 393224 | tf_op jit(solution)/shard_map/ppermute | solution.py:258
  19.0 4.5 %collective-permute-start.5 = (bf16[16,4096]{1,0:T(8,128)(2,1)S(1)}, bf16[16,4096]{1,0:T(8,128)(2,1)S(1)}, u32[]{:S(2)}, u32[]{:S(2)}) collective-permute-start(bf16[16,4096]{1,0:T(8,128)(2,1)S(1)} %get-tuple-element.39.refs_4_), channel_id=1, source_target_pairs={{0,2},{1,3},{2,0},{3,1},{4,6},{5,7},{6,4},{7,5},{8,10},{9,11},{10,... | collective-permute-start | bytes 393224 | tf_op jit(solution)/shard_map/ppermute | solution.py:262
  23.5 2.3 %expand.5 = (bf16[1024,4096]{1,0:T(8,128)(2,1)S(1)}, bf16[16,128]{1,0:T(8,128)(2,1)S(1)}) custom-call(bf16[1024,128]{1,0:T(8,128)(2,1)S(1)} %bitcast.13, bf16[128,128,128]{2,1,0:T(8,128)(2,1)S(1)} %get-tuple-element.40.grad_ref, bf16[16,128]{1,0:T(8,128)(2,1)S(1)} %get-tuple-element.41.rest_0_), custom_call_target="tpu_custom_call" | custom-call | flops 2147483648 | bytes 1048576 | tf_op jit(solution)/shard_map/expand/pallas_call | solution.py:60
  25.8 2.3 %expand.6 = (bf16[1024,4096]{1,0:T(8,128)(2,1)S(1)}, bf16[16,128]{1,0:T(8,128)(2,1)S(1)}) custom-call(bf16[1024,128]{1,0:T(8,128)(2,1)S(1)} %bitcast.14, bf16[128,128,128]{2,1,0:T(8,128)(2,1)S(1)} %get-tuple-element.40.grad_ref, bf16[16,128]{1,0:T(8,128)(2,1)S(1)} %get-tuple-element.42.rest_0_), custom_call_target="tpu_custom_call" | custom-call | flops 2147483648 | bytes 1048576 | tf_op jit(solution)/shard_map/expand/pallas_call | solution.py:60
  29.7 2.6 %collective-permute-start.11 = (bf16[32,4096]{1,0:T(8,128)(2,1)S(1)}, bf16[32,4096]{1,0:T(8,128)(2,1)S(1)}, u32[]{:S(2)}, u32[]{:S(2)}) collective-permute-start(bf16[32,4096]{1,0:T(8,128)(2,1)S(1)} %get-tuple-element.55.refs_0_), channel_id=1, source_target_pairs={{0,8},{4,12},{8,0},{12,4},{1,9},{5,13},{9,1},{13,5},{2,10},{6,14},... | collective-permute-start | bytes 786440 | tf_op jit(solution)/shard_map/ppermute | solution.py:258
  32.3 2.3 %expand.7 = (bf16[1024,4096]{1,0:T(8,128)(2,1)S(1)}, bf16[16,128]{1,0:T(8,128)(2,1)}) custom-call(bf16[1024,128]{1,0:T(8,128)(2,1)S(1)} %bitcast.15, bf16[128,128,128]{2,1,0:T(8,128)(2,1)S(1)} %get-tuple-element.40.grad_ref, bf16[16,128]{1,0:T(8,128)(2,1)S(1)} %get-tuple-element.48.rest_0_), custom_call_target="tpu_custom_call" | custom-call | flops 2147483648 | bytes 1048576 | tf_op jit(solution)/shard_map/expand/pallas_call | solution.py:60
  34.7 9.7 %left_partial.1 = (bf16[16,128]{1,0:T(8,128)(2,1)S(1)}, f32[32,4096]{1,0:T(8,128)S(1)}, bf16[32,4096]{1,0:T(8,128)(2,1)S(1)}, bf16[32,4096]{1,0:T(8,128)(2,1)S(1)}, bf16[32,4096]{1,0:T(8,128)(2,1)S(1)}) custom-call(s32[16]{0:T(128)S(1)} %get-tuple-element.35.table_ref, bf16[64,4096]{1,0:T(8,128)(2,1)S(1)} %get-tuple-element.44.refs_0_, ...), custom_call_target="tpu_custom_call" | custom-call | flops 8589934592 | bytes 1048576 | tf_op jit(solution)/shard_map/left_partial/pallas_call | solution.py:141
  44.4 3.3 %collective-permute-start.7 = (bf16[32,4096]{1,0:T(8,128)(2,1)S(1)}, bf16[32,4096]{1,0:T(8,128)(2,1)S(1)}, u32[]{:S(2)}, u32[]{:S(2)}) collective-permute-start(bf16[32,4096]{1,0:T(8,128)(2,1)S(1)} %get-tuple-element.51), channel_id=1, source_target_pairs={{0,4},{4,8},{8,12},{12,0},{1,5},{5,9},{9,13},{13,1},{2,6},{6,10},{... | collective-permute-start | bytes 786440 | tf_op jit(solution)/shard_map/ppermute | solution.py:258
  47.9 1.3 %collective-permute-start.9 = (bf16[32,4096]{1,0:T(8,128)(2,1)S(1)}, bf16[32,4096]{1,0:T(8,128)(2,1)S(1)}, u32[]{:S(2)}, u32[]{:S(2)}) collective-permute-start(bf16[32,4096]{1,0:T(8,128)(2,1)S(1)} %get-tuple-element.53), channel_id=1, source_target_pairs={{0,12},{4,0},{8,4},{12,8},{1,13},{5,1},{9,5},{13,9},{2,14},{6,2},{... | collective-permute-start | bytes 786440 | tf_op jit(solution)/shard_map/ppermute | solution.py:258
  49.2 5.3 %right_partial.1 = (f32[64,4096]{1,0:T(8,128)S(1)}, f32[64,4096]{1,0:T(8,128)S(1)}) custom-call(s32[16]{0:T(128)S(1)} %get-tuple-element.54.table_ref, bf16[32,4096]{1,0:T(8,128)(2,1)S(1)} %get-tuple-element.55.refs_0_, bf16[32,4096]{1,0:T(8,128)(2,1)S(1)} %collective-permute-done.10.refs_1_, bf16[32,4096]{1,0:T(8,128)(2,1)S(1)} %collective-permute-done.11.refs_2_, ...), custom_call_target="tpu_custom_call" | custom-call | flops 4294967296 | bytes 1048576 | tf_op jit(solution)/shard_map/right_partial/pallas_call | solution.py:192
  54.6 4.0 %collective-permute-done.7 = bf16[32,4096]{1,0:T(8,128)(2,1)S(1)} collective-permute-done((bf16[32,4096]{1,0:T(8,128)(2,1)S(1)}, bf16[32,4096]{1,0:T(8,128)(2,1)S(1)}, u32[]{:S(2)}, u32[]{:S(2)}) %collective-permute-start.7) | collective-permute-done | bytes 262176 | tf_op jit(solution)/shard_map/ppermute | solution.py:258
  58.6 3.6 %collective-permute-done.9 = bf16[32,4096]{1,0:T(8,128)(2,1)S(1)} collective-permute-done((bf16[32,4096]{1,0:T(8,128)(2,1)S(1)}, bf16[32,4096]{1,0:T(8,128)(2,1)S(1)}, u32[]{:S(2)}, u32[]{:S(2)}) %collective-permute-start.9) | collective-permute-done | bytes 262176 | tf_op jit(solution)/shard_map/ppermute | solution.py:258
  63.9 1.3 %collective-permute-start.18 = (bf16[16,4096]{1,0:T(8,128)(2,1)S(1)}, bf16[16,4096]{1,0:T(8,128)(2,1)S(1)}, u32[]{:S(2)}, u32[]{:S(2)}) collective-permute-start(bf16[16,4096]{1,0:T(8,128)(2,1)S(1)} %get-tuple-element.66), channel_id=1, source_target_pairs={{0,64},{32,96},{64,0},{96,32},{1,65},{33,97},{65,1},{97,33},{2,66}... | collective-permute-start | bytes 393224 | tf_op jit(solution)/shard_map/ppermute | solution.py:258
  65.2 1.3 %collective-permute-start.19 = (bf16[16,4096]{1,0:T(8,128)(2,1)S(1)}, bf16[16,4096]{1,0:T(8,128)(2,1)S(1)}, u32[]{:S(2)}, u32[]{:S(2)}) collective-permute-start(bf16[16,4096]{1,0:T(8,128)(2,1)S(1)} %get-tuple-element.67), channel_id=1, source_target_pairs={{0,96},{32,0},{64,32},{96,64},{1,97},{33,1},{65,33},{97,65},{2,98}... | collective-permute-start | bytes 393224 | tf_op jit(solution)/shard_map/ppermute | solution.py:258
  66.5 3.4 %collective-permute-start.14 = (bf16[8,4096]{1,0:T(8,128)(2,1)S(1)}, bf16[8,4096]{1,0:T(8,128)(2,1)S(1)}, u32[]{:S(2)}, u32[]{:S(2)}) collective-permute-start(bf16[8,4096]{1,0:T(8,128)(2,1)S(1)} %get-tuple-element.61), channel_id=1, source_target_pairs={{0,3},{1,0},{2,1},{3,2},{4,7},{5,4},{6,5},{7,6},{8,11},{9,8},{10,9... | collective-permute-start | bytes 196616 | tf_op jit(solution)/shard_map/ppermute | solution.py:258
  70.9 1.4 %collective-permute-done.17 = bf16[16,4096]{1,0:T(8,128)(2,1)S(1)} collective-permute-done((bf16[16,4096]{1,0:T(8,128)(2,1)S(1)}, bf16[16,4096]{1,0:T(8,128)(2,1)S(1)}, u32[]{:S(2)}, u32[]{:S(2)}) %collective-permute-start.17) | collective-permute-done | bytes 131104 | tf_op jit(solution)/shard_map/ppermute | solution.py:258
  74.0 2.5 %collective-permute-done.16 = bf16[8,4096]{1,0:T(8,128)(2,1)S(1)} collective-permute-done((bf16[8,4096]{1,0:T(8,128)(2,1)S(1)}, bf16[8,4096]{1,0:T(8,128)(2,1)S(1)}, u32[]{:S(2)}, u32[]{:S(2)}) %collective-permute-start.16) | collective-permute-done | bytes 65568 | tf_op jit(solution)/shard_map/ppermute | solution.py:258
  (42 shorter events, 9.0 us)
Async XLA Ops:
  1.9 11.3 %collective-permute-start.1 = (bf16[8,4096]{1,0:T(8,128)(2,1)S(1)}, bf16[8,4096]{1,0:T(8,128)(2,1)S(1)}, u32[]{:S(2)}, u32[]{:S(2)}) collective-permute-start(bf16[8,4096]{1,0:T(8,128)(2,1)S(1)} %reshape.25.refs_2_), channel_id=1, source_target_pairs={{0,1},{1,0},{2,3},{3,2},{4,5},{5,4},{6,7},{7,6},{8,9},{9,8},{10,11... | collective-permute-start | bytes 196616 | tf_op jit(solution)/shard_map/ppermute | solution.py:262
  6.2 7.1 %collective-permute-start = (bf16[8,4096]{1,0:T(8,128)(2,1)S(1)}, bf16[8,4096]{1,0:T(8,128)(2,1)S(1)}, u32[]{:S(2)}, u32[]{:S(2)}) collective-permute-start(bf16[8,4096]{1,0:T(8,128)(2,1)S(1)} %bitcast.16), channel_id=1, source_target_pairs={{0,128},{128,0},{1,129},{129,1},{2,130},{130,2},{3,131},{131,3},{4... | collective-permute-start | bytes 196616 | tf_op jit(solution)/shard_map/ppermute | solution.py:262
  13.3 14.9 %collective-permute-start.2 = (bf16[16,4096]{1,0:T(8,128)(2,1)S(1)}, bf16[16,4096]{1,0:T(8,128)(2,1)S(1)}, u32[]{:S(2)}, u32[]{:S(2)}) collective-permute-start(bf16[16,4096]{1,0:T(8,128)(2,1)S(1)} %get-tuple-element.38.refs_0_), channel_id=1, source_target_pairs={{0,32},{32,64},{64,96},{96,0},{1,33},{33,65},{65,97},{97,1},{2,34}... | collective-permute-start | bytes 393224 | tf_op jit(solution)/shard_map/ppermute | solution.py:258
  14.8 13.3 %collective-permute-start.3 = (bf16[16,4096]{1,0:T(8,128)(2,1)S(1)}, bf16[16,4096]{1,0:T(8,128)(2,1)S(1)}, u32[]{:S(2)}, u32[]{:S(2)}) collective-permute-start(bf16[16,4096]{1,0:T(8,128)(2,1)S(1)} %get-tuple-element.38.refs_0_), channel_id=1, source_target_pairs={{0,64},{32,96},{64,0},{96,32},{1,65},{33,97},{65,1},{97,33},{2,66}... | collective-permute-start | bytes 393224 | tf_op jit(solution)/shard_map/ppermute | solution.py:258
  17.5 10.6 %collective-permute-start.4 = (bf16[16,4096]{1,0:T(8,128)(2,1)S(1)}, bf16[16,4096]{1,0:T(8,128)(2,1)S(1)}, u32[]{:S(2)}, u32[]{:S(2)}) collective-permute-start(bf16[16,4096]{1,0:T(8,128)(2,1)S(1)} %get-tuple-element.38.refs_0_), channel_id=1, source_target_pairs={{0,96},{32,0},{64,32},{96,64},{1,97},{33,1},{65,33},{97,65},{2,98}... | collective-permute-start | bytes 393224 | tf_op jit(solution)/shard_map/ppermute | solution.py:258
  19.0 10.1 %collective-permute-start.5 = (bf16[16,4096]{1,0:T(8,128)(2,1)S(1)}, bf16[16,4096]{1,0:T(8,128)(2,1)S(1)}, u32[]{:S(2)}, u32[]{:S(2)}) collective-permute-start(bf16[16,4096]{1,0:T(8,128)(2,1)S(1)} %get-tuple-element.39.refs_4_), channel_id=1, source_target_pairs={{0,2},{1,3},{2,0},{3,1},{4,6},{5,7},{6,4},{7,5},{8,10},{9,11},{10,... | collective-permute-start | bytes 393224 | tf_op jit(solution)/shard_map/ppermute | solution.py:262
  29.2 5.5 %collective-permute-start.6 = (bf16[64,4096]{1,0:T(8,128)(2,1)S(1)}, bf16[64,4096]{1,0:T(8,128)(2,1)S(1)}, u32[]{:S(2)}, u32[]{:S(2)}) collective-permute-start(bf16[64,4096]{1,0:T(8,128)(2,1)S(1)} %get-tuple-element.44.refs_0_), channel_id=1, source_target_pairs={{0,16},{16,0},{1,17},{17,1},{2,18},{18,2},{3,19},{19,3},{4,20},{20... | collective-permute-start | bytes 1572872 | tf_op jit(solution)/shard_map/ppermute | solution.py:262
  29.4 18.4 %collective-permute-start.10 = (bf16[32,4096]{1,0:T(8,128)(2,1)S(1)}, bf16[32,4096]{1,0:T(8,128)(2,1)S(1)}, u32[]{:S(2)}, u32[]{:S(2)}) collective-permute-start(bf16[32,4096]{1,0:T(8,128)(2,1)S(1)} %get-tuple-element.55.refs_0_), channel_id=1, source_target_pairs={{0,4},{4,8},{8,12},{12,0},{1,5},{5,9},{9,13},{13,1},{2,6},{6,10},{... | collective-permute-start | bytes 786440 | tf_op jit(solution)/shard_map/ppermute | solution.py:258
  29.7 19.5 %collective-permute-start.11 = (bf16[32,4096]{1,0:T(8,128)(2,1)S(1)}, bf16[32,4096]{1,0:T(8,128)(2,1)S(1)}, u32[]{:S(2)}, u32[]{:S(2)}) collective-permute-start(bf16[32,4096]{1,0:T(8,128)(2,1)S(1)} %get-tuple-element.55.refs_0_), channel_id=1, source_target_pairs={{0,8},{4,12},{8,0},{12,4},{1,9},{5,13},{9,1},{13,5},{2,10},{6,14},... | collective-permute-start | bytes 786440 | tf_op jit(solution)/shard_map/ppermute | solution.py:258
  32.3 16.9 %collective-permute-start.12 = (bf16[32,4096]{1,0:T(8,128)(2,1)S(1)}, bf16[32,4096]{1,0:T(8,128)(2,1)S(1)}, u32[]{:S(2)}, u32[]{:S(2)}) collective-permute-start(bf16[32,4096]{1,0:T(8,128)(2,1)S(1)} %get-tuple-element.55.refs_0_), channel_id=1, source_target_pairs={{0,12},{4,0},{8,4},{12,8},{1,13},{5,1},{9,5},{13,9},{2,14},{6,2},{... | collective-permute-start | bytes 786440 | tf_op jit(solution)/shard_map/ppermute | solution.py:258
  44.4 14.3 %collective-permute-start.7 = (bf16[32,4096]{1,0:T(8,128)(2,1)S(1)}, bf16[32,4096]{1,0:T(8,128)(2,1)S(1)}, u32[]{:S(2)}, u32[]{:S(2)}) collective-permute-start(bf16[32,4096]{1,0:T(8,128)(2,1)S(1)} %get-tuple-element.51), channel_id=1, source_target_pairs={{0,4},{4,8},{8,12},{12,0},{1,5},{5,9},{9,13},{13,1},{2,6},{6,10},{... | collective-permute-start | bytes 786440 | tf_op jit(solution)/shard_map/ppermute | solution.py:258
  47.7 10.9 %collective-permute-start.8 = (bf16[32,4096]{1,0:T(8,128)(2,1)S(1)}, bf16[32,4096]{1,0:T(8,128)(2,1)S(1)}, u32[]{:S(2)}, u32[]{:S(2)}) collective-permute-start(bf16[32,4096]{1,0:T(8,128)(2,1)S(1)} %get-tuple-element.52), channel_id=1, source_target_pairs={{0,8},{4,12},{8,0},{12,4},{1,9},{5,13},{9,1},{13,5},{2,10},{6,14},... | collective-permute-start | bytes 786440 | tf_op jit(solution)/shard_map/ppermute | solution.py:258
  47.9 14.4 %collective-permute-start.9 = (bf16[32,4096]{1,0:T(8,128)(2,1)S(1)}, bf16[32,4096]{1,0:T(8,128)(2,1)S(1)}, u32[]{:S(2)}, u32[]{:S(2)}) collective-permute-start(bf16[32,4096]{1,0:T(8,128)(2,1)S(1)} %get-tuple-element.53), channel_id=1, source_target_pairs={{0,12},{4,0},{8,4},{12,8},{1,13},{5,1},{9,5},{13,9},{2,14},{6,2},{... | collective-permute-start | bytes 786440 | tf_op jit(solution)/shard_map/ppermute | solution.py:258
  54.5 7.8 %collective-permute-start.13 = (f32[64,4096]{1,0:T(8,128)S(1)}, f32[64,4096]{1,0:T(8,128)S(1)}, u32[]{:S(2)}, u32[]{:S(2)}) collective-permute-start(f32[64,4096]{1,0:T(8,128)S(1)} %get-tuple-element.58), channel_id=1, source_target_pairs={{0,16},{16,0},{1,17},{17,1},{2,18},{18,2},{3,19},{19,3},{4,20},{20... | collective-permute-start | bytes 3145736 | tf_op jit(solution)/shard_map/ppermute | solution.py:262
  62.5 7.5 %collective-permute-start.15 = (bf16[8,4096]{1,0:T(8,128)(2,1)S(1)}, bf16[8,4096]{1,0:T(8,128)(2,1)S(1)}, u32[]{:S(2)}, u32[]{:S(2)}) collective-permute-start(bf16[8,4096]{1,0:T(8,128)(2,1)S(1)} %get-tuple-element.63), channel_id=1, source_target_pairs={{0,1},{1,2},{2,3},{3,0},{4,5},{5,6},{6,7},{7,4},{8,9},{9,10},{10,1... | collective-permute-start | bytes 196616 | tf_op jit(solution)/shard_map/ppermute | solution.py:258
  63.3 9.1 %collective-permute-start.17 = (bf16[16,4096]{1,0:T(8,128)(2,1)S(1)}, bf16[16,4096]{1,0:T(8,128)(2,1)S(1)}, u32[]{:S(2)}, u32[]{:S(2)}) collective-permute-start(bf16[16,4096]{1,0:T(8,128)(2,1)S(1)} %get-tuple-element.65), channel_id=1, source_target_pairs={{0,32},{32,64},{64,96},{96,0},{1,33},{33,65},{65,97},{97,1},{2,34}... | collective-permute-start | bytes 393224 | tf_op jit(solution)/shard_map/ppermute | solution.py:258
  63.9 8.5 %collective-permute-start.18 = (bf16[16,4096]{1,0:T(8,128)(2,1)S(1)}, bf16[16,4096]{1,0:T(8,128)(2,1)S(1)}, u32[]{:S(2)}, u32[]{:S(2)}) collective-permute-start(bf16[16,4096]{1,0:T(8,128)(2,1)S(1)} %get-tuple-element.66), channel_id=1, source_target_pairs={{0,64},{32,96},{64,0},{96,32},{1,65},{33,97},{65,1},{97,33},{2,66}... | collective-permute-start | bytes 393224 | tf_op jit(solution)/shard_map/ppermute | solution.py:258
  65.2 7.8 %collective-permute-start.19 = (bf16[16,4096]{1,0:T(8,128)(2,1)S(1)}, bf16[16,4096]{1,0:T(8,128)(2,1)S(1)}, u32[]{:S(2)}, u32[]{:S(2)}) collective-permute-start(bf16[16,4096]{1,0:T(8,128)(2,1)S(1)} %get-tuple-element.67), channel_id=1, source_target_pairs={{0,96},{32,0},{64,32},{96,64},{1,97},{33,1},{65,33},{97,65},{2,98}... | collective-permute-start | bytes 393224 | tf_op jit(solution)/shard_map/ppermute | solution.py:258
  66.5 7.5 %collective-permute-start.14 = (bf16[8,4096]{1,0:T(8,128)(2,1)S(1)}, bf16[8,4096]{1,0:T(8,128)(2,1)S(1)}, u32[]{:S(2)}, u32[]{:S(2)}) collective-permute-start(bf16[8,4096]{1,0:T(8,128)(2,1)S(1)} %get-tuple-element.61), channel_id=1, source_target_pairs={{0,3},{1,0},{2,1},{3,2},{4,7},{5,4},{6,5},{7,6},{8,11},{9,8},{10,9... | collective-permute-start | bytes 196616 | tf_op jit(solution)/shard_map/ppermute | solution.py:258
  70.0 6.6 %collective-permute-start.16 = (bf16[8,4096]{1,0:T(8,128)(2,1)S(1)}, bf16[8,4096]{1,0:T(8,128)(2,1)S(1)}, u32[]{:S(2)}, u32[]{:S(2)}) collective-permute-start(bf16[8,4096]{1,0:T(8,128)(2,1)S(1)} %add_convert_fusion), channel_id=1, source_target_pairs={{0,1},{1,2},{2,3},{3,0},{4,5},{5,6},{6,7},{7,4},{8,9},{9,10},{10,1... | collective-permute-start | bytes 196616 | tf_op jit(solution)/shard_map/ppermute | solution.py:258
  73.0 4.6 %collective-permute-start.20 = (bf16[8,4096]{1,0:T(8,128)(2,1)S(1)}, bf16[8,4096]{1,0:T(8,128)(2,1)S(1)}, u32[]{:S(2)}, u32[]{:S(2)}) collective-permute-start(bf16[8,4096]{1,0:T(8,128)(2,1)S(1)} %slice.15), channel_id=1, source_target_pairs={{0,128},{128,0},{1,129},{129,1},{2,130},{130,2},{3,131},{131,3},{4... | collective-permute-start | bytes 196616 | tf_op jit(solution)/shard_map/ppermute | solution.py:262

commit v6 on v5

--- a/solution.py
+++ b/solution.py
@@ -19,17 +19,19 @@
     return pltpu.CompilerParams(vmem_limit_bytes=VMEM)
 
 
-def expand(pair_grad, weights, channels, number, after=()):
+def expand(pair_grad, weights, channels, numbers, after=()):
     rows, width, cols = pair_grad.shape
     wide = weights.shape[0]
     entries = wide // channels
     held = rows // PIECES
     step = 2
     chunk = 8
-    first = number == 0
+    first = 0 in numbers
 
     def body(weight_ref, grad_ref, *rest):
-        out_ref, token_ref, *rest = rest[len(after) :]
+        rest = rest[len(after) :]
+        out_refs = rest[: len(numbers)]
+        token_ref, *rest = rest[len(numbers) :]
         copies = []
         if first:
             source_ref = grad_ref
@@ -38,37 +40,38 @@
                 part = pl.ds(k * chunk, chunk)
                 copies.append(pltpu.make_async_copy(source_ref.at[part], grad_ref.at[part], sems.at[k]))
                 copies[k].start()
-        for t in range(held // 2):
-            if first and t * 2 % chunk == 0:
-                copies[t * 2 // chunk].wait()
-            i = number * held + t * 2
-            pair = jnp.concatenate([grad_ref[i], grad_ref[i + 1]], axis=1)
-            base = t * 2 * channels
-            for entry in range(0, entries, step):
-                piece = weight_ref[entry * channels : (entry + step) * channels, :]
-                value = jnp.dot(piece, pair, preferred_element_type=jnp.float32).astype(jnp.bfloat16)
-                for k in range(step):
-                    block = value[k * channels : (k + 1) * channels]
-                    stacked = jnp.concatenate([block[:, :cols], block[:, cols:]], axis=0)
-                    side = (entry + k) * cols
-                    out_ref[base : base + 2 * channels, side : side + cols] = stacked
+        for out_ref, number in zip(out_refs, numbers):
+            for t in range(held // 2):
+                if first and t * 2 % chunk == 0:
+                    copies[t * 2 // chunk].wait()
+                i = number * held + t * 2
+                pair = jnp.concatenate([grad_ref[i], grad_ref[i + 1]], axis=1)
+                base = t * 2 * channels
+                for entry in range(0, entries, step):
+                    piece = weight_ref[entry * channels : (entry + step) * channels, :]
+                    value = jnp.dot(piece, pair, preferred_element_type=jnp.float32).astype(jnp.bfloat16)
+                    for k in range(step):
+                        block = value[k * channels : (k + 1) * channels]
+                        stacked = jnp.concatenate([block[:, :cols], block[:, cols:]], axis=0)
+                        side = (entry + k) * cols
+                        out_ref[base : base + 2 * channels, side : side + cols] = stacked
         for copy in copies[held // chunk :]:
             copy.wait()
-        token_ref[...] = out_ref[:16, :128]
+        token_ref[...] = out_refs[-1][:16, :128]
 
     moved_shape = pltpu.VMEM(pair_grad.shape, pair_grad.dtype)
     return pl.pallas_call(
         body,
         in_specs=[WHOLE, pl.BlockSpec(memory_space=pltpu.HBM) if first else WHOLE] + [WHOLE] * len(after),
-        out_specs=[WHOLE] * (3 if first else 2),
+        out_specs=[WHOLE] * (len(numbers) + (2 if first else 1)),
         out_shape=[
-            pltpu.VMEM((held * channels, entries * cols), jnp.bfloat16),
+            *[pltpu.VMEM((held * channels, entries * cols), jnp.bfloat16)] * len(numbers),
             jax.ShapeDtypeStruct((16, 128), jnp.bfloat16),
         ]
         + ([moved_shape] if first else []),
         scratch_shapes=[pltpu.SemaphoreType.DMA((rows // chunk,))] if first else [],
         compiler_params=params(),
-        cost_estimate=pl.CostEstimate(flops=4 * held * wide * width * cols, transcendentals=0, bytes_accessed=1 << 20),
+        cost_estimate=pl.CostEstimate(flops=4 * len(numbers) * held * wide * width * cols, transcendentals=0, bytes_accessed=1 << 20),
         name="expand",
     )(weights, pair_grad, *after)
 
@@ -287,18 +290,16 @@
     from_z = swapped(right_flat, "z_lo", 1)
     from_hi = swapped(left_flat, "z_hi", 1)
     pair_grad = pltpu.with_memory_space_constraint(pair_grad, pltpu.HBM)
-    piece, token, pair_grad = expand(pair_grad, weights, channels, 0)
+    piece, token, pair_grad = expand(pair_grad, weights, channels, [0])
     expanded = [piece]
     near_right, near_left, token = join([[right_flat, from_z], [left_flat, from_hi]], [token])
     from_x = [moved(near_right, "x", d) for d in (1, 2, 3)]
     from_hi = swapped(near_left, "z_hi", 2)
-    for number in (1, 2):
-        piece, token = expand(pair_grad, weights, channels, number, [token])
-        expanded.append(piece)
+    *pieces, token = expand(pair_grad, weights, channels, range(1, PIECES), [token])
+    expanded += pieces
     along_x, along_z, token = join([[near_right, *from_x], [near_left, from_hi]], [token])
     right_sources = [along_x, swapped(along_x, "core", 1)]
     left_sources = [along_z] + [moved(along_z, "y", d) for d in (1, 2, 3)]
-    expanded.append(expand(pair_grad, weights, channels, 3, [token])[0])
 
     token, own, *others = left_partial(left_table, right_sources, expanded, held, inverse)
     right_own, *right_others = right_partial(right_table, left_sources, expanded, shared, inverse, token)

time: 79.3 us -> 78.4 us (0.989)
  starting transfers between devices: 33 us -> 32.2 us
    ppermute x15, waiting for transfers between devices: 12.2 us -> 13.5 us  [moved(): lax.ppermute(value, axis, [(k, (k + distance) % size) for k in range(size)])]
    ppermute x6, waiting for transfers between devices: 0.93 us -> 0.02 us  [swapped(): lax.ppermute(value, axis, [(k, k ^ bit) for k in range(lax.axis_size(axis...]
    pallas_call x4 -> x2, Pallas kernels: 11 us -> 10.7 us  [expand(): pl.pallas_call(body, in_specs=[WHOLE, pl.BlockSpec(memory_space=pltpu.HBM...]
  transfers between devices with their start and end apart: 21 -> 21, of which waited for: 6 -> 5; matrix products, arithmetic and copies ran while one was open for 4% -> 4% of each run, Pallas kernels for 33% -> 33%
where the time goes in v6:
time: 78.4 us; the launch traced here: 78.2 us
  starting transfers between devices  32.2 us (41%)
  Pallas kernels  26.5 us (34%)
  waiting for transfers between devices  13.5 us (17%)
  local copies, waits for them, and re-layouts  4.9 us (6%)
  between operations  0.81 us (1%)
    ppermute x15, starting transfers between devices, moved(): lax.ppermute(value, axis, [(k, (k + distance) % size) for k in range(size)])  21.2 us
    ppermute x15, waiting for transfers between devices, moved(): lax.ppermute(value, axis, [(k, (k + distance) % size) for k in range(size)])  13.5 us
    ppermute x6, starting transfers between devices, swapped(): lax.ppermute(value, axis, [(k, k ^ bit) for k in range(lax.axis_size(axis...  11 us
    pallas_call x2, Pallas kernels, expand(): pl.pallas_call(body, in_specs=[WHOLE, pl.BlockSpec(memory_space=pltpu.HBM...  10.7 us
    pallas_call x1, Pallas kernels, left_partial(): pl.pallas_call(body, in_specs=[TABLE] + [WHOLE] * (len(sources) + len(exp...  9.67 us
    pallas_call x1, Pallas kernels, right_partial(): pl.pallas_call(body, in_specs=[TABLE] + [WHOLE] * (len(sources) + len(exp...  5.31 us
    unnamed x3, local copies, waits for them, and re-layouts  2.38 us
  transfers between devices with their start and end apart: 21, of which 5 were waited for; matrix products, arithmetic and copies ran while one was open for 4% of the time, Pallas kernels for 33%

profile of v6, /device:TPU:24, one launch (start us, length us, event | category | flops | bytes accessed | tf_op | source)
XLA Modules:
  0.0 78.2 jit_solution(17146525233961563638)
XLA Ops:
  0.6 1.0 %copy.11 = bf16[8,128,32]{2,1,0:T(8,128)(2,1)S(1)} copy(bf16[8,128,32]{1,2,0:T(8,128)(2,1)} %bitcast.18) | data formatting | bytes 131072 | tf_op jit(solution)/shard_map/transpose | solution.py:281
  1.9 3.4 %collective-permute-start.1 = (bf16[8,4096]{1,0:T(8,128)(2,1)S(1)}, bf16[8,4096]{1,0:T(8,128)(2,1)S(1)}, u32[]{:S(2)}, u32[]{:S(2)}) collective-permute-start(bf16[8,4096]{1,0:T(8,128)(2,1)S(1)} %reshape.25.refs_2_), channel_id=1, source_target_pairs={{0,1},{1,0},{2,3},{3,2},{4,5},{5,4},{6,7},{7,6},{8,9},{9,8},{10,11... | collective-permute-start | bytes 196616 | tf_op jit(solution)/shard_map/ppermute | solution.py:265
  5.3 0.9 %copy.16 = bf16[1,8,32,128]{3,1,2,0:T(8,128)(2,1)S(1)} copy(bf16[1,8,32,128]{3,2,1,0:T(8,128)(2,1)} %bitcast.19) | data formatting | bytes 131072
  6.2 2.0 %collective-permute-start = (bf16[8,4096]{1,0:T(8,128)(2,1)S(1)}, bf16[8,4096]{1,0:T(8,128)(2,1)S(1)}, u32[]{:S(2)}, u32[]{:S(2)}) collective-permute-start(bf16[8,4096]{1,0:T(8,128)(2,1)S(1)} %bitcast.14), channel_id=1, source_target_pairs={{0,128},{128,0},{1,129},{129,1},{2,130},{130,2},{3,131},{131,3},{4... | collective-permute-start | bytes 196616 | tf_op jit(solution)/shard_map/ppermute | solution.py:265
  8.2 1.1 %copy.10 = bf16[32,32,128]{2,0,1:T(8,128)(2,1)S(1)} copy(bf16[32,32,128]{2,1,0:T(8,128)(2,1)} %bitcast.17) | data formatting | bytes 524288 | tf_op jit(solution)/shard_map/reshape | solution.py:283
  9.3 3.9 %expand.2 = (bf16[1024,4096]{1,0:T(8,128)(2,1)S(1)}, bf16[16,128]{1,0:T(8,128)(2,1)S(1)}, bf16[128,128,128]{2,1,0:T(8,128)(2,1)S(1)}) custom-call(bf16[1024,128]{1,0:T(8,128)(2,1)S(1)} %bitcast.12, bf16[128,128,128]{2,1,0:T(8,128)(2,1)} %grad_ref.1), custom_call_target="tpu_custom_call" | custom-call | flops 2147483648 | bytes 1048576 | tf_op jit(solution)/shard_map/expand/pallas_call | solution.py:63
  13.3 1.6 %collective-permute-start.2 = (bf16[16,4096]{1,0:T(8,128)(2,1)S(1)}, bf16[16,4096]{1,0:T(8,128)(2,1)S(1)}, u32[]{:S(2)}, u32[]{:S(2)}) collective-permute-start(bf16[16,4096]{1,0:T(8,128)(2,1)S(1)} %get-tuple-element.36.refs_0_), channel_id=1, source_target_pairs={{0,32},{32,64},{64,96},{96,0},{1,33},{33,65},{65,97},{97,1},{2,34}... | collective-permute-start | bytes 393224 | tf_op jit(solution)/shard_map/ppermute | solution.py:261
  14.8 2.7 %collective-permute-start.3 = (bf16[16,4096]{1,0:T(8,128)(2,1)S(1)}, bf16[16,4096]{1,0:T(8,128)(2,1)S(1)}, u32[]{:S(2)}, u32[]{:S(2)}) collective-permute-start(bf16[16,4096]{1,0:T(8,128)(2,1)S(1)} %get-tuple-element.36.refs_0_), channel_id=1, source_target_pairs={{0,64},{32,96},{64,0},{96,32},{1,65},{33,97},{65,1},{97,33},{2,66}... | collective-permute-start | bytes 393224 | tf_op jit(solution)/shard_map/ppermute | solution.py:261
  17.6 1.4 %collective-permute-start.4 = (bf16[16,4096]{1,0:T(8,128)(2,1)S(1)}, bf16[16,4096]{1,0:T(8,128)(2,1)S(1)}, u32[]{:S(2)}, u32[]{:S(2)}) collective-permute-start(bf16[16,4096]{1,0:T(8,128)(2,1)S(1)} %get-tuple-element.36.refs_0_), channel_id=1, source_target_pairs={{0,96},{32,0},{64,32},{96,64},{1,97},{33,1},{65,33},{97,65},{2,98}... | collective-permute-start | bytes 393224 | tf_op jit(solution)/shard_map/ppermute | solution.py:261
  19.0 4.5 %collective-permute-start.5 = (bf16[16,4096]{1,0:T(8,128)(2,1)S(1)}, bf16[16,4096]{1,0:T(8,128)(2,1)S(1)}, u32[]{:S(2)}, u32[]{:S(2)}) collective-permute-start(bf16[16,4096]{1,0:T(8,128)(2,1)S(1)} %get-tuple-element.37.refs_4_), channel_id=1, source_target_pairs={{0,2},{1,3},{2,0},{3,1},{4,6},{5,7},{6,4},{7,5},{8,10},{9,11},{10,... | collective-permute-start | bytes 393224 | tf_op jit(solution)/shard_map/ppermute | solution.py:265
  23.5 6.8 %expand.3 = (bf16[1024,4096]{1,0:T(8,128)(2,1)S(1)}, bf16[1024,4096]{1,0:T(8,128)(2,1)S(1)}, bf16[1024,4096]{1,0:T(8,128)(2,1)S(1)}, bf16[16,128]{1,0:T(8,128)(2,1)S(1)}) custom-call(bf16[1024,128]{1,0:T(8,128)(2,1)S(1)} %bitcast.13, bf16[128,128,128]{2,1,0:T(8,128)(2,1)S(1)} %get-tuple-element.38.grad_ref, bf16[16,128]{1,0:T(8,128)(2,1)S(1)} %get-tuple-element.39.rest_0_), custom_call_target="tpu_custom_call" | custom-call | flops 6442450944 | bytes 1048576 | tf_op jit(solution)/shard_map/expand/pallas_call | solution.py:63
  31.2 2.6 %collective-permute-start.11 = (bf16[32,4096]{1,0:T(8,128)(2,1)S(1)}, bf16[32,4096]{1,0:T(8,128)(2,1)S(1)}, u32[]{:S(2)}, u32[]{:S(2)}) collective-permute-start(bf16[32,4096]{1,0:T(8,128)(2,1)S(1)} %get-tuple-element.51.refs_0_), channel_id=1, source_target_pairs={{0,8},{4,12},{8,0},{12,4},{1,9},{5,13},{9,1},{13,5},{2,10},{6,14},... | collective-permute-start | bytes 786440 | tf_op jit(solution)/shard_map/ppermute | solution.py:261
  33.7 9.7 %left_partial.1 = (bf16[16,128]{1,0:T(8,128)(2,1)S(1)}, f32[32,4096]{1,0:T(8,128)S(1)}, bf16[32,4096]{1,0:T(8,128)(2,1)S(1)}, bf16[32,4096]{1,0:T(8,128)(2,1)S(1)}, bf16[32,4096]{1,0:T(8,128)(2,1)S(1)}) custom-call(s32[16]{0:T(128)S(1)} %get-tuple-element.33.table_ref, bf16[64,4096]{1,0:T(8,128)(2,1)S(1)} %get-tuple-element.41.refs_0_, ...), custom_call_target="tpu_custom_call" | custom-call | flops 8589934592 | bytes 1048576 | tf_op jit(solution)/shard_map/left_partial/pallas_call | solution.py:144
  43.4 3.3 %collective-permute-start.7 = (bf16[32,4096]{1,0:T(8,128)(2,1)S(1)}, bf16[32,4096]{1,0:T(8,128)(2,1)S(1)}, u32[]{:S(2)}, u32[]{:S(2)}) collective-permute-start(bf16[32,4096]{1,0:T(8,128)(2,1)S(1)} %get-tuple-element.47), channel_id=1, source_target_pairs={{0,4},{4,8},{8,12},{12,0},{1,5},{5,9},{9,13},{13,1},{2,6},{6,10},{... | collective-permute-start | bytes 786440 | tf_op jit(solution)/shard_map/ppermute | solution.py:261
  46.9 1.3 %collective-permute-start.9 = (bf16[32,4096]{1,0:T(8,128)(2,1)S(1)}, bf16[32,4096]{1,0:T(8,128)(2,1)S(1)}, u32[]{:S(2)}, u32[]{:S(2)}) collective-permute-start(bf16[32,4096]{1,0:T(8,128)(2,1)S(1)} %get-tuple-element.49), channel_id=1, source_target_pairs={{0,12},{4,0},{8,4},{12,8},{1,13},{5,1},{9,5},{13,9},{2,14},{6,2},{... | collective-permute-start | bytes 786440 | tf_op jit(solution)/shard_map/ppermute | solution.py:261
  48.3 5.3 %right_partial.1 = (f32[64,4096]{1,0:T(8,128)S(1)}, f32[64,4096]{1,0:T(8,128)S(1)}) custom-call(s32[16]{0:T(128)S(1)} %get-tuple-element.50.table_ref, bf16[32,4096]{1,0:T(8,128)(2,1)S(1)} %get-tuple-element.51.refs_0_, bf16[32,4096]{1,0:T(8,128)(2,1)S(1)} %collective-permute-done.10.refs_1_, bf16[32,4096]{1,0:T(8,128)(2,1)S(1)} %collective-permute-done.11.refs_2_, ...), custom_call_target="tpu_custom_call" | custom-call | flops 4294967296 | bytes 1048576 | tf_op jit(solution)/shard_map/right_partial/pallas_call | solution.py:195
  53.7 4.0 %collective-permute-done.7 = bf16[32,4096]{1,0:T(8,128)(2,1)S(1)} collective-permute-done((bf16[32,4096]{1,0:T(8,128)(2,1)S(1)}, bf16[32,4096]{1,0:T(8,128)(2,1)S(1)}, u32[]{:S(2)}, u32[]{:S(2)}) %collective-permute-start.7) | collective-permute-done | bytes 262176 | tf_op jit(solution)/shard_map/ppermute | solution.py:261
  57.7 3.6 %collective-permute-done.9 = bf16[32,4096]{1,0:T(8,128)(2,1)S(1)} collective-permute-done((bf16[32,4096]{1,0:T(8,128)(2,1)S(1)}, bf16[32,4096]{1,0:T(8,128)(2,1)S(1)}, u32[]{:S(2)}, u32[]{:S(2)}) %collective-permute-start.9) | collective-permute-done | bytes 262176 | tf_op jit(solution)/shard_map/ppermute | solution.py:261
  61.7 1.5 %collective-permute-start.15 = (bf16[8,4096]{1,0:T(8,128)(2,1)S(1)}, bf16[8,4096]{1,0:T(8,128)(2,1)S(1)}, u32[]{:S(2)}, u32[]{:S(2)}) collective-permute-start(bf16[8,4096]{1,0:T(8,128)(2,1)S(1)} %get-tuple-element.59), channel_id=1, source_target_pairs={{0,1},{1,2},{2,3},{3,0},{4,5},{5,6},{6,7},{7,4},{8,9},{9,10},{10,1... | collective-permute-start | bytes 196616 | tf_op jit(solution)/shard_map/ppermute | solution.py:261
  64.7 1.8 %collective-permute-start.19 = (bf16[16,4096]{1,0:T(8,128)(2,1)S(1)}, bf16[16,4096]{1,0:T(8,128)(2,1)S(1)}, u32[]{:S(2)}, u32[]{:S(2)}) collective-permute-start(bf16[16,4096]{1,0:T(8,128)(2,1)S(1)} %get-tuple-element.63), channel_id=1, source_target_pairs={{0,96},{32,0},{64,32},{96,64},{1,97},{33,1},{65,33},{97,65},{2,98}... | collective-permute-start | bytes 393224 | tf_op jit(solution)/shard_map/ppermute | solution.py:261
  66.5 2.7 %collective-permute-start.14 = (bf16[8,4096]{1,0:T(8,128)(2,1)S(1)}, bf16[8,4096]{1,0:T(8,128)(2,1)S(1)}, u32[]{:S(2)}, u32[]{:S(2)}) collective-permute-start(bf16[8,4096]{1,0:T(8,128)(2,1)S(1)} %get-tuple-element.57), channel_id=1, source_target_pairs={{0,3},{1,0},{2,1},{3,2},{4,7},{5,4},{6,5},{7,6},{8,11},{9,8},{10,9... | collective-permute-start | bytes 196616 | tf_op jit(solution)/shard_map/ppermute | solution.py:261
  69.5 2.8 %collective-permute-done.17 = bf16[16,4096]{1,0:T(8,128)(2,1)S(1)} collective-permute-done((bf16[16,4096]{1,0:T(8,128)(2,1)S(1)}, bf16[16,4096]{1,0:T(8,128)(2,1)S(1)}, u32[]{:S(2)}, u32[]{:S(2)}) %collective-permute-start.17) | collective-permute-done | bytes 131104 | tf_op jit(solution)/shard_map/ppermute | solution.py:261
  73.0 1.1 %collective-permute-start.20 = (bf16[8,4096]{1,0:T(8,128)(2,1)S(1)}, bf16[8,4096]{1,0:T(8,128)(2,1)S(1)}, u32[]{:S(2)}, u32[]{:S(2)}) collective-permute-start(bf16[8,4096]{1,0:T(8,128)(2,1)S(1)} %slice.15), channel_id=1, source_target_pairs={{0,128},{128,0},{1,129},{129,1},{2,130},{130,2},{3,131},{131,3},{4... | collective-permute-start | bytes 196616 | tf_op jit(solution)/shard_map/ppermute | solution.py:265
  74.1 2.4 %collective-permute-done.16 = bf16[8,4096]{1,0:T(8,128)(2,1)S(1)} collective-permute-done((bf16[8,4096]{1,0:T(8,128)(2,1)S(1)}, bf16[8,4096]{1,0:T(8,128)(2,1)S(1)}, u32[]{:S(2)}, u32[]{:S(2)}) %collective-permute-start.16) | collective-permute-done | bytes 65568 | tf_op jit(solution)/shard_map/ppermute | solution.py:261
  (40 shorter events, 6.1 us)
Async XLA Ops:
  1.9 11.3 %collective-permute-start.1 = (bf16[8,4096]{1,0:T(8,128)(2,1)S(1)}, bf16[8,4096]{1,0:T(8,128)(2,1)S(1)}, u32[]{:S(2)}, u32[]{:S(2)}) collective-permute-start(bf16[8,4096]{1,0:T(8,128)(2,1)S(1)} %reshape.25.refs_2_), channel_id=1, source_target_pairs={{0,1},{1,0},{2,3},{3,2},{4,5},{5,4},{6,7},{7,6},{8,9},{9,8},{10,11... | collective-permute-start | bytes 196616 | tf_op jit(solution)/shard_map/ppermute | solution.py:265
  6.2 7.1 %collective-permute-start = (bf16[8,4096]{1,0:T(8,128)(2,1)S(1)}, bf16[8,4096]{1,0:T(8,128)(2,1)S(1)}, u32[]{:S(2)}, u32[]{:S(2)}) collective-permute-start(bf16[8,4096]{1,0:T(8,128)(2,1)S(1)} %bitcast.14), channel_id=1, source_target_pairs={{0,128},{128,0},{1,129},{129,1},{2,130},{130,2},{3,131},{131,3},{4... | collective-permute-start | bytes 196616 | tf_op jit(solution)/shard_map/ppermute | solution.py:265
  13.3 17.0 %collective-permute-start.2 = (bf16[16,4096]{1,0:T(8,128)(2,1)S(1)}, bf16[16,4096]{1,0:T(8,128)(2,1)S(1)}, u32[]{:S(2)}, u32[]{:S(2)}) collective-permute-start(bf16[16,4096]{1,0:T(8,128)(2,1)S(1)} %get-tuple-element.36.refs_0_), channel_id=1, source_target_pairs={{0,32},{32,64},{64,96},{96,0},{1,33},{33,65},{65,97},{97,1},{2,34}... | collective-permute-start | bytes 393224 | tf_op jit(solution)/shard_map/ppermute | solution.py:261
  14.8 15.4 %collective-permute-start.3 = (bf16[16,4096]{1,0:T(8,128)(2,1)S(1)}, bf16[16,4096]{1,0:T(8,128)(2,1)S(1)}, u32[]{:S(2)}, u32[]{:S(2)}) collective-permute-start(bf16[16,4096]{1,0:T(8,128)(2,1)S(1)} %get-tuple-element.36.refs_0_), channel_id=1, source_target_pairs={{0,64},{32,96},{64,0},{96,32},{1,65},{33,97},{65,1},{97,33},{2,66}... | collective-permute-start | bytes 393224 | tf_op jit(solution)/shard_map/ppermute | solution.py:261
  17.6 12.7 %collective-permute-start.4 = (bf16[16,4096]{1,0:T(8,128)(2,1)S(1)}, bf16[16,4096]{1,0:T(8,128)(2,1)S(1)}, u32[]{:S(2)}, u32[]{:S(2)}) collective-permute-start(bf16[16,4096]{1,0:T(8,128)(2,1)S(1)} %get-tuple-element.36.refs_0_), channel_id=1, source_target_pairs={{0,96},{32,0},{64,32},{96,64},{1,97},{33,1},{65,33},{97,65},{2,98}... | collective-permute-start | bytes 393224 | tf_op jit(solution)/shard_map/ppermute | solution.py:261
  19.0 11.3 %collective-permute-start.5 = (bf16[16,4096]{1,0:T(8,128)(2,1)S(1)}, bf16[16,4096]{1,0:T(8,128)(2,1)S(1)}, u32[]{:S(2)}, u32[]{:S(2)}) collective-permute-start(bf16[16,4096]{1,0:T(8,128)(2,1)S(1)} %get-tuple-element.37.refs_4_), channel_id=1, source_target_pairs={{0,2},{1,3},{2,0},{3,1},{4,6},{5,7},{6,4},{7,5},{8,10},{9,11},{10,... | collective-permute-start | bytes 393224 | tf_op jit(solution)/shard_map/ppermute | solution.py:265
  30.9 2.8 %collective-permute-start.6 = (bf16[64,4096]{1,0:T(8,128)(2,1)S(1)}, bf16[64,4096]{1,0:T(8,128)(2,1)S(1)}, u32[]{:S(2)}, u32[]{:S(2)}) collective-permute-start(bf16[64,4096]{1,0:T(8,128)(2,1)S(1)} %get-tuple-element.41.refs_0_), channel_id=1, source_target_pairs={{0,16},{16,0},{1,17},{17,1},{2,18},{18,2},{3,19},{19,3},{4,20},{20... | collective-permute-start | bytes 1572872 | tf_op jit(solution)/shard_map/ppermute | solution.py:265
  30.9 16.0 %collective-permute-start.10 = (bf16[32,4096]{1,0:T(8,128)(2,1)S(1)}, bf16[32,4096]{1,0:T(8,128)(2,1)S(1)}, u32[]{:S(2)}, u32[]{:S(2)}) collective-permute-start(bf16[32,4096]{1,0:T(8,128)(2,1)S(1)} %get-tuple-element.51.refs_0_), channel_id=1, source_target_pairs={{0,4},{4,8},{8,12},{12,0},{1,5},{5,9},{9,13},{13,1},{2,6},{6,10},{... | collective-permute-start | bytes 786440 | tf_op jit(solution)/shard_map/ppermute | solution.py:261
  31.2 17.1 %collective-permute-start.11 = (bf16[32,4096]{1,0:T(8,128)(2,1)S(1)}, bf16[32,4096]{1,0:T(8,128)(2,1)S(1)}, u32[]{:S(2)}, u32[]{:S(2)}) collective-permute-start(bf16[32,4096]{1,0:T(8,128)(2,1)S(1)} %get-tuple-element.51.refs_0_), channel_id=1, source_target_pairs={{0,8},{4,12},{8,0},{12,4},{1,9},{5,13},{9,1},{13,5},{2,10},{6,14},... | collective-permute-start | bytes 786440 | tf_op jit(solution)/shard_map/ppermute | solution.py:261
  33.7 14.5 %collective-permute-start.12 = (bf16[32,4096]{1,0:T(8,128)(2,1)S(1)}, bf16[32,4096]{1,0:T(8,128)(2,1)S(1)}, u32[]{:S(2)}, u32[]{:S(2)}) collective-permute-start(bf16[32,4096]{1,0:T(8,128)(2,1)S(1)} %get-tuple-element.51.refs_0_), channel_id=1, source_target_pairs={{0,12},{4,0},{8,4},{12,8},{1,13},{5,1},{9,5},{13,9},{2,14},{6,2},{... | collective-permute-start | bytes 786440 | tf_op jit(solution)/shard_map/ppermute | solution.py:261
  43.4 14.3 %collective-permute-start.7 = (bf16[32,4096]{1,0:T(8,128)(2,1)S(1)}, bf16[32,4096]{1,0:T(8,128)(2,1)S(1)}, u32[]{:S(2)}, u32[]{:S(2)}) collective-permute-start(bf16[32,4096]{1,0:T(8,128)(2,1)S(1)} %get-tuple-element.47), channel_id=1, source_target_pairs={{0,4},{4,8},{8,12},{12,0},{1,5},{5,9},{9,13},{13,1},{2,6},{6,10},{... | collective-permute-start | bytes 786440 | tf_op jit(solution)/shard_map/ppermute | solution.py:261
  46.7 11.0 %collective-permute-start.8 = (bf16[32,4096]{1,0:T(8,128)(2,1)S(1)}, bf16[32,4096]{1,0:T(8,128)(2,1)S(1)}, u32[]{:S(2)}, u32[]{:S(2)}) collective-permute-start(bf16[32,4096]{1,0:T(8,128)(2,1)S(1)} %get-tuple-element.48), channel_id=1, source_target_pairs={{0,8},{4,12},{8,0},{12,4},{1,9},{5,13},{9,1},{13,5},{2,10},{6,14},... | collective-permute-start | bytes 786440 | tf_op jit(solution)/shard_map/ppermute | solution.py:261
  46.9 14.4 %collective-permute-start.9 = (bf16[32,4096]{1,0:T(8,128)(2,1)S(1)}, bf16[32,4096]{1,0:T(8,128)(2,1)S(1)}, u32[]{:S(2)}, u32[]{:S(2)}) collective-permute-start(bf16[32,4096]{1,0:T(8,128)(2,1)S(1)} %get-tuple-element.49), channel_id=1, source_target_pairs={{0,12},{4,0},{8,4},{12,8},{1,13},{5,1},{9,5},{13,9},{2,14},{6,2},{... | collective-permute-start | bytes 786440 | tf_op jit(solution)/shard_map/ppermute | solution.py:261
  53.6 7.9 %collective-permute-start.13 = (f32[64,4096]{1,0:T(8,128)S(1)}, f32[64,4096]{1,0:T(8,128)S(1)}, u32[]{:S(2)}, u32[]{:S(2)}) collective-permute-start(f32[64,4096]{1,0:T(8,128)S(1)} %get-tuple-element.54), channel_id=1, source_target_pairs={{0,16},{16,0},{1,17},{17,1},{2,18},{18,2},{3,19},{19,3},{4,20},{20... | collective-permute-start | bytes 3145736 | tf_op jit(solution)/shard_map/ppermute | solution.py:265
  61.7 7.5 %collective-permute-start.15 = (bf16[8,4096]{1,0:T(8,128)(2,1)S(1)}, bf16[8,4096]{1,0:T(8,128)(2,1)S(1)}, u32[]{:S(2)}, u32[]{:S(2)}) collective-permute-start(bf16[8,4096]{1,0:T(8,128)(2,1)S(1)} %get-tuple-element.59), channel_id=1, source_target_pairs={{0,1},{1,2},{2,3},{3,0},{4,5},{5,6},{6,7},{7,4},{8,9},{9,10},{10,1... | collective-permute-start | bytes 196616 | tf_op jit(solution)/shard_map/ppermute | solution.py:261
  63.2 9.1 %collective-permute-start.17 = (bf16[16,4096]{1,0:T(8,128)(2,1)S(1)}, bf16[16,4096]{1,0:T(8,128)(2,1)S(1)}, u32[]{:S(2)}, u32[]{:S(2)}) collective-permute-start(bf16[16,4096]{1,0:T(8,128)(2,1)S(1)} %get-tuple-element.61), channel_id=1, source_target_pairs={{0,32},{32,64},{64,96},{96,0},{1,33},{33,65},{65,97},{97,1},{2,34}... | collective-permute-start | bytes 393224 | tf_op jit(solution)/shard_map/ppermute | solution.py:261
  63.8 8.5 %collective-permute-start.18 = (bf16[16,4096]{1,0:T(8,128)(2,1)S(1)}, bf16[16,4096]{1,0:T(8,128)(2,1)S(1)}, u32[]{:S(2)}, u32[]{:S(2)}) collective-permute-start(bf16[16,4096]{1,0:T(8,128)(2,1)S(1)} %get-tuple-element.62), channel_id=1, source_target_pairs={{0,64},{32,96},{64,0},{96,32},{1,65},{33,97},{65,1},{97,33},{2,66}... | collective-permute-start | bytes 393224 | tf_op jit(solution)/shard_map/ppermute | solution.py:261
  64.7 8.2 %collective-permute-start.19 = (bf16[16,4096]{1,0:T(8,128)(2,1)S(1)}, bf16[16,4096]{1,0:T(8,128)(2,1)S(1)}, u32[]{:S(2)}, u32[]{:S(2)}) collective-permute-start(bf16[16,4096]{1,0:T(8,128)(2,1)S(1)} %get-tuple-element.63), channel_id=1, source_target_pairs={{0,96},{32,0},{64,32},{96,64},{1,97},{33,1},{65,33},{97,65},{2,98}... | collective-permute-start | bytes 393224 | tf_op jit(solution)/shard_map/ppermute | solution.py:261
  66.5 7.6 %collective-permute-start.14 = (bf16[8,4096]{1,0:T(8,128)(2,1)S(1)}, bf16[8,4096]{1,0:T(8,128)(2,1)S(1)}, u32[]{:S(2)}, u32[]{:S(2)}) collective-permute-start(bf16[8,4096]{1,0:T(8,128)(2,1)S(1)} %get-tuple-element.57), channel_id=1, source_target_pairs={{0,3},{1,0},{2,1},{3,2},{4,7},{5,4},{6,5},{7,6},{8,11},{9,8},{10,9... | collective-permute-start | bytes 196616 | tf_op jit(solution)/shard_map/ppermute | solution.py:261
  69.2 7.2 %collective-permute-start.16 = (bf16[8,4096]{1,0:T(8,128)(2,1)S(1)}, bf16[8,4096]{1,0:T(8,128)(2,1)S(1)}, u32[]{:S(2)}, u32[]{:S(2)}) collective-permute-start(bf16[8,4096]{1,0:T(8,128)(2,1)S(1)} %add_convert_fusion), channel_id=1, source_target_pairs={{0,1},{1,2},{2,3},{3,0},{4,5},{5,6},{6,7},{7,4},{8,9},{9,10},{10,1... | collective-permute-start | bytes 196616 | tf_op jit(solution)/shard_map/ppermute | solution.py:261
  73.0 4.5 %collective-permute-start.20 = (bf16[8,4096]{1,0:T(8,128)(2,1)S(1)}, bf16[8,4096]{1,0:T(8,128)(2,1)S(1)}, u32[]{:S(2)}, u32[]{:S(2)}) collective-permute-start(bf16[8,4096]{1,0:T(8,128)(2,1)S(1)} %slice.15), channel_id=1, source_target_pairs={{0,128},{128,0},{1,129},{129,1},{2,130},{130,2},{3,131},{131,3},{4... | collective-permute-start | bytes 196616 | tf_op jit(solution)/shard_map/ppermute | solution.py:265
